TPU v7x, 128 devices: a whole 4x4x4 slice. The times are simulated.
128 devices in a mesh: dp: 16 (over x, z), expert: 8 (over y, core).
Axes of the slice: x: 4, y: 4, z: 4, core: 2. Of those that a mesh axis runs over, the one named last changes fastest.
Arguments:
- tokens: bfloat16 [65536, 1024], P(('dp', 'expert')), may hold values from -6 to 6
- block_expert: int32 [512], P(('dp', 'expert')), may hold values from 0 to 63, as said below
- gate_weight: bfloat16 [64, 1024, 384], P('expert'), may hold values from -0.1875 to 0.1875
- up_weight: bfloat16 [64, 1024, 384], P('expert'), may hold values from -0.1875 to 0.1875
Outputs:
- gram_factor: float32 [64, 384, 384], P('expert', 'dp')
Inputs may be any that keep to these rules, and one draw needn't show every extreme that they name: `block_expert`: expert e is held by index e // 8 of the expert axis. Among the 4 blocks of one device, at most 1 name experts of any one index of the expert axis; in every group of devices along the expert axis, one index of the expert axis receives exactly 1 block from every device of the group.
All inputs are finite; a program needn't handle non-finite values.
Results may differ from a plain program's by a relative error of at most 0.0031.
Values may be sent and summed in bfloat16 or wider, within the bound.
No kernel may reach another device: no remote copies, remote signals or barrier semaphores. Data moves between devices by JAX's collectives and lax.ppermute only.
A program may use at most 128 MiB of HBM per device.

v0:
```python
import jax
import jax.numpy as jnp
from jax import lax
from jax.experimental import pallas as pl
from jax.experimental.pallas import tpu as pltpu
from jax.sharding import PartitionSpec as P


BLOCK = 128
RIDGE = 0.05
LANE = 128
TAG = 16
SIDE = 4
VMEM_BYTES = 20 << 20
EDGES = (0, 2, 6, 7, 8)
STRIP = 64
F32 = jnp.float32
BF16 = jnp.bfloat16
HIGH = lax.Precision.HIGHEST
TN = (((0,), (0,)), ((), ()))
HALF = 64
TIP = 320
TIP_ODD = 256


def near(x):
    return pltpu.with_memory_space_constraint(x, pltpu.VMEM)


def far(x):
    return pltpu.with_memory_space_constraint(x, pltpu.HBM)


def pack_kernel(member_ref, assign_hbm, tok_hbm, *rest, experts_each, shifts, chips):
    outs = rest[: len(shifts)]
    assign_ref, tok_ref, sem = rest[len(shifts) :]
    blocks, chunks = tok_ref.shape[0] // BLOCK, tok_ref.shape[1] // LANE
    fetch = [
        pltpu.make_async_copy(assign_hbm, assign_ref, sem.at[0]),
        pltpu.make_async_copy(tok_hbm, tok_ref, sem.at[1]),
    ]
    for copy in fetch:
        copy.start()
    for copy in fetch:
        copy.wait()
    chip = lax.div(member_ref[0], 2)
    core = lax.rem(member_ref[0], 2)
    for (dy, dc), out in zip(shifts, outs):
        dest = lax.rem(chip + dy, chips) * 2 + lax.rem(core + dc, 2)
        block = jnp.int32(0)
        code = jnp.int32(0)
        for b in range(blocks):
            expert = assign_ref[b]
            owner = lax.div(expert, experts_each)
            hit = owner == dest
            block = jnp.where(hit, b, block)
            code = jnp.where(hit, expert - owner * experts_each + 1, code)
        row = pl.multiple_of(block * BLOCK, BLOCK)
        for c in range(chunks):
            out[c * BLOCK : (c + 1) * BLOCK, :] = tok_ref[
                pl.ds(row, BLOCK), c * LANE : (c + 1) * LANE
            ]
        out[chunks * BLOCK :, :] = jnp.full((TAG, LANE), code.astype(F32), F32).astype(BF16)


def pack(assign, member, tokens, experts_each, shifts, chips):
    rows = BLOCK * tokens.shape[1] // LANE + TAG
    return pl.pallas_call(
        lambda *refs: pack_kernel(*refs, experts_each=experts_each, shifts=shifts, chips=chips),
        in_specs=[pl.BlockSpec(memory_space=pltpu.SMEM)]
        + [pl.BlockSpec(memory_space=pl.ANY)] * 2,
        out_specs=[pl.BlockSpec(memory_space=pltpu.VMEM)] * len(shifts),
        out_shape=[pltpu.VMEM((rows, LANE), BF16)] * len(shifts),
        scratch_shapes=[
            pltpu.SMEM(assign.shape, assign.dtype),
            pltpu.VMEM(tokens.shape, tokens.dtype),
            pltpu.SemaphoreType.DMA((2,)),
        ],
        compiler_params=pltpu.CompilerParams(vmem_limit_bytes=VMEM_BYTES),
        name="pack",
    )(member, far(assign), far(tokens))


def hidden_kernel(*refs, slots, model_width):
    xs = refs[:slots]
    gate_ref, up_ref, out_ref = refs[slots:]
    chunks = model_width // LANE
    codes = []
    for s in range(slots):
        tag = xs[s][chunks * BLOCK : chunks * BLOCK + TAG, :].astype(F32)
        codes.append(jnp.max(tag).astype(jnp.int32))

    width = out_ref.shape[1]
    lane = lax.broadcasted_iota(jnp.int32, (TAG, width), 1)
    tags = jnp.zeros((TAG, width), F32)
    for s in range(slots):
        tags = jnp.where(lane == s, codes[s].astype(F32), tags)
    out_ref[slots * BLOCK :, :] = tags.astype(BF16)
    for s in range(slots):

        @pl.when(codes[s] > 0)
        def _(s=s):
            expert = codes[s] - 1
            x = jnp.concatenate(
                [xs[s][c * BLOCK : (c + 1) * BLOCK, :] for c in range(chunks)], axis=1
            )
            gate = jnp.dot(x, gate_ref[expert], preferred_element_type=F32)
            up = jnp.dot(x, up_ref[expert], preferred_element_type=F32)
            hidden = gate / (1.0 + jnp.exp(-gate)) * up
            out_ref[s * BLOCK : (s + 1) * BLOCK, :] = hidden.astype(BF16)


def hidden_rows(arrived, gate_weight, up_weight):
    slots = len(arrived)
    _, model_width, hidden_width = gate_weight.shape
    return pl.pallas_call(
        lambda *refs: hidden_kernel(*refs, slots=slots, model_width=model_width),
        in_specs=[pl.BlockSpec(memory_space=pltpu.VMEM)] * (slots + 2),
        out_specs=pl.BlockSpec(memory_space=pltpu.VMEM),
        out_shape=pltpu.VMEM((slots * BLOCK + TAG, hidden_width), BF16),
        compiler_params=pltpu.CompilerParams(vmem_limit_bytes=VMEM_BYTES),
        name="hidden",
    )(*[near(x) for x in (*arrived, gate_weight, up_weight)])


def bring_kernel(_, gate_ref, up_ref, gate_out, up_out, sem):
    copies = [
        pltpu.make_async_copy(gate_ref, gate_out, sem.at[0]),
        pltpu.make_async_copy(up_ref, up_out, sem.at[1]),
    ]
    for copy in copies:
        copy.start()
    for copy in copies:
        copy.wait()


def bring(after, gate_weight, up_weight):
    return pl.pallas_call(
        bring_kernel,
        in_specs=[pl.BlockSpec(memory_space=pl.ANY)] * 3,
        out_specs=[pl.BlockSpec(memory_space=pltpu.VMEM)] * 2,
        out_shape=[pltpu.VMEM(w.shape, w.dtype) for w in (gate_weight, up_weight)],
        scratch_shapes=[pltpu.SemaphoreType.DMA((2,))],
        compiler_params=pltpu.CompilerParams(vmem_limit_bytes=VMEM_BYTES),
        name="bring",
    )(after, far(gate_weight), far(up_weight))


def fold(tile):
    row = lax.broadcasted_iota(jnp.int32, (HALF, LANE), 0)
    lane = lax.broadcasted_iota(jnp.int32, (HALF, LANE), 1)
    upper, lower = tile[:HALF, :], tile[HALF:, :]
    folded = jnp.where((lane < HALF) & (lane < row), pltpu.roll(lower, HALF, 1), upper)
    corner = jnp.sum(jnp.where(lane == row + HALF, lower, 0.0), axis=0, keepdims=True)
    return folded, corner


def unfold(folded, corner):
    row = lax.broadcasted_iota(jnp.int32, (HALF, LANE), 0)
    lane = lax.broadcasted_iota(jnp.int32, (HALF, LANE), 1)
    flipped = jnp.concatenate([folded, jnp.zeros((HALF, LANE), F32)], axis=0).T
    upper = jnp.where(lane < row, flipped[:HALF, :], folded)
    below, above = pltpu.roll(folded, HALF, 1), pltpu.roll(flipped[:HALF, :], HALF, 1)
    inner = jnp.where(lane - HALF < row, below, jnp.where(lane - HALF == row, corner, above))
    return jnp.concatenate([upper, jnp.where(lane < HALF, flipped[HALF:, :], inner)], axis=0)


def gram_kernel(first_ref, *refs, counts, kept):
    groups, out_ref = refs[: len(counts)], refs[-1]
    out_ref[...] = refs[-2][...] if len(refs) > len(counts) + 1 else jnp.zeros(out_ref.shape, F32)
    lane = lax.broadcasted_iota(jnp.int32, (TAG, LANE), 1)
    where = [(ref, s, n) for ref, n in zip(groups, counts) for s in range(n)]
    codes = []
    for ref, s, n in where:
        tag = ref[n * BLOCK : n * BLOCK + TAG, :LANE].astype(F32)
        codes.append(jnp.max(jnp.where(lane == s, tag, 0.0)).astype(jnp.int32))
    for code, (ref, s, n) in zip(codes, where):
        local = code - 1 - first_ref[0]

        @pl.when((local >= 0) & (local < kept))
        def _(ref=ref, s=s, local=local):
            hidden = ref[s * BLOCK : (s + 1) * BLOCK, :]
            even, odd = 2 * local, 2 * local + 1
            for i, (chunk, base, tip, sides) in enumerate(
                ((even, 0, TIP, (HALF, HALF + LANE)), (odd, 0, TIP_ODD, (LANE,)), (odd, HALF, TIP_ODD + 1, ()))
            ):
                part = lax.dot_general(
                    hidden[:, i * LANE : (i + 1) * LANE],
                    hidden[:, i * LANE :],
                    TN,
                    preferred_element_type=F32,
                )
                folded, corner = fold(part[:, :LANE])
                out_ref[chunk, base : base + HALF, :] += folded
                out_ref[chunk, tip : tip + 1, :] += corner
                for j, side in enumerate(sides):
                    out_ref[chunk, side : side + LANE, :] += part[:, (j + 1) * LANE : (j + 2) * LANE]


def gram(first, kept, groups, prior=()):
    counts = [(g.shape[0] - TAG) // BLOCK for g in groups]
    return pl.pallas_call(
        lambda *refs: gram_kernel(*refs, counts=counts, kept=kept),
        in_specs=[pl.BlockSpec(memory_space=pltpu.SMEM)]
        + [pl.BlockSpec(memory_space=pltpu.VMEM)] * (len(groups) + len(prior)),
        out_specs=pl.BlockSpec(memory_space=pltpu.VMEM),
        out_shape=pltpu.VMEM((2 * kept, TIP + 8, LANE), F32),
        compiler_params=pltpu.CompilerParams(vmem_limit_bytes=VMEM_BYTES),
        name="gram",
    )(first, *[near(x) for x in (*groups, *prior)])


def factor_strip(groups, lane0, sub):
    wide = lambda v: jnp.concatenate([v] * (groups[0].shape[1] // LANE), axis=1)
    groups = list(groups)
    wide_sub = wide(sub)
    for b in range(len(groups)):
        base = lane0 + 8 * b
        cols = [
            [jnp.broadcast_to(g[:, base + j : base + j + 1], (8, LANE)) for g in groups[b:]]
            for j in range(8)
        ]
        for k in range(8):
            inv = lax.rsqrt(cols[k][0][k : k + 1, :])
            row = groups[b][k : k + 1, :] * wide(inv)
            mult = [jnp.where(sub > k, cols[k][0], 0.0)] + cols[k][1:]
            mult = [c * inv for c in mult]
            for g, m in enumerate(mult):
                groups[b + g] = groups[b + g] - wide(m) * row
            groups[b] = jnp.where(wide_sub == k, row, groups[b])
            for j in range(k + 1, 8):
                top = cols[j][0][k : k + 1, :] * inv
                cols[j] = [c - m * top for c, m in zip(cols[j], mult)]
    return groups


def dot_high(a, b, dims):
    return lax.dot_general(a, b, dims, precision=HIGH, preferred_element_type=F32)


def factor_panel(work):
    sub = lax.broadcasted_iota(jnp.int32, (8, LANE), 0)
    lane = lax.broadcasted_iota(jnp.int32, (8, LANE), 1)
    width = work.shape[1]
    for r0 in range(0, LANE, STRIP):
        r1 = r0 + STRIP
        groups = factor_strip([work[r : r + 8, :] for r in range(r0, r1, 8)], r0, sub)
        diag = jnp.concatenate(
            [
                jnp.where(lane >= r0 + 8 * g + sub, rows[:, :LANE], 0.0)
                for g, rows in enumerate(groups)
            ],
            axis=0,
        )
        strip = diag
        if width > LANE:
            right = jnp.concatenate([rows[:, LANE:] for rows in groups], axis=0)
            strip = jnp.concatenate([diag, right], axis=1)
        work[r0:r1, :] = strip
        if r1 < LANE:
            work[r1:, :] = work[r1:, :] - dot_high(diag.T[r1:, :], strip, (((1,), (0,)), ((), ())))


def diagonal(ref, base, tip, scale):
    tile = unfold(ref[base : base + HALF, :] * scale, ref[tip : tip + 1, :] * scale)
    eye = lax.broadcasted_iota(jnp.int32, tile.shape, 0) == lax.broadcasted_iota(
        jnp.int32, tile.shape, 1
    )
    return tile + jnp.where(eye, RIDGE, 0.0)


def first_kernel(part_ref, out_ref, *, scale):
    out_ref[:, :LANE] = diagonal(part_ref, 0, TIP, scale)
    for t in range(2):
        side = part_ref[HALF + t * LANE : HALF + (t + 1) * LANE, :]
        out_ref[:, (t + 1) * LANE : (t + 2) * LANE] = side * scale
    factor_panel(out_ref)


def first_panel(part, width, scale):
    return pl.pallas_call(
        lambda *refs: first_kernel(*refs, scale=scale),
        out_shape=pltpu.VMEM((LANE, width), F32),
        compiler_params=pltpu.CompilerParams(vmem_limit_bytes=VMEM_BYTES),
        name="first_panel",
    )(near(part))


def rest_kernel(part_ref, top_ref, out_ref, mid, low, *, scale):
    top = top_ref[...]
    mid[:, :LANE] = diagonal(part_ref, 0, TIP_ODD, scale)
    mid[:, LANE:] = part_ref[LANE : 2 * LANE, :] * scale
    mid[...] = mid[...] - dot_high(top[:, LANE : 2 * LANE], top[:, LANE:], TN)
    low[...] = diagonal(part_ref, HALF, TIP_ODD + 1, scale) - dot_high(
        top[:, 2 * LANE :], top[:, 2 * LANE :], TN
    )
    factor_panel(mid)
    right = mid[:, LANE:]
    low[...] = low[...] - dot_high(right, right, TN)
    factor_panel(low)
    kind = out_ref.dtype
    out_ref[:LANE, :] = top.astype(kind)
    out_ref[LANE : 2 * LANE, :LANE] = jnp.zeros((LANE, LANE), kind)
    out_ref[LANE : 2 * LANE, LANE:] = mid[...].astype(kind)
    out_ref[2 * LANE :, : 2 * LANE] = jnp.zeros((LANE, 2 * LANE), kind)
    out_ref[2 * LANE :, 2 * LANE :] = low[...].astype(kind)


def rest_panels(part, top, scale):
    width = top.shape[1]
    return pl.pallas_call(
        lambda *refs: rest_kernel(*refs, scale=scale),
        out_shape=pltpu.VMEM((width, width), BF16),
        scratch_shapes=[pltpu.VMEM((LANE, 2 * LANE), F32), pltpu.VMEM((LANE, LANE), F32)],
        compiler_params=pltpu.CompilerParams(vmem_limit_bytes=VMEM_BYTES),
        name="rest_panels",
    )(near(part), near(top))


def on_device(tokens, block_expert, gate_weight, up_weight):
    owners = lax.axis_size("expert")
    replicas = lax.axis_size("dp")
    experts_each, _, hidden_width = gate_weight.shape
    chips = owners // 2
    shifts = [(0, 0), (0, 1)] + [(dy, dc) for dc in range(2) for dy in (1, chips - 1)]
    shifts += [(2, 0), (2, 1)]
    member = lax.axis_index("expert").reshape(1)
    outgoing = pack(block_expert, member, tokens, experts_each, shifts, chips)
    pairs = [(d, d ^ SIDE) for d in range(replicas)]
    arrived, gathered = [], []
    for (dy, dc), payload in zip(shifts, outgoing):
        route = [
            (y * 2 + c, ((y + dy) % chips) * 2 + (c + dc) % 2)
            for y in range(chips)
            for c in range(2)
        ]
        if dy == 2:
            payload, arrived[1] = lax.optimization_barrier((payload, arrived[1]))
        arrived.append(payload if dy == dc == 0 else lax.ppermute(payload, "expert", route))
    weights = bring(arrived[1], gate_weight, up_weight)
    for g, (lo, hi) in enumerate(zip(EDGES, EDGES[1:])):
        blocks = arrived[lo:hi]
        if g == 1:
            blocks[0], gathered[0][1] = lax.optimization_barrier((blocks[0], gathered[0][1]))
        rows = hidden_rows(blocks, *weights)
        gathered.append([rows, lax.ppermute(rows, "dp", pairs)])
    kept = experts_each // 2
    first = (lax.axis_index("dp") // SIDE % 2 * kept).reshape(1)
    partial_gram = gram(first, kept, [rows for pair in gathered[:-1] for rows in pair])
    partial_gram = gram(first, kept, gathered[-1], (partial_gram,))
    classes = [[d for d in range(replicas) if d // SIDE % 2 == p] for p in range(2)]
    pieces = lax.all_to_all(
        partial_gram, "dp", split_axis=0, concat_axis=0, axis_index_groups=classes, tiled=True
    )
    own = jnp.sum(pieces, axis=0)
    other = lax.ppermute(own[: TIP_ODD + 8], "dp", [(d + 1, d) for d in range(0, replicas, 2)])
    scale = experts_each / (tokens.shape[0] * replicas)
    top = first_panel(own, hidden_width, scale)
    result = rest_panels(other, top, scale)
    row_count = hidden_width // replicas
    sent = result.reshape(replicas, row_count, hidden_width)
    returned = lax.all_to_all(sent, "dp", split_axis=0, concat_axis=0, tiled=True)
    returned = returned.reshape(2, 2, 2, 2, row_count, hidden_width)[:, :, :, 0]
    returned = jnp.swapaxes(returned, 0, 1).reshape(experts_each, row_count, hidden_width)
    return returned.astype(F32)


def solution(mesh):
    placed = (
        P(("dp", "expert"), None),
        P(("dp", "expert")),
        P("expert", None, None),
        P("expert", None, None),
    )

    return jax.shard_map(
        on_device, mesh=mesh, in_specs=placed, out_specs=P("expert", "dp", None), check_vma=False
    )
```

profile of v0, /device:TPU:0, one launch (start us, length us, event | category | flops | bytes accessed | tf_op | source)
XLA Modules:
  0.0 96.3 jit_solution(7365153742477109779)
XLA Ops:
  0.0 1.7 %pack.1 = (bf16[1040,128]{1,0:T(8,128)(2,1)S(1)}, bf16[1040,128]{1,0:T(8,128)(2,1)S(1)}, bf16[1040,128]{1,0:T(8,128)(2,1)S(1)}, bf16[1040,128]{1,0:T(8,128)(2,1)...) custom-call(s32[1]{0:T(128)} %bitcast.1.refs_0_, ...), custom_call_target="tpu_custom_call" | custom-call | tf_op jit(solution)/shard_map/pack/pallas_call | solution.py:68
  1.7 0.1 collective-permute-start
  1.8 1.8 %collective-permute-start.3 = (bf16[1040,128]{1,0:T(8,128)(2,1)S(1)}, bf16[1040,128]{1,0:T(8,128)(2,1)S(1)}, u32[]{:S(2)}, u32[]{:S(2)}) collective-permute-start(bf16[1040,128]{1,0:T(8,128)(2,1)S(1)} %get-tuple-element.30), channel_id=1, source_target_pairs={{0,2},{1,3},{2,4},{3,5},{4,6},{5,7},{6,0},{7,1},{8,10},{9,11},{10,... | collective-permute-start | bytes 798728 | tf_op jit(solution)/shard_map/ppermute | solution.py:339
  3.5 1.5 %collective-permute-start.5 = (bf16[1040,128]{1,0:T(8,128)(2,1)S(1)}, bf16[1040,128]{1,0:T(8,128)(2,1)S(1)}, u32[]{:S(2)}, u32[]{:S(2)}) collective-permute-start(bf16[1040,128]{1,0:T(8,128)(2,1)S(1)} %get-tuple-element.33), channel_id=1, source_target_pairs={{0,6},{1,7},{2,0},{3,1},{4,2},{5,3},{6,4},{7,5},{8,14},{9,15},{10,... | collective-permute-start | bytes 798728 | tf_op jit(solution)/shard_map/ppermute | solution.py:339
  5.1 0.0 collective-permute-start.6
  5.1 3.0 %collective-permute-start.7 = (bf16[1040,128]{1,0:T(8,128)(2,1)S(1)}, bf16[1040,128]{1,0:T(8,128)(2,1)S(1)}, u32[]{:S(2)}, u32[]{:S(2)}) collective-permute-start(bf16[1040,128]{1,0:T(8,128)(2,1)S(1)} %get-tuple-element.35), channel_id=1, source_target_pairs={{0,7},{1,6},{2,1},{3,0},{4,3},{5,2},{6,5},{7,4},{8,15},{9,14},{10,... | collective-permute-start | bytes 798728 | tf_op jit(solution)/shard_map/ppermute | solution.py:339
  8.0 4.6 %bring.1 = (bf16[8,1024,384]{2,1,0:T(8,128)(2,1)S(1)}, bf16[8,1024,384]{2,1,0:T(8,128)(2,1)S(1)}) custom-call(bf16[1040,128]{1,0:T(8,128)(2,1)S(1)} %collective-permute-done._.refs_1_, bf16[8,1024,384]{2,1,0:T(8,128)(2,1)} %gate_ref.1, bf16[8,1024,384]{2,1,0:T(8,128)(2,1)} %up_ref.1), custom_call_target="tpu_custom_call" | custom-call | tf_op jit(solution)/shard_map/bring/pallas_call | solution.py:138
  12.7 0.1 hidden.5.refs_1_
  12.8 1.7 %collective-permute-start.4 = (bf16[272,384]{1,0:T(8,128)(2,1)S(1)}, bf16[272,384]{1,0:T(8,128)(2,1)S(1)}, u32[]{:S(2)}, u32[]{:S(2)}) collective-permute-start(bf16[272,384]{1,0:T(8,128)(2,1)S(1)} %hidden.5.refs_1_), channel_id=1, source_target_pairs={{0,32},{8,40},{16,48},{24,56},{32,0},{40,8},{48,16},{56,24},{64,96... | collective-permute-start | bytes 626696 | tf_op jit(solution)/shard_map/ppermute | solution.py:346
  14.5 6.1 %collective-permute-done.4.refs_2_ = bf16[272,384]{1,0:T(8,128)(2,1)S(1)} collective-permute-done((bf16[272,384]{1,0:T(8,128)(2,1)S(1)}, bf16[272,384]{1,0:T(8,128)(2,1)S(1)}, u32[]{:S(2)}, u32[]{:S(2)}) %collective-permute-start.4) | collective-permute-done | bytes 208928 | tf_op jit(solution)/shard_map/ppermute | solution.py:346
  20.6 0.6 hidden.6.refs_3_
  21.2 1.8 %collective-permute-start.8 = (bf16[528,384]{1,0:T(8,128)(2,1)S(1)}, bf16[528,384]{1,0:T(8,128)(2,1)S(1)}, u32[]{:S(2)}, u32[]{:S(2)}) collective-permute-start(bf16[528,384]{1,0:T(8,128)(2,1)S(1)} %hidden.6.refs_3_), channel_id=1, source_target_pairs={{0,32},{8,40},{16,48},{24,56},{32,0},{40,8},{48,16},{56,24},{64,96... | collective-permute-start | bytes 1216520 | tf_op jit(solution)/shard_map/ppermute | solution.py:346
  23.0 0.3 collective-permute-start.9
  23.3 2.2 %collective-permute-start.1 = (bf16[1040,128]{1,0:T(8,128)(2,1)S(1)}, bf16[1040,128]{1,0:T(8,128)(2,1)S(1)}, u32[]{:S(2)}, u32[]{:S(2)}) collective-permute-start(bf16[1040,128]{1,0:T(8,128)(2,1)S(1)} %get-tuple-element.25), channel_id=1, source_target_pairs={{0,5},{1,4},{2,7},{3,6},{4,1},{5,0},{6,3},{7,2},{8,13},{9,12},{10,... | collective-permute-start | bytes 798728 | tf_op jit(solution)/shard_map/ppermute | solution.py:339
  25.6 8.3 %collective-permute-done.9.refs_0_ = bf16[1040,128]{1,0:T(8,128)(2,1)S(1)} collective-permute-done((bf16[1040,128]{1,0:T(8,128)(2,1)S(1)}, bf16[1040,128]{1,0:T(8,128)(2,1)S(1)}, u32[]{:S(2)}, u32[]{:S(2)}) %collective-permute-start.9) | collective-permute-done | bytes 266272 | tf_op jit(solution)/shard_map/ppermute | solution.py:339
  33.8 0.1 hidden.7.refs_5_
  33.9 0.8 collective-permute-start.10
  34.7 2.2 %collective-permute-done.1.refs_0_ = bf16[1040,128]{1,0:T(8,128)(2,1)S(1)} collective-permute-done((bf16[1040,128]{1,0:T(8,128)(2,1)S(1)}, bf16[1040,128]{1,0:T(8,128)(2,1)S(1)}, u32[]{:S(2)}, u32[]{:S(2)}) %collective-permute-start.1) | collective-permute-done | bytes 266272 | tf_op jit(solution)/shard_map/ppermute | solution.py:339
  36.9 0.6 hidden.4.refs_1_
  37.5 0.5 collective-permute-start.2
  38.0 0.8 collective-permute-done.10.refs_6_
  38.8 1.2 %gram.2.refs_3_ = f32[8,328,128]{2,1,0:T(8,128)S(1)} custom-call(s32[1]{0:T(128)} %bitcast.refs_0_, bf16[272,384]{1,0:T(8,128)(2,1)S(1)} %hidden.5.refs_1_, bf16[272,384]{1,0:T(8,128)(2,1)S(1)} %collective-permute-done.4.refs_2_, bf16[528,384]{1,0:T(8,128)(2,1)S(1)} %hidden.6.refs_3_, bf16[528,384]{1,0:T(8,128)(2,1)S(1)} %collective-permute-done.8.refs_4_, ...), custom_call_target="tpu_custom_call" | custom-call | tf_op jit(solution)/shard_map/gram/pallas_call | solution.py:202
  39.9 3.4 %collective-permute-done.2.refs_2_ = bf16[144,384]{1,0:T(8,128)(2,1)S(1)} collective-permute-done((bf16[144,384]{1,0:T(8,128)(2,1)S(1)}, bf16[144,384]{1,0:T(8,128)(2,1)S(1)}, u32[]{:S(2)}, u32[]{:S(2)}) %collective-permute-start.2) | collective-permute-done | bytes 110624 | tf_op jit(solution)/shard_map/ppermute | solution.py:346
  43.3 0.7 gram.3
  44.1 25.8 %all_to_all.10 = f32[8,328,128]{2,1,0:T(8,128)S(1)} all-to-all(f32[8,328,128]{2,1,0:T(8,128)S(1)} %gram.3), channel_id=1, replica_groups={{0,8,16,24,64,72,80,88},{32,40,48,56,96,104,112,120},{1,9,17,25,65,73,8..., dimensions={0} | all-to-all | bytes 2686976 | tf_op jit(solution)/shard_map/all_to_all | solution.py:352
  69.9 0.1 reduce_sum.9.refs_0_
  70.0 1.5 %collective-permute-start.11 = (f32[264,128]{1,0:T(8,128)S(1)}, f32[264,128]{1,0:T(8,128)S(1)}, u32[]{:S(2)}, u32[]{:S(2)}) collective-permute-start(f32[264,128]{1,0:T(8,128)S(1)} %slice.8), channel_id=1, source_target_pairs={{8,0},{24,16},{40,32},{56,48},{72,64},{88,80},{104,96},{120,112},{... | collective-permute-start | bytes 405512 | tf_op jit(solution)/shard_map/ppermute | solution.py:356
  71.4 3.3 %first_panel.1.refs_1_ = f32[128,384]{1,0:T(8,128)S(1)} custom-call(f32[328,128]{1,0:T(8,128)S(1)} %reduce_sum.9.refs_0_), custom_call_target="tpu_custom_call" | custom-call | tf_op jit(solution)/shard_map/first_panel/pallas_call | solution.py:281
  74.8 2.1 %collective-permute-done.11.refs_0_ = f32[264,128]{1,0:T(8,128)S(1)} collective-permute-done((f32[264,128]{1,0:T(8,128)S(1)}, f32[264,128]{1,0:T(8,128)S(1)}, u32[]{:S(2)}, u32[]{:S(2)}) %collective-permute-start.11) | collective-permute-done | bytes 135200 | tf_op jit(solution)/shard_map/ppermute | solution.py:356
  76.9 7.1 %rest_panels.1 = bf16[384,384]{1,0:T(8,128)(2,1)S(1)} custom-call(f32[264,128]{1,0:T(8,128)S(1)} %collective-permute-done.11.refs_0_, f32[128,384]{1,0:T(8,128)S(1)} %first_panel.1.refs_1_), custom_call_target="tpu_custom_call" | custom-call | tf_op jit(solution)/shard_map/rest_panels/pallas_call | solution.py:311
  83.9 11.6 %all_to_all.11 = bf16[16,24,384]{2,1,0:T(8,128)(2,1)S(1)} all-to-all(bf16[16,24,384]{2,1,0:T(8,128)(2,1)S(1)} %bitcast.12), channel_id=1, replica_groups=mesh['dp'=16,'expert'=8] {'dp'}, dimensions={0} | all-to-all | bytes 589824 | tf_op jit(solution)/shard_map/all_to_all | solution.py:362
  95.6 0.7 fusion
  (7 shorter events, 0.0 us)
Async XLA Ops:
  1.7 6.4 %collective-permute-start = (bf16[1040,128]{1,0:T(8,128)(2,1)S(1)}, bf16[1040,128]{1,0:T(8,128)(2,1)S(1)}, u32[]{:S(2)}, u32[]{:S(2)}) collective-permute-start(bf16[1040,128]{1,0:T(8,128)(2,1)S(1)} %get-tuple-element.23), channel_id=1, source_target_pairs={{0,1},{1,0},{2,3},{3,2},{4,5},{5,4},{6,7},{7,6},{8,9},{9,8},{10,11... | collective-permute-start | bytes 798728 | tf_op jit(solution)/shard_map/ppermute | solution.py:339
  1.8 12.7 %collective-permute-start.3 = (bf16[1040,128]{1,0:T(8,128)(2,1)S(1)}, bf16[1040,128]{1,0:T(8,128)(2,1)S(1)}, u32[]{:S(2)}, u32[]{:S(2)}) collective-permute-start(bf16[1040,128]{1,0:T(8,128)(2,1)S(1)} %get-tuple-element.30), channel_id=1, source_target_pairs={{0,2},{1,3},{2,4},{3,5},{4,6},{5,7},{6,0},{7,1},{8,10},{9,11},{10,... | collective-permute-start | bytes 798728 | tf_op jit(solution)/shard_map/ppermute | solution.py:339
  3.5 17.1 %collective-permute-start.5 = (bf16[1040,128]{1,0:T(8,128)(2,1)S(1)}, bf16[1040,128]{1,0:T(8,128)(2,1)S(1)}, u32[]{:S(2)}, u32[]{:S(2)}) collective-permute-start(bf16[1040,128]{1,0:T(8,128)(2,1)S(1)} %get-tuple-element.33), channel_id=1, source_target_pairs={{0,6},{1,7},{2,0},{3,1},{4,2},{5,3},{6,4},{7,5},{8,14},{9,15},{10,... | collective-permute-start | bytes 798728 | tf_op jit(solution)/shard_map/ppermute | solution.py:339
  5.1 15.6 %collective-permute-start.6 = (bf16[1040,128]{1,0:T(8,128)(2,1)S(1)}, bf16[1040,128]{1,0:T(8,128)(2,1)S(1)}, u32[]{:S(2)}, u32[]{:S(2)}) collective-permute-start(bf16[1040,128]{1,0:T(8,128)(2,1)S(1)} %get-tuple-element.34), channel_id=1, source_target_pairs={{0,3},{1,2},{2,5},{3,4},{4,7},{5,6},{6,1},{7,0},{8,11},{9,10},{10,... | collective-permute-start | bytes 798728 | tf_op jit(solution)/shard_map/ppermute | solution.py:339
  5.1 15.6 %collective-permute-start.7 = (bf16[1040,128]{1,0:T(8,128)(2,1)S(1)}, bf16[1040,128]{1,0:T(8,128)(2,1)S(1)}, u32[]{:S(2)}, u32[]{:S(2)}) collective-permute-start(bf16[1040,128]{1,0:T(8,128)(2,1)S(1)} %get-tuple-element.35), channel_id=1, source_target_pairs={{0,7},{1,6},{2,1},{3,0},{4,3},{5,2},{6,5},{7,4},{8,15},{9,14},{10,... | collective-permute-start | bytes 798728 | tf_op jit(solution)/shard_map/ppermute | solution.py:339
  12.8 7.8 %collective-permute-start.4 = (bf16[272,384]{1,0:T(8,128)(2,1)S(1)}, bf16[272,384]{1,0:T(8,128)(2,1)S(1)}, u32[]{:S(2)}, u32[]{:S(2)}) collective-permute-start(bf16[272,384]{1,0:T(8,128)(2,1)S(1)} %hidden.5.refs_1_), channel_id=1, source_target_pairs={{0,32},{8,40},{16,48},{24,56},{32,0},{40,8},{48,16},{56,24},{64,96... | collective-permute-start | bytes 626696 | tf_op jit(solution)/shard_map/ppermute | solution.py:346
  21.2 17.6 %collective-permute-start.8 = (bf16[528,384]{1,0:T(8,128)(2,1)S(1)}, bf16[528,384]{1,0:T(8,128)(2,1)S(1)}, u32[]{:S(2)}, u32[]{:S(2)}) collective-permute-start(bf16[528,384]{1,0:T(8,128)(2,1)S(1)} %hidden.6.refs_3_), channel_id=1, source_target_pairs={{0,32},{8,40},{16,48},{24,56},{32,0},{40,8},{48,16},{56,24},{64,96... | collective-permute-start | bytes 1216520 | tf_op jit(solution)/shard_map/ppermute | solution.py:346
  23.0 10.8 %collective-permute-start.9 = (bf16[1040,128]{1,0:T(8,128)(2,1)S(1)}, bf16[1040,128]{1,0:T(8,128)(2,1)S(1)}, u32[]{:S(2)}, u32[]{:S(2)}) collective-permute-start(bf16[1040,128]{1,0:T(8,128)(2,1)S(1)} %get-tuple-element.36), channel_id=1, source_target_pairs={{0,4},{1,5},{2,6},{3,7},{4,0},{5,1},{6,2},{7,3},{8,12},{9,13},{10,... | collective-permute-start | bytes 798728 | tf_op jit(solution)/shard_map/ppermute | solution.py:339
  23.3 13.6 %collective-permute-start.1 = (bf16[1040,128]{1,0:T(8,128)(2,1)S(1)}, bf16[1040,128]{1,0:T(8,128)(2,1)S(1)}, u32[]{:S(2)}, u32[]{:S(2)}) collective-permute-start(bf16[1040,128]{1,0:T(8,128)(2,1)S(1)} %get-tuple-element.25), channel_id=1, source_target_pairs={{0,5},{1,4},{2,7},{3,6},{4,1},{5,0},{6,3},{7,2},{8,13},{9,12},{10,... | collective-permute-start | bytes 798728 | tf_op jit(solution)/shard_map/ppermute | solution.py:339
  33.9 4.8 %collective-permute-start.10 = (bf16[144,384]{1,0:T(8,128)(2,1)S(1)}, bf16[144,384]{1,0:T(8,128)(2,1)S(1)}, u32[]{:S(2)}, u32[]{:S(2)}) collective-permute-start(bf16[144,384]{1,0:T(8,128)(2,1)S(1)} %hidden.7.refs_5_), channel_id=1, source_target_pairs={{0,32},{8,40},{16,48},{24,56},{32,0},{40,8},{48,16},{56,24},{64,96... | collective-permute-start | bytes 331784 | tf_op jit(solution)/shard_map/ppermute | solution.py:346
  37.5 5.8 %collective-permute-start.2 = (bf16[144,384]{1,0:T(8,128)(2,1)S(1)}, bf16[144,384]{1,0:T(8,128)(2,1)S(1)}, u32[]{:S(2)}, u32[]{:S(2)}) collective-permute-start(bf16[144,384]{1,0:T(8,128)(2,1)S(1)} %hidden.4.refs_1_), channel_id=1, source_target_pairs={{0,32},{8,40},{16,48},{24,56},{32,0},{40,8},{48,16},{56,24},{64,96... | collective-permute-start | bytes 331784 | tf_op jit(solution)/shard_map/ppermute | solution.py:346
  70.0 6.9 %collective-permute-start.11 = (f32[264,128]{1,0:T(8,128)S(1)}, f32[264,128]{1,0:T(8,128)S(1)}, u32[]{:S(2)}, u32[]{:S(2)}) collective-permute-start(f32[264,128]{1,0:T(8,128)S(1)} %slice.8), channel_id=1, source_target_pairs={{8,0},{24,16},{40,32},{56,48},{72,64},{88,80},{104,96},{120,112},{... | collective-permute-start | bytes 405512 | tf_op jit(solution)/shard_map/ppermute | solution.py:356
where the time goes:
time: 96.5 us; the launch traced here: 96.3 us
  blocking collectives  37.4 us (39%)
  waiting for transfers between devices  22.8 us (24%)
  Pallas kernels  20 us (21%)
  starting transfers between devices  15.2 us (16%)
    all_to_all x1, blocking collectives, on_device(): lax.all_to_all(partial_gram, 'dp', split_axis=0, concat_axis=0, axis_inde...  25.8 us
    all_to_all x1, blocking collectives, on_device(): lax.all_to_all(sent, 'dp', split_axis=0, concat_axis=0, tiled=True)  11.6 us
    ppermute x7, waiting for transfers between devices, on_device(): lax.ppermute(payload, 'expert', route)  10.4 us
    ppermute x4, waiting for transfers between devices, on_device(): gathered.append([rows, lax.ppermute(rows, 'dp', pairs)])  10.3 us
    ppermute x7, starting transfers between devices, on_device(): lax.ppermute(payload, 'expert', route)  8.86 us
    pallas_call x1, Pallas kernels, rest_panels(): pl.pallas_call(lambda *refs: rest_kernel(*refs, scale=scale), out_shape=p...  7.05 us
    ppermute x4, starting transfers between devices, on_device(): gathered.append([rows, lax.ppermute(rows, 'dp', pairs)])  4.84 us
    pallas_call x1, Pallas kernels, bring(): pl.pallas_call(bring_kernel, in_specs=[pl.BlockSpec(memory_space=pl.ANY)]...  4.62 us
  transfers between devices with their start and end apart: 12, of which 6 were waited for; matrix products, arithmetic and copies ran while one was open for 0% of the time, Pallas kernels for 10%

commit v1 on v0

--- a/solution.py
+++ b/solution.py
@@ -12,7 +12,7 @@
 TAG = 16
 SIDE = 4
 VMEM_BYTES = 20 << 20
-EDGES = (0, 2, 6, 7, 8)
+EDGES = (0, 2, 4, 6, 7, 8)
 STRIP = 64
 F32 = jnp.float32
 BF16 = jnp.bfloat16
@@ -328,22 +328,25 @@
     outgoing = pack(block_expert, member, tokens, experts_each, shifts, chips)
     pairs = [(d, d ^ SIDE) for d in range(replicas)]
     arrived, gathered = [], []
+    weights = bring(outgoing[0], gate_weight, up_weight)
+
+    def swap_rows(g):
+        rows = hidden_rows(arrived[EDGES[g] : EDGES[g + 1]], *weights)
+        gathered.append([rows, lax.ppermute(rows, "dp", pairs)])
+
     for (dy, dc), payload in zip(shifts, outgoing):
         route = [
             (y * 2 + c, ((y + dy) % chips) * 2 + (c + dc) % 2)
             for y in range(chips)
             for c in range(2)
         ]
+        if dy == 2 and not gathered:
+            swap_rows(0)
         if dy == 2:
-            payload, arrived[1] = lax.optimization_barrier((payload, arrived[1]))
+            payload, _ = lax.optimization_barrier((payload, gathered[0][0]))
         arrived.append(payload if dy == dc == 0 else lax.ppermute(payload, "expert", route))
-    weights = bring(arrived[1], gate_weight, up_weight)
-    for g, (lo, hi) in enumerate(zip(EDGES, EDGES[1:])):
-        blocks = arrived[lo:hi]
-        if g == 1:
-            blocks[0], gathered[0][1] = lax.optimization_barrier((blocks[0], gathered[0][1]))
-        rows = hidden_rows(blocks, *weights)
-        gathered.append([rows, lax.ppermute(rows, "dp", pairs)])
+    for g in range(1, len(EDGES) - 1):
+        swap_rows(g)
     kept = experts_each // 2
     first = (lax.axis_index("dp") // SIDE % 2 * kept).reshape(1)
     partial_gram = gram(first, kept, [rows for pair in gathered[:-1] for rows in pair])

time: 96.5 us -> 94.1 us (0.975)
  waiting for transfers between devices: 22.8 us -> 13.1 us
  starting transfers between devices: 15.2 us -> 18.9 us
  blocking collectives: 37.4 us -> 40.8 us
    ppermute x4 -> x5, waiting for transfers between devices: 10.3 us -> 4.51 us  [swap_rows(): gathered.append([rows, lax.ppermute(rows, 'dp', pairs)])]
    ppermute x7, waiting for transfers between devices: 10.4 us -> 6.52 us  [on_device(): lax.ppermute(payload, 'expert', route)]
    all_to_all x1, blocking collectives: 25.8 us -> 29.6 us  [on_device(): lax.all_to_all(partial_gram, 'dp', split_axis=0, concat_axis=0, axis_inde...]
    ppermute x4 -> x5, starting transfers between devices: 4.84 us -> 7.69 us  [swap_rows(): gathered.append([rows, lax.ppermute(rows, 'dp', pairs)])]
  transfers between devices with their start and end apart: 12 -> 13, of which waited for: 6 -> 6; matrix products, arithmetic and copies ran while one was open for 0% -> 0% of each run, Pallas kernels for 10% -> 11%
where the time goes in v1:
time: 94.1 us; the launch traced here: 93.9 us
  blocking collectives  40.8 us (43%)
  Pallas kernels  20.1 us (21%)
  starting transfers between devices  18.9 us (20%)
  waiting for transfers between devices  13.1 us (14%)
    all_to_all x1, blocking collectives, on_device(): lax.all_to_all(partial_gram, 'dp', split_axis=0, concat_axis=0, axis_inde...  29.6 us
    all_to_all x1, blocking collectives, on_device(): lax.all_to_all(sent, 'dp', split_axis=0, concat_axis=0, tiled=True)  11.2 us
    ppermute x7, starting transfers between devices, on_device(): lax.ppermute(payload, 'expert', route)  9.75 us
    ppermute x5, starting transfers between devices, swap_rows(): gathered.append([rows, lax.ppermute(rows, 'dp', pairs)])  7.69 us
    pallas_call x1, Pallas kernels, rest_panels(): pl.pallas_call(lambda *refs: rest_kernel(*refs, scale=scale), out_shape=p...  7.05 us
    ppermute x7, waiting for transfers between devices, on_device(): lax.ppermute(payload, 'expert', route)  6.52 us
    pallas_call x1, Pallas kernels, bring(): pl.pallas_call(bring_kernel, in_specs=[pl.BlockSpec(memory_space=pl.ANY)]...  4.62 us
    ppermute x5, waiting for transfers between devices, swap_rows(): gathered.append([rows, lax.ppermute(rows, 'dp', pairs)])  4.51 us
  transfers between devices with their start and end apart: 13, of which 6 were waited for; matrix products, arithmetic and copies ran while one was open for 0% of the time, Pallas kernels for 11%

profile of v1, /device:TPU:0, one launch (start us, length us, event | category | flops | bytes accessed | tf_op | source)
XLA Modules:
  0.0 93.9 jit_solution(17339129546090567673)
XLA Ops:
  0.0 1.7 %pack.1 = (bf16[1040,128]{1,0:T(8,128)(2,1)S(1)}, bf16[1040,128]{1,0:T(8,128)(2,1)S(1)}, bf16[1040,128]{1,0:T(8,128)(2,1)S(1)}, bf16[1040,128]{1,0:T(8,128)(2,1)...) custom-call(s32[1]{0:T(128)} %bitcast.1.refs_0_, ...), custom_call_target="tpu_custom_call" | custom-call | tf_op jit(solution)/shard_map/pack/pallas_call | solution.py:68
  1.7 0.1 collective-permute-start
  1.8 1.8 %collective-permute-start.4 = (bf16[1040,128]{1,0:T(8,128)(2,1)S(1)}, bf16[1040,128]{1,0:T(8,128)(2,1)S(1)}, u32[]{:S(2)}, u32[]{:S(2)}) collective-permute-start(bf16[1040,128]{1,0:T(8,128)(2,1)S(1)} %get-tuple-element.23), channel_id=1, source_target_pairs={{0,2},{1,3},{2,4},{3,5},{4,6},{5,7},{6,0},{7,1},{8,10},{9,11},{10,... | collective-permute-start | bytes 798728 | tf_op jit(solution)/shard_map/ppermute | solution.py:347
  3.5 1.5 %collective-permute-start.5 = (bf16[1040,128]{1,0:T(8,128)(2,1)S(1)}, bf16[1040,128]{1,0:T(8,128)(2,1)S(1)}, u32[]{:S(2)}, u32[]{:S(2)}) collective-permute-start(bf16[1040,128]{1,0:T(8,128)(2,1)S(1)} %get-tuple-element.24), channel_id=1, source_target_pairs={{0,6},{1,7},{2,0},{3,1},{4,2},{5,3},{6,4},{7,5},{8,14},{9,15},{10,... | collective-permute-start | bytes 798728 | tf_op jit(solution)/shard_map/ppermute | solution.py:347
  5.1 3.0 %collective-permute-start.8 = (bf16[1040,128]{1,0:T(8,128)(2,1)S(1)}, bf16[1040,128]{1,0:T(8,128)(2,1)S(1)}, u32[]{:S(2)}, u32[]{:S(2)}) collective-permute-start(bf16[1040,128]{1,0:T(8,128)(2,1)S(1)} %get-tuple-element.26), channel_id=1, source_target_pairs={{0,7},{1,6},{2,1},{3,0},{4,3},{5,2},{6,5},{7,4},{8,15},{9,14},{10,... | collective-permute-start | bytes 798728 | tf_op jit(solution)/shard_map/ppermute | solution.py:347
  8.0 4.6 %bring.1 = (bf16[8,1024,384]{2,1,0:T(8,128)(2,1)S(1)}, bf16[8,1024,384]{2,1,0:T(8,128)(2,1)S(1)}) custom-call(bf16[1040,128]{1,0:T(8,128)(2,1)S(1)} %get-tuple-element.18._.refs_0_, bf16[8,1024,384]{2,1,0:T(8,128)(2,1)} %gate_ref.1, bf16[8,1024,384]{2,1,0:T(8,128)(2,1)} %up_ref.1), custom_call_target="tpu_custom_call" | custom-call | tf_op jit(solution)/shard_map/bring/pallas_call | solution.py:138
  12.7 0.1 hidden.5.refs_1_
  12.8 1.4 %collective-permute-start.10 = (bf16[1040,128]{1,0:T(8,128)(2,1)S(1)}, bf16[1040,128]{1,0:T(8,128)(2,1)S(1)}, u32[]{:S(2)}, u32[]{:S(2)}) collective-permute-start(bf16[1040,128]{1,0:T(8,128)(2,1)S(1)} %get-tuple-element.28), channel_id=1, source_target_pairs={{0,4},{1,5},{2,6},{3,7},{4,0},{5,1},{6,2},{7,3},{8,12},{9,13},{10,... | collective-permute-start | bytes 798728 | tf_op jit(solution)/shard_map/ppermute | solution.py:347
  14.2 2.0 %collective-permute-start.1 = (bf16[1040,128]{1,0:T(8,128)(2,1)S(1)}, bf16[1040,128]{1,0:T(8,128)(2,1)S(1)}, u32[]{:S(2)}, u32[]{:S(2)}) collective-permute-start(bf16[1040,128]{1,0:T(8,128)(2,1)S(1)} %get-tuple-element.22), channel_id=1, source_target_pairs={{0,5},{1,4},{2,7},{3,6},{4,1},{5,0},{6,3},{7,2},{8,13},{9,12},{10,... | collective-permute-start | bytes 798728 | tf_op jit(solution)/shard_map/ppermute | solution.py:347
  16.2 0.6 hidden.7.refs_3_
  16.8 2.0 %collective-permute-start.6 = (bf16[272,384]{1,0:T(8,128)(2,1)S(1)}, bf16[272,384]{1,0:T(8,128)(2,1)S(1)}, u32[]{:S(2)}, u32[]{:S(2)}) collective-permute-start(bf16[272,384]{1,0:T(8,128)(2,1)S(1)} %hidden.7.refs_3_), channel_id=1, source_target_pairs={{0,32},{8,40},{16,48},{24,56},{32,0},{40,8},{48,16},{56,24},{64,96... | collective-permute-start | bytes 626696 | tf_op jit(solution)/shard_map/ppermute | solution.py:335
  18.8 0.1 hidden.8.refs_5_
  18.9 0.5 collective-permute-start.9
  19.5 1.6 %collective-permute-start.3 = (bf16[272,384]{1,0:T(8,128)(2,1)S(1)}, bf16[272,384]{1,0:T(8,128)(2,1)S(1)}, u32[]{:S(2)}, u32[]{:S(2)}) collective-permute-start(bf16[272,384]{1,0:T(8,128)(2,1)S(1)} %hidden.5.refs_1_), channel_id=1, source_target_pairs={{0,32},{8,40},{16,48},{24,56},{32,0},{40,8},{48,16},{56,24},{64,96... | collective-permute-start | bytes 626696 | tf_op jit(solution)/shard_map/ppermute | solution.py:335
  21.0 4.0 %collective-permute-done.10.refs_0_ = bf16[1040,128]{1,0:T(8,128)(2,1)S(1)} collective-permute-done((bf16[1040,128]{1,0:T(8,128)(2,1)S(1)}, bf16[1040,128]{1,0:T(8,128)(2,1)S(1)}, u32[]{:S(2)}, u32[]{:S(2)}) %collective-permute-start.10) | collective-permute-done | bytes 266272 | tf_op jit(solution)/shard_map/ppermute | solution.py:347
  25.1 0.1 hidden.9.refs_7_
  25.2 2.0 %collective-permute-start.11 = (bf16[144,384]{1,0:T(8,128)(2,1)S(1)}, bf16[144,384]{1,0:T(8,128)(2,1)S(1)}, u32[]{:S(2)}, u32[]{:S(2)}) collective-permute-start(bf16[144,384]{1,0:T(8,128)(2,1)S(1)} %hidden.9.refs_7_), channel_id=1, source_target_pairs={{0,32},{8,40},{16,48},{24,56},{32,0},{40,8},{48,16},{56,24},{64,96... | collective-permute-start | bytes 331784 | tf_op jit(solution)/shard_map/ppermute | solution.py:335
  27.2 2.5 %collective-permute-done.1.refs_0_ = bf16[1040,128]{1,0:T(8,128)(2,1)S(1)} collective-permute-done((bf16[1040,128]{1,0:T(8,128)(2,1)S(1)}, bf16[1040,128]{1,0:T(8,128)(2,1)S(1)}, u32[]{:S(2)}, u32[]{:S(2)}) %collective-permute-start.1) | collective-permute-done | bytes 266272 | tf_op jit(solution)/shard_map/ppermute | solution.py:347
  29.7 0.6 hidden.6.refs_1_
  30.2 1.6 %collective-permute-start.2 = (bf16[144,384]{1,0:T(8,128)(2,1)S(1)}, bf16[144,384]{1,0:T(8,128)(2,1)S(1)}, u32[]{:S(2)}, u32[]{:S(2)}) collective-permute-start(bf16[144,384]{1,0:T(8,128)(2,1)S(1)} %hidden.6.refs_1_), channel_id=1, source_target_pairs={{0,32},{8,40},{16,48},{24,56},{32,0},{40,8},{48,16},{56,24},{64,96... | collective-permute-start | bytes 331784 | tf_op jit(solution)/shard_map/ppermute | solution.py:335
  31.8 2.0 %collective-permute-done.3.refs_2_ = bf16[272,384]{1,0:T(8,128)(2,1)S(1)} collective-permute-done((bf16[272,384]{1,0:T(8,128)(2,1)S(1)}, bf16[272,384]{1,0:T(8,128)(2,1)S(1)}, u32[]{:S(2)}, u32[]{:S(2)}) %collective-permute-start.3) | collective-permute-done | bytes 208928 | tf_op jit(solution)/shard_map/ppermute | solution.py:335
  33.9 2.4 %collective-permute-done.11.refs_8_ = bf16[144,384]{1,0:T(8,128)(2,1)S(1)} collective-permute-done((bf16[144,384]{1,0:T(8,128)(2,1)S(1)}, bf16[144,384]{1,0:T(8,128)(2,1)S(1)}, u32[]{:S(2)}, u32[]{:S(2)}) %collective-permute-start.11) | collective-permute-done | bytes 110624 | tf_op jit(solution)/shard_map/ppermute | solution.py:335
  36.2 1.2 %gram.2.refs_3_ = f32[8,328,128]{2,1,0:T(8,128)S(1)} custom-call(s32[1]{0:T(128)} %bitcast.refs_0_, bf16[272,384]{1,0:T(8,128)(2,1)S(1)} %hidden.5.refs_1_, bf16[272,384]{1,0:T(8,128)(2,1)S(1)} %collective-permute-done.3.refs_2_, bf16[272,384]{1,0:T(8,128)(2,1)S(1)} %hidden.7.refs_3_, bf16[272,384]{1,0:T(8,128)(2,1)S(1)} %collective-permute-done.6.refs_4_, ...), custom_call_target="tpu_custom_call" | custom-call | tf_op jit(solution)/shard_map/gram/pallas_call | solution.py:202
  37.4 0.1 collective-permute-done.2.refs_2_
  37.5 0.7 gram.3
  38.3 29.6 %all_to_all.10 = f32[8,328,128]{2,1,0:T(8,128)S(1)} all-to-all(f32[8,328,128]{2,1,0:T(8,128)S(1)} %gram.3), channel_id=1, replica_groups={{0,8,16,24,64,72,80,88},{32,40,48,56,96,104,112,120},{1,9,17,25,65,73,8..., dimensions={0} | all-to-all | bytes 2686976 | tf_op jit(solution)/shard_map/all_to_all | solution.py:355
  67.9 1.5 %collective-permute-start.12 = (f32[264,128]{1,0:T(8,128)S(1)}, f32[264,128]{1,0:T(8,128)S(1)}, u32[]{:S(2)}, u32[]{:S(2)}) collective-permute-start(f32[264,128]{1,0:T(8,128)S(1)} %slice.8), channel_id=1, source_target_pairs={{8,0},{24,16},{40,32},{56,48},{72,64},{88,80},{104,96},{120,112},{... | collective-permute-start | bytes 405512 | tf_op jit(solution)/shard_map/ppermute | solution.py:359
  69.4 3.3 %first_panel.1.refs_1_ = f32[128,384]{1,0:T(8,128)S(1)} custom-call(f32[328,128]{1,0:T(8,128)S(1)} %reduce_sum.9.refs_0_), custom_call_target="tpu_custom_call" | custom-call | tf_op jit(solution)/shard_map/first_panel/pallas_call | solution.py:281
  72.7 2.1 %collective-permute-done.12.refs_0_ = f32[264,128]{1,0:T(8,128)S(1)} collective-permute-done((f32[264,128]{1,0:T(8,128)S(1)}, f32[264,128]{1,0:T(8,128)S(1)}, u32[]{:S(2)}, u32[]{:S(2)}) %collective-permute-start.12) | collective-permute-done | bytes 135200 | tf_op jit(solution)/shard_map/ppermute | solution.py:359
  74.8 7.0 %rest_panels.1 = bf16[384,384]{1,0:T(8,128)(2,1)S(1)} custom-call(f32[264,128]{1,0:T(8,128)S(1)} %collective-permute-done.12.refs_0_, f32[128,384]{1,0:T(8,128)S(1)} %first_panel.1.refs_1_), custom_call_target="tpu_custom_call" | custom-call | tf_op jit(solution)/shard_map/rest_panels/pallas_call | solution.py:311
  81.9 11.2 %all_to_all.11 = bf16[16,24,384]{2,1,0:T(8,128)(2,1)S(1)} all-to-all(bf16[16,24,384]{2,1,0:T(8,128)(2,1)S(1)} %bitcast.12), channel_id=1, replica_groups=mesh['dp'=16,'expert'=8] {'dp'}, dimensions={0} | all-to-all | bytes 589824 | tf_op jit(solution)/shard_map/all_to_all | solution.py:365
  93.1 0.7 fusion
  (10 shorter events, 0.1 us)
Async XLA Ops:
  1.7 11.0 %collective-permute-start = (bf16[1040,128]{1,0:T(8,128)(2,1)S(1)}, bf16[1040,128]{1,0:T(8,128)(2,1)S(1)}, u32[]{:S(2)}, u32[]{:S(2)}) collective-permute-start(bf16[1040,128]{1,0:T(8,128)(2,1)S(1)} %get-tuple-element.19), channel_id=1, source_target_pairs={{0,1},{1,0},{2,3},{3,2},{4,5},{5,4},{6,7},{7,6},{8,9},{9,8},{10,11... | collective-permute-start | bytes 798728 | tf_op jit(solution)/shard_map/ppermute | solution.py:347
  1.8 12.4 %collective-permute-start.4 = (bf16[1040,128]{1,0:T(8,128)(2,1)S(1)}, bf16[1040,128]{1,0:T(8,128)(2,1)S(1)}, u32[]{:S(2)}, u32[]{:S(2)}) collective-permute-start(bf16[1040,128]{1,0:T(8,128)(2,1)S(1)} %get-tuple-element.23), channel_id=1, source_target_pairs={{0,2},{1,3},{2,4},{3,5},{4,6},{5,7},{6,0},{7,1},{8,10},{9,11},{10,... | collective-permute-start | bytes 798728 | tf_op jit(solution)/shard_map/ppermute | solution.py:347
  3.5 12.7 %collective-permute-start.5 = (bf16[1040,128]{1,0:T(8,128)(2,1)S(1)}, bf16[1040,128]{1,0:T(8,128)(2,1)S(1)}, u32[]{:S(2)}, u32[]{:S(2)}) collective-permute-start(bf16[1040,128]{1,0:T(8,128)(2,1)S(1)} %get-tuple-element.24), channel_id=1, source_target_pairs={{0,6},{1,7},{2,0},{3,1},{4,2},{5,3},{6,4},{7,5},{8,14},{9,15},{10,... | collective-permute-start | bytes 798728 | tf_op jit(solution)/shard_map/ppermute | solution.py:347
  5.1 13.7 %collective-permute-start.7 = (bf16[1040,128]{1,0:T(8,128)(2,1)S(1)}, bf16[1040,128]{1,0:T(8,128)(2,1)S(1)}, u32[]{:S(2)}, u32[]{:S(2)}) collective-permute-start(bf16[1040,128]{1,0:T(8,128)(2,1)S(1)} %get-tuple-element.25), channel_id=1, source_target_pairs={{0,3},{1,2},{2,5},{3,4},{4,7},{5,6},{6,1},{7,0},{8,11},{9,10},{10,... | collective-permute-start | bytes 798728 | tf_op jit(solution)/shard_map/ppermute | solution.py:347
  5.1 13.7 %collective-permute-start.8 = (bf16[1040,128]{1,0:T(8,128)(2,1)S(1)}, bf16[1040,128]{1,0:T(8,128)(2,1)S(1)}, u32[]{:S(2)}, u32[]{:S(2)}) collective-permute-start(bf16[1040,128]{1,0:T(8,128)(2,1)S(1)} %get-tuple-element.26), channel_id=1, source_target_pairs={{0,7},{1,6},{2,1},{3,0},{4,3},{5,2},{6,5},{7,4},{8,15},{9,14},{10,... | collective-permute-start | bytes 798728 | tf_op jit(solution)/shard_map/ppermute | solution.py:347
  12.8 12.3 %collective-permute-start.10 = (bf16[1040,128]{1,0:T(8,128)(2,1)S(1)}, bf16[1040,128]{1,0:T(8,128)(2,1)S(1)}, u32[]{:S(2)}, u32[]{:S(2)}) collective-permute-start(bf16[1040,128]{1,0:T(8,128)(2,1)S(1)} %get-tuple-element.28), channel_id=1, source_target_pairs={{0,4},{1,5},{2,6},{3,7},{4,0},{5,1},{6,2},{7,3},{8,12},{9,13},{10,... | collective-permute-start | bytes 798728 | tf_op jit(solution)/shard_map/ppermute | solution.py:347
  14.2 15.5 %collective-permute-start.1 = (bf16[1040,128]{1,0:T(8,128)(2,1)S(1)}, bf16[1040,128]{1,0:T(8,128)(2,1)S(1)}, u32[]{:S(2)}, u32[]{:S(2)}) collective-permute-start(bf16[1040,128]{1,0:T(8,128)(2,1)S(1)} %get-tuple-element.22), channel_id=1, source_target_pairs={{0,5},{1,4},{2,7},{3,6},{4,1},{5,0},{6,3},{7,2},{8,13},{9,12},{10,... | collective-permute-start | bytes 798728 | tf_op jit(solution)/shard_map/ppermute | solution.py:347
  16.8 15.0 %collective-permute-start.6 = (bf16[272,384]{1,0:T(8,128)(2,1)S(1)}, bf16[272,384]{1,0:T(8,128)(2,1)S(1)}, u32[]{:S(2)}, u32[]{:S(2)}) collective-permute-start(bf16[272,384]{1,0:T(8,128)(2,1)S(1)} %hidden.7.refs_3_), channel_id=1, source_target_pairs={{0,32},{8,40},{16,48},{24,56},{32,0},{40,8},{48,16},{56,24},{64,96... | collective-permute-start | bytes 626696 | tf_op jit(solution)/shard_map/ppermute | solution.py:335
  18.9 12.9 %collective-permute-start.9 = (bf16[272,384]{1,0:T(8,128)(2,1)S(1)}, bf16[272,384]{1,0:T(8,128)(2,1)S(1)}, u32[]{:S(2)}, u32[]{:S(2)}) collective-permute-start(bf16[272,384]{1,0:T(8,128)(2,1)S(1)} %hidden.8.refs_5_), channel_id=1, source_target_pairs={{0,32},{8,40},{16,48},{24,56},{32,0},{40,8},{48,16},{56,24},{64,96... | collective-permute-start | bytes 626696 | tf_op jit(solution)/shard_map/ppermute | solution.py:335
  19.5 14.4 %collective-permute-start.3 = (bf16[272,384]{1,0:T(8,128)(2,1)S(1)}, bf16[272,384]{1,0:T(8,128)(2,1)S(1)}, u32[]{:S(2)}, u32[]{:S(2)}) collective-permute-start(bf16[272,384]{1,0:T(8,128)(2,1)S(1)} %hidden.5.refs_1_), channel_id=1, source_target_pairs={{0,32},{8,40},{16,48},{24,56},{32,0},{40,8},{48,16},{56,24},{64,96... | collective-permute-start | bytes 626696 | tf_op jit(solution)/shard_map/ppermute | solution.py:335
  25.2 11.0 %collective-permute-start.11 = (bf16[144,384]{1,0:T(8,128)(2,1)S(1)}, bf16[144,384]{1,0:T(8,128)(2,1)S(1)}, u32[]{:S(2)}, u32[]{:S(2)}) collective-permute-start(bf16[144,384]{1,0:T(8,128)(2,1)S(1)} %hidden.9.refs_7_), channel_id=1, source_target_pairs={{0,32},{8,40},{16,48},{24,56},{32,0},{40,8},{48,16},{56,24},{64,96... | collective-permute-start | bytes 331784 | tf_op jit(solution)/shard_map/ppermute | solution.py:335
  30.2 7.3 %collective-permute-start.2 = (bf16[144,384]{1,0:T(8,128)(2,1)S(1)}, bf16[144,384]{1,0:T(8,128)(2,1)S(1)}, u32[]{:S(2)}, u32[]{:S(2)}) collective-permute-start(bf16[144,384]{1,0:T(8,128)(2,1)S(1)} %hidden.6.refs_1_), channel_id=1, source_target_pairs={{0,32},{8,40},{16,48},{24,56},{32,0},{40,8},{48,16},{56,24},{64,96... | collective-permute-start | bytes 331784 | tf_op jit(solution)/shard_map/ppermute | solution.py:335
  67.9 6.9 %collective-permute-start.12 = (f32[264,128]{1,0:T(8,128)S(1)}, f32[264,128]{1,0:T(8,128)S(1)}, u32[]{:S(2)}, u32[]{:S(2)}) collective-permute-start(f32[264,128]{1,0:T(8,128)S(1)} %slice.8), channel_id=1, source_target_pairs={{8,0},{24,16},{40,32},{56,48},{72,64},{88,80},{104,96},{120,112},{... | collective-permute-start | bytes 405512 | tf_op jit(solution)/shard_map/ppermute | solution.py:359

commit v2 on v1

--- a/solution.py
+++ b/solution.py
@@ -18,9 +18,12 @@
 BF16 = jnp.bfloat16
 HIGH = lax.Precision.HIGHEST
 TN = (((0,), (0,)), ((), ()))
+NN = (((1,), (0,)), ((), ()))
 HALF = 64
-TIP = 320
-TIP_ODD = 256
+QUARTER = 32
+SECOND = HALF + LANE
+THIRD = SECOND + HALF
+TIP = THIRD + QUARTER
 
 
 def near(x):
@@ -181,20 +184,25 @@
         def _(ref=ref, s=s, local=local):
             hidden = ref[s * BLOCK : (s + 1) * BLOCK, :]
             even, odd = 2 * local, 2 * local + 1
-            for i, (chunk, base, tip, sides) in enumerate(
-                ((even, 0, TIP, (HALF, HALF + LANE)), (odd, 0, TIP_ODD, (LANE,)), (odd, HALF, TIP_ODD + 1, ()))
-            ):
-                part = lax.dot_general(
+            parts = [
+                lax.dot_general(
                     hidden[:, i * LANE : (i + 1) * LANE],
                     hidden[:, i * LANE :],
                     TN,
                     preferred_element_type=F32,
                 )
-                folded, corner = fold(part[:, :LANE])
-                out_ref[chunk, base : base + HALF, :] += folded
-                out_ref[chunk, tip : tip + 1, :] += corner
-                for j, side in enumerate(sides):
-                    out_ref[chunk, side : side + LANE, :] += part[:, (j + 1) * LANE : (j + 2) * LANE]
+                for i in range(3)
+            ]
+            folds = [fold(part[:, :LANE]) for part in parts]
+            for i, (_, corner) in enumerate(folds):
+                out_ref[even, TIP + i : TIP + i + 1, :] += corner
+            out_ref[even, :HALF, :] += folds[0][0]
+            out_ref[even, HALF:SECOND, :] += parts[0][:, LANE : 2 * LANE]
+            out_ref[even, SECOND:THIRD, :] += folds[1][0]
+            out_ref[even, THIRD:TIP, :] += folds[2][0][:QUARTER, :]
+            out_ref[odd, :LANE, :] += parts[0][:, 2 * LANE :]
+            out_ref[odd, LANE : 2 * LANE, :] += parts[1][:, LANE:]
+            out_ref[odd, THIRD:TIP, :] += folds[2][0][QUARTER:, :]
 
 
 def gram(first, kept, groups, prior=()):
@@ -258,63 +266,70 @@
             strip = jnp.concatenate([diag, right], axis=1)
         work[r0:r1, :] = strip
         if r1 < LANE:
-            work[r1:, :] = work[r1:, :] - dot_high(diag.T[r1:, :], strip, (((1,), (0,)), ((), ())))
-
-
-def diagonal(ref, base, tip, scale):
-    tile = unfold(ref[base : base + HALF, :] * scale, ref[tip : tip + 1, :] * scale)
-    eye = lax.broadcasted_iota(jnp.int32, tile.shape, 0) == lax.broadcasted_iota(
-        jnp.int32, tile.shape, 1
+            work[r1:, :] = work[r1:, :] - dot_high(diag.T[r1:, :], strip, NN)
+
+
+def identity_tile():
+    shape = (LANE, LANE)
+    rows, cols = (lax.broadcasted_iota(jnp.int32, shape, axis) for axis in range(2))
+    return jnp.where(rows == cols, 1.0, 0.0)
+
+
+def diagonal(folded, corner, scale):
+    return unfold(folded * scale, corner * scale) + RIDGE * identity_tile()
+
+
+def first_kernel(part_ref, top_ref, mid_ref, *, scale):
+    tip = lambda i: part_ref[TIP + i : TIP + i + 1, :]
+    top_ref[:, :LANE] = diagonal(part_ref[:HALF, :], tip(0), scale)
+    top_ref[:, LANE : 2 * LANE] = part_ref[HALF:SECOND, :] * scale
+    top_ref[:, 2 * LANE :] = identity_tile()
+    factor_panel(top_ref)
+    side = top_ref[:, LANE : 2 * LANE]
+    mid_ref[:, :LANE] = diagonal(part_ref[SECOND:THIRD, :], tip(1), scale) - dot_high(side, side, TN)
+    mid_ref[:, LANE:] = identity_tile()
+    factor_panel(mid_ref)
+
+
+def first_panels(part, scale):
+    return pl.pallas_call(
+        lambda *refs: first_kernel(*refs, scale=scale),
+        out_shape=[pltpu.VMEM((LANE, 3 * LANE), F32), pltpu.VMEM((LANE, 2 * LANE), F32)],
+        compiler_params=pltpu.CompilerParams(vmem_limit_bytes=VMEM_BYTES),
+        name="first_panels",
+    )(near(part))
+
+
+def last_kernel(part_ref, other_ref, top_ref, mid_ref, out_ref, low, *, scale):
+    right = dot_high(top_ref[:, 2 * LANE :], other_ref[:LANE, :] * scale, NN)
+    rest = other_ref[LANE : 2 * LANE, :] * scale - dot_high(top_ref[:, LANE : 2 * LANE], right, TN)
+    below = dot_high(mid_ref[:, LANE:], rest, NN)
+    folded = jnp.concatenate([part_ref[THIRD:TIP, :], other_ref[THIRD:TIP, :]], axis=0)
+    low[...] = (
+        diagonal(folded, part_ref[TIP + 2 : TIP + 3, :], scale)
+        - dot_high(right, right, TN)
+        - dot_high(below, below, TN)
     )
-    return tile + jnp.where(eye, RIDGE, 0.0)
-
-
-def first_kernel(part_ref, out_ref, *, scale):
-    out_ref[:, :LANE] = diagonal(part_ref, 0, TIP, scale)
-    for t in range(2):
-        side = part_ref[HALF + t * LANE : HALF + (t + 1) * LANE, :]
-        out_ref[:, (t + 1) * LANE : (t + 2) * LANE] = side * scale
-    factor_panel(out_ref)
-
-
-def first_panel(part, width, scale):
-    return pl.pallas_call(
-        lambda *refs: first_kernel(*refs, scale=scale),
-        out_shape=pltpu.VMEM((LANE, width), F32),
-        compiler_params=pltpu.CompilerParams(vmem_limit_bytes=VMEM_BYTES),
-        name="first_panel",
-    )(near(part))
-
-
-def rest_kernel(part_ref, top_ref, out_ref, mid, low, *, scale):
-    top = top_ref[...]
-    mid[:, :LANE] = diagonal(part_ref, 0, TIP_ODD, scale)
-    mid[:, LANE:] = part_ref[LANE : 2 * LANE, :] * scale
-    mid[...] = mid[...] - dot_high(top[:, LANE : 2 * LANE], top[:, LANE:], TN)
-    low[...] = diagonal(part_ref, HALF, TIP_ODD + 1, scale) - dot_high(
-        top[:, 2 * LANE :], top[:, 2 * LANE :], TN
-    )
-    factor_panel(mid)
-    right = mid[:, LANE:]
-    low[...] = low[...] - dot_high(right, right, TN)
     factor_panel(low)
     kind = out_ref.dtype
-    out_ref[:LANE, :] = top.astype(kind)
+    out_ref[:LANE, : 2 * LANE] = top_ref[:, : 2 * LANE].astype(kind)
+    out_ref[:LANE, 2 * LANE :] = right.astype(kind)
     out_ref[LANE : 2 * LANE, :LANE] = jnp.zeros((LANE, LANE), kind)
-    out_ref[LANE : 2 * LANE, LANE:] = mid[...].astype(kind)
+    out_ref[LANE : 2 * LANE, LANE : 2 * LANE] = mid_ref[:, :LANE].astype(kind)
+    out_ref[LANE : 2 * LANE, 2 * LANE :] = below.astype(kind)
     out_ref[2 * LANE :, : 2 * LANE] = jnp.zeros((LANE, 2 * LANE), kind)
     out_ref[2 * LANE :, 2 * LANE :] = low[...].astype(kind)
 
 
-def rest_panels(part, top, scale):
+def last_panel(part, other, top, mid, scale):
     width = top.shape[1]
     return pl.pallas_call(
-        lambda *refs: rest_kernel(*refs, scale=scale),
+        lambda *refs: last_kernel(*refs, scale=scale),
         out_shape=pltpu.VMEM((width, width), BF16),
-        scratch_shapes=[pltpu.VMEM((LANE, 2 * LANE), F32), pltpu.VMEM((LANE, LANE), F32)],
-        compiler_params=pltpu.CompilerParams(vmem_limit_bytes=VMEM_BYTES),
-        name="rest_panels",
-    )(near(part), near(top))
+        scratch_shapes=[pltpu.VMEM((LANE, LANE), F32)],
+        compiler_params=pltpu.CompilerParams(vmem_limit_bytes=VMEM_BYTES),
+        name="last_panel",
+    )(near(part), near(other), near(top), near(mid))
 
 
 def on_device(tokens, block_expert, gate_weight, up_weight):
@@ -349,17 +364,18 @@
         swap_rows(g)
     kept = experts_each // 2
     first = (lax.axis_index("dp") // SIDE % 2 * kept).reshape(1)
-    partial_gram = gram(first, kept, [rows for pair in gathered[:-1] for rows in pair])
-    partial_gram = gram(first, kept, gathered[-1], (partial_gram,))
+    partial_gram = gram(first, kept, [rows for pair in gathered[:-2] for rows in pair])
+    tail = [rows for pair in gathered[-2:] for rows in pair]
+    partial_gram = gram(first, kept, tail, (partial_gram,))
     classes = [[d for d in range(replicas) if d // SIDE % 2 == p] for p in range(2)]
     pieces = lax.all_to_all(
         partial_gram, "dp", split_axis=0, concat_axis=0, axis_index_groups=classes, tiled=True
     )
     own = jnp.sum(pieces, axis=0)
-    other = lax.ppermute(own[: TIP_ODD + 8], "dp", [(d + 1, d) for d in range(0, replicas, 2)])
+    other = lax.ppermute(own[:TIP], "dp", [(d + 1, d) for d in range(0, replicas, 2)])
     scale = experts_each / (tokens.shape[0] * replicas)
-    top = first_panel(own, hidden_width, scale)
-    result = rest_panels(other, top, scale)
+    top, mid = first_panels(own, scale)
+    result = last_panel(own, other, top, mid, scale)
     row_count = hidden_width // replicas
     sent = result.reshape(replicas, row_count, hidden_width)
     returned = lax.all_to_all(sent, "dp", split_axis=0, concat_axis=0, tiled=True)

time: 94.1 us -> 91.4 us (0.971)
  waiting for transfers between devices: 13.1 us -> 11.1 us
  blocking collectives: 40.8 us -> 39.5 us
    all_to_all x1, blocking collectives: 29.6 us -> 26.8 us  [on_device(): lax.all_to_all(partial_gram, 'dp', split_axis=0, concat_axis=0, axis_inde...]
    ppermute x1, waiting for transfers between devices: 2.08 us -> 0.01 us  [on_device(): lax.ppermute(own[:TIP], 'dp', [(d + 1, d) for d in range(0, replicas, 2)])]
    all_to_all x1, blocking collectives: 11.2 us -> 12.7 us  [on_device(): lax.all_to_all(sent, 'dp', split_axis=0, concat_axis=0, tiled=True)]
  transfers between devices with their start and end apart: 13 -> 13, of which waited for: 6 -> 5; matrix products, arithmetic and copies ran while one was open for 0% -> 0% of each run, Pallas kernels for 11% -> 15%
where the time goes in v2:
time: 91.4 us; the launch traced here: 91.2 us
  blocking collectives  39.5 us (43%)
  Pallas kernels  20.7 us (23%)
  starting transfers between devices  18.9 us (21%)
  waiting for transfers between devices  11.1 us (12%)
    all_to_all x1, blocking collectives, on_device(): lax.all_to_all(partial_gram, 'dp', split_axis=0, concat_axis=0, axis_inde...  26.8 us
    all_to_all x1, blocking collectives, on_device(): lax.all_to_all(sent, 'dp', split_axis=0, concat_axis=0, tiled=True)  12.7 us
    ppermute x7, starting transfers between devices, on_device(): lax.ppermute(payload, 'expert', route)  9.75 us
    ppermute x5, starting transfers between devices, swap_rows(): gathered.append([rows, lax.ppermute(rows, 'dp', pairs)])  7.69 us
    pallas_call x1, Pallas kernels, first_panels(): pl.pallas_call(lambda *refs: first_kernel(*refs, scale=scale), out_shape=...  6.85 us
    ppermute x7, waiting for transfers between devices, on_device(): lax.ppermute(payload, 'expert', route)  6.51 us
    ppermute x5, waiting for transfers between devices, swap_rows(): gathered.append([rows, lax.ppermute(rows, 'dp', pairs)])  4.62 us
    pallas_call x1, Pallas kernels, bring(): pl.pallas_call(bring_kernel, in_specs=[pl.BlockSpec(memory_space=pl.ANY)]...  4.62 us
  transfers between devices with their start and end apart: 13, of which 5 were waited for; matrix products, arithmetic and copies ran while one was open for 0% of the time, Pallas kernels for 15%

profile of v2, /device:TPU:0, one launch (start us, length us, event | category | flops | bytes accessed | tf_op | source)
XLA Modules:
  0.0 91.2 jit_solution(1253558542278385366)
XLA Ops:
  0.0 1.7 %pack.1 = (bf16[1040,128]{1,0:T(8,128)(2,1)S(1)}, bf16[1040,128]{1,0:T(8,128)(2,1)S(1)}, bf16[1040,128]{1,0:T(8,128)(2,1)S(1)}, bf16[1040,128]{1,0:T(8,128)(2,1)...) custom-call(s32[1]{0:T(128)} %bitcast.1.refs_0_, ...), custom_call_target="tpu_custom_call" | custom-call | tf_op jit(solution)/shard_map/pack/pallas_call | solution.py:71
  1.7 0.1 collective-permute-start
  1.8 1.8 %collective-permute-start.6 = (bf16[1040,128]{1,0:T(8,128)(2,1)S(1)}, bf16[1040,128]{1,0:T(8,128)(2,1)S(1)}, u32[]{:S(2)}, u32[]{:S(2)}) collective-permute-start(bf16[1040,128]{1,0:T(8,128)(2,1)S(1)} %get-tuple-element.27), channel_id=1, source_target_pairs={{0,2},{1,3},{2,4},{3,5},{4,6},{5,7},{6,0},{7,1},{8,10},{9,11},{10,... | collective-permute-start | bytes 798728 | tf_op jit(solution)/shard_map/ppermute | solution.py:362
  3.5 1.5 %collective-permute-start.7 = (bf16[1040,128]{1,0:T(8,128)(2,1)S(1)}, bf16[1040,128]{1,0:T(8,128)(2,1)S(1)}, u32[]{:S(2)}, u32[]{:S(2)}) collective-permute-start(bf16[1040,128]{1,0:T(8,128)(2,1)S(1)} %get-tuple-element.28), channel_id=1, source_target_pairs={{0,6},{1,7},{2,0},{3,1},{4,2},{5,3},{6,4},{7,5},{8,14},{9,15},{10,... | collective-permute-start | bytes 798728 | tf_op jit(solution)/shard_map/ppermute | solution.py:362
  5.1 3.0 %collective-permute-start.10 = (bf16[1040,128]{1,0:T(8,128)(2,1)S(1)}, bf16[1040,128]{1,0:T(8,128)(2,1)S(1)}, u32[]{:S(2)}, u32[]{:S(2)}) collective-permute-start(bf16[1040,128]{1,0:T(8,128)(2,1)S(1)} %get-tuple-element.30), channel_id=1, source_target_pairs={{0,7},{1,6},{2,1},{3,0},{4,3},{5,2},{6,5},{7,4},{8,15},{9,14},{10,... | collective-permute-start | bytes 798728 | tf_op jit(solution)/shard_map/ppermute | solution.py:362
  8.0 4.6 %bring.1 = (bf16[8,1024,384]{2,1,0:T(8,128)(2,1)S(1)}, bf16[8,1024,384]{2,1,0:T(8,128)(2,1)S(1)}) custom-call(bf16[1040,128]{1,0:T(8,128)(2,1)S(1)} %get-tuple-element.20._.refs_0_, bf16[8,1024,384]{2,1,0:T(8,128)(2,1)} %gate_ref.1, bf16[8,1024,384]{2,1,0:T(8,128)(2,1)} %up_ref.1), custom_call_target="tpu_custom_call" | custom-call | tf_op jit(solution)/shard_map/bring/pallas_call | solution.py:141
  12.7 0.1 hidden.5.refs_1_
  12.8 1.4 %collective-permute-start.1 = (bf16[1040,128]{1,0:T(8,128)(2,1)S(1)}, bf16[1040,128]{1,0:T(8,128)(2,1)S(1)}, u32[]{:S(2)}, u32[]{:S(2)}) collective-permute-start(bf16[1040,128]{1,0:T(8,128)(2,1)S(1)} %get-tuple-element.24), channel_id=1, source_target_pairs={{0,4},{1,5},{2,6},{3,7},{4,0},{5,1},{6,2},{7,3},{8,12},{9,13},{10,... | collective-permute-start | bytes 798728 | tf_op jit(solution)/shard_map/ppermute | solution.py:362
  14.2 2.0 %collective-permute-start.3 = (bf16[1040,128]{1,0:T(8,128)(2,1)S(1)}, bf16[1040,128]{1,0:T(8,128)(2,1)S(1)}, u32[]{:S(2)}, u32[]{:S(2)}) collective-permute-start(bf16[1040,128]{1,0:T(8,128)(2,1)S(1)} %get-tuple-element.26), channel_id=1, source_target_pairs={{0,5},{1,4},{2,7},{3,6},{4,1},{5,0},{6,3},{7,2},{8,13},{9,12},{10,... | collective-permute-start | bytes 798728 | tf_op jit(solution)/shard_map/ppermute | solution.py:362
  16.2 1.9 %collective-permute-start.5 = (bf16[272,384]{1,0:T(8,128)(2,1)S(1)}, bf16[272,384]{1,0:T(8,128)(2,1)S(1)}, u32[]{:S(2)}, u32[]{:S(2)}) collective-permute-start(bf16[272,384]{1,0:T(8,128)(2,1)S(1)} %hidden.5.refs_1_), channel_id=1, source_target_pairs={{0,32},{8,40},{16,48},{24,56},{32,0},{40,8},{48,16},{56,24},{64,96... | collective-permute-start | bytes 626696 | tf_op jit(solution)/shard_map/ppermute | solution.py:350
  18.1 0.6 hidden.8.refs_3_
  18.7 0.2 collective-permute-start.8
  18.9 0.1 hidden.9.refs_5_
  19.0 2.0 %collective-permute-start.11 = (bf16[272,384]{1,0:T(8,128)(2,1)S(1)}, bf16[272,384]{1,0:T(8,128)(2,1)S(1)}, u32[]{:S(2)}, u32[]{:S(2)}) collective-permute-start(bf16[272,384]{1,0:T(8,128)(2,1)S(1)} %hidden.9.refs_5_), channel_id=1, source_target_pairs={{0,32},{8,40},{16,48},{24,56},{32,0},{40,8},{48,16},{56,24},{64,96... | collective-permute-start | bytes 626696 | tf_op jit(solution)/shard_map/ppermute | solution.py:350
  21.0 4.0 %collective-permute-done.1.refs_0_ = bf16[1040,128]{1,0:T(8,128)(2,1)S(1)} collective-permute-done((bf16[1040,128]{1,0:T(8,128)(2,1)S(1)}, bf16[1040,128]{1,0:T(8,128)(2,1)S(1)}, u32[]{:S(2)}, u32[]{:S(2)}) %collective-permute-start.1) | collective-permute-done | bytes 266272 | tf_op jit(solution)/shard_map/ppermute | solution.py:362
  25.1 0.1 hidden.6.refs_1_
  25.2 2.0 %collective-permute-start.2 = (bf16[144,384]{1,0:T(8,128)(2,1)S(1)}, bf16[144,384]{1,0:T(8,128)(2,1)S(1)}, u32[]{:S(2)}, u32[]{:S(2)}) collective-permute-start(bf16[144,384]{1,0:T(8,128)(2,1)S(1)} %hidden.6.refs_1_), channel_id=1, source_target_pairs={{0,32},{8,40},{16,48},{24,56},{32,0},{40,8},{48,16},{56,24},{64,96... | collective-permute-start | bytes 331784 | tf_op jit(solution)/shard_map/ppermute | solution.py:350
  27.2 2.5 %collective-permute-done.3.refs_0_ = bf16[1040,128]{1,0:T(8,128)(2,1)S(1)} collective-permute-done((bf16[1040,128]{1,0:T(8,128)(2,1)S(1)}, bf16[1040,128]{1,0:T(8,128)(2,1)S(1)}, u32[]{:S(2)}, u32[]{:S(2)}) %collective-permute-start.3) | collective-permute-done | bytes 266272 | tf_op jit(solution)/shard_map/ppermute | solution.py:362
  29.7 0.6 hidden.7.refs_3_
  30.3 1.6 %collective-permute-start.4 = (bf16[144,384]{1,0:T(8,128)(2,1)S(1)}, bf16[144,384]{1,0:T(8,128)(2,1)S(1)}, u32[]{:S(2)}, u32[]{:S(2)}) collective-permute-start(bf16[144,384]{1,0:T(8,128)(2,1)S(1)} %hidden.7.refs_3_), channel_id=1, source_target_pairs={{0,32},{8,40},{16,48},{24,56},{32,0},{40,8},{48,16},{56,24},{64,96... | collective-permute-start | bytes 331784 | tf_op jit(solution)/shard_map/ppermute | solution.py:350
  31.8 1.4 %collective-permute-done.11.refs_6_ = bf16[272,384]{1,0:T(8,128)(2,1)S(1)} collective-permute-done((bf16[272,384]{1,0:T(8,128)(2,1)S(1)}, bf16[272,384]{1,0:T(8,128)(2,1)S(1)}, u32[]{:S(2)}, u32[]{:S(2)}) %collective-permute-start.11) | collective-permute-done | bytes 208928 | tf_op jit(solution)/shard_map/ppermute | solution.py:350
  33.2 0.8 gram.2.refs_5_
  34.1 1.5 %collective-permute-done.2.refs_2_ = bf16[144,384]{1,0:T(8,128)(2,1)S(1)} collective-permute-done((bf16[144,384]{1,0:T(8,128)(2,1)S(1)}, bf16[144,384]{1,0:T(8,128)(2,1)S(1)}, u32[]{:S(2)}, u32[]{:S(2)}) %collective-permute-start.2) | collective-permute-done | bytes 110624 | tf_op jit(solution)/shard_map/ppermute | solution.py:350
  35.6 1.7 %collective-permute-done.4.refs_4_ = bf16[144,384]{1,0:T(8,128)(2,1)S(1)} collective-permute-done((bf16[144,384]{1,0:T(8,128)(2,1)S(1)}, bf16[144,384]{1,0:T(8,128)(2,1)S(1)}, u32[]{:S(2)}, u32[]{:S(2)}) %collective-permute-start.4) | collective-permute-done | bytes 110624 | tf_op jit(solution)/shard_map/ppermute | solution.py:350
  37.3 1.1 %gram.3 = f32[8,296,128]{2,1,0:T(8,128)S(1)} custom-call(s32[1]{0:T(128)} %bitcast.refs_0_, bf16[144,384]{1,0:T(8,128)(2,1)S(1)} %hidden.6.refs_1_, bf16[144,384]{1,0:T(8,128)(2,1)S(1)} %collective-permute-done.2.refs_2_, bf16[144,384]{1,0:T(8,128)(2,1)S(1)} %hidden.7.refs_3_, bf16[144,384]{1,0:T(8,128)(2,1)S(1)} %collective-permute-done.4.refs_4_, ...), custom_call_target="tpu_custom_call" | custom-call | tf_op jit(solution)/shard_map/gram/pallas_call | solution.py:210
  38.4 26.8 %all_to_all.10 = f32[8,296,128]{2,1,0:T(8,128)S(1)} all-to-all(f32[8,296,128]{2,1,0:T(8,128)S(1)} %gram.3), channel_id=1, replica_groups={{0,8,16,24,64,72,80,88},{32,40,48,56,96,104,112,120},{1,9,17,25,65,73,8..., dimensions={0} | all-to-all | bytes 2424832 | tf_op jit(solution)/shard_map/all_to_all | solution.py:371
  65.1 0.1 reduce_sum.9.refs_0_
  65.2 1.5 %collective-permute-start.12 = (f32[288,128]{1,0:T(8,128)S(1)}, f32[288,128]{1,0:T(8,128)S(1)}, u32[]{:S(2)}, u32[]{:S(2)}) collective-permute-start(f32[288,128]{1,0:T(8,128)S(1)} %slice.8), channel_id=1, source_target_pairs={{8,0},{24,16},{40,32},{56,48},{72,64},{88,80},{104,96},{120,112},{... | collective-permute-start | bytes 442376 | tf_op jit(solution)/shard_map/ppermute | solution.py:375
  66.7 6.9 %first_panels.1 = (f32[128,384]{1,0:T(8,128)S(1)}, f32[128,256]{1,0:T(8,128)S(1)}) custom-call(f32[296,128]{1,0:T(8,128)S(1)} %reduce_sum.9.refs_0_), custom_call_target="tpu_custom_call" | custom-call | tf_op jit(solution)/shard_map/first_panels/pallas_call | solution.py:295
  73.6 4.2 %last_panel.1 = bf16[384,384]{1,0:T(8,128)(2,1)S(1)} custom-call(f32[296,128]{1,0:T(8,128)S(1)} %reduce_sum.9.refs_0_, f32[288,128]{1,0:T(8,128)S(1)} %collective-permute-done.12.refs_1_, f32[128,384]{1,0:T(8,128)S(1)} %get-tuple-element.31.refs_2_, f32[128,256]{1,0:T(8,128)S(1)} %get-tuple-element.32.refs_3_), custom_call_target="tpu_custom_call" | custom-call | tf_op jit(solution)/shard_map/last_panel/pallas_call | solution.py:326
  77.8 12.7 %all_to_all.11 = bf16[16,24,384]{2,1,0:T(8,128)(2,1)S(1)} all-to-all(bf16[16,24,384]{2,1,0:T(8,128)(2,1)S(1)} %bitcast.12), channel_id=1, replica_groups=mesh['dp'=16,'expert'=8] {'dp'}, dimensions={0} | all-to-all | bytes 589824 | tf_op jit(solution)/shard_map/all_to_all | solution.py:381
  90.5 0.7 fusion
  (10 shorter events, 0.0 us)
Async XLA Ops:
  1.7 11.0 %collective-permute-start = (bf16[1040,128]{1,0:T(8,128)(2,1)S(1)}, bf16[1040,128]{1,0:T(8,128)(2,1)S(1)}, u32[]{:S(2)}, u32[]{:S(2)}) collective-permute-start(bf16[1040,128]{1,0:T(8,128)(2,1)S(1)} %get-tuple-element.21), channel_id=1, source_target_pairs={{0,1},{1,0},{2,3},{3,2},{4,5},{5,4},{6,7},{7,6},{8,9},{9,8},{10,11... | collective-permute-start | bytes 798728 | tf_op jit(solution)/shard_map/ppermute | solution.py:362
  1.8 12.4 %collective-permute-start.6 = (bf16[1040,128]{1,0:T(8,128)(2,1)S(1)}, bf16[1040,128]{1,0:T(8,128)(2,1)S(1)}, u32[]{:S(2)}, u32[]{:S(2)}) collective-permute-start(bf16[1040,128]{1,0:T(8,128)(2,1)S(1)} %get-tuple-element.27), channel_id=1, source_target_pairs={{0,2},{1,3},{2,4},{3,5},{4,6},{5,7},{6,0},{7,1},{8,10},{9,11},{10,... | collective-permute-start | bytes 798728 | tf_op jit(solution)/shard_map/ppermute | solution.py:362
  3.5 12.7 %collective-permute-start.7 = (bf16[1040,128]{1,0:T(8,128)(2,1)S(1)}, bf16[1040,128]{1,0:T(8,128)(2,1)S(1)}, u32[]{:S(2)}, u32[]{:S(2)}) collective-permute-start(bf16[1040,128]{1,0:T(8,128)(2,1)S(1)} %get-tuple-element.28), channel_id=1, source_target_pairs={{0,6},{1,7},{2,0},{3,1},{4,2},{5,3},{6,4},{7,5},{8,14},{9,15},{10,... | collective-permute-start | bytes 798728 | tf_op jit(solution)/shard_map/ppermute | solution.py:362
  5.1 13.6 %collective-permute-start.9 = (bf16[1040,128]{1,0:T(8,128)(2,1)S(1)}, bf16[1040,128]{1,0:T(8,128)(2,1)S(1)}, u32[]{:S(2)}, u32[]{:S(2)}) collective-permute-start(bf16[1040,128]{1,0:T(8,128)(2,1)S(1)} %get-tuple-element.29), channel_id=1, source_target_pairs={{0,3},{1,2},{2,5},{3,4},{4,7},{5,6},{6,1},{7,0},{8,11},{9,10},{10,... | collective-permute-start | bytes 798728 | tf_op jit(solution)/shard_map/ppermute | solution.py:362
  5.1 13.8 %collective-permute-start.10 = (bf16[1040,128]{1,0:T(8,128)(2,1)S(1)}, bf16[1040,128]{1,0:T(8,128)(2,1)S(1)}, u32[]{:S(2)}, u32[]{:S(2)}) collective-permute-start(bf16[1040,128]{1,0:T(8,128)(2,1)S(1)} %get-tuple-element.30), channel_id=1, source_target_pairs={{0,7},{1,6},{2,1},{3,0},{4,3},{5,2},{6,5},{7,4},{8,15},{9,14},{10,... | collective-permute-start | bytes 798728 | tf_op jit(solution)/shard_map/ppermute | solution.py:362
  12.8 12.3 %collective-permute-start.1 = (bf16[1040,128]{1,0:T(8,128)(2,1)S(1)}, bf16[1040,128]{1,0:T(8,128)(2,1)S(1)}, u32[]{:S(2)}, u32[]{:S(2)}) collective-permute-start(bf16[1040,128]{1,0:T(8,128)(2,1)S(1)} %get-tuple-element.24), channel_id=1, source_target_pairs={{0,4},{1,5},{2,6},{3,7},{4,0},{5,1},{6,2},{7,3},{8,12},{9,13},{10,... | collective-permute-start | bytes 798728 | tf_op jit(solution)/shard_map/ppermute | solution.py:362
  14.2 15.5 %collective-permute-start.3 = (bf16[1040,128]{1,0:T(8,128)(2,1)S(1)}, bf16[1040,128]{1,0:T(8,128)(2,1)S(1)}, u32[]{:S(2)}, u32[]{:S(2)}) collective-permute-start(bf16[1040,128]{1,0:T(8,128)(2,1)S(1)} %get-tuple-element.26), channel_id=1, source_target_pairs={{0,5},{1,4},{2,7},{3,6},{4,1},{5,0},{6,3},{7,2},{8,13},{9,12},{10,... | collective-permute-start | bytes 798728 | tf_op jit(solution)/shard_map/ppermute | solution.py:362
  16.2 15.6 %collective-permute-start.5 = (bf16[272,384]{1,0:T(8,128)(2,1)S(1)}, bf16[272,384]{1,0:T(8,128)(2,1)S(1)}, u32[]{:S(2)}, u32[]{:S(2)}) collective-permute-start(bf16[272,384]{1,0:T(8,128)(2,1)S(1)} %hidden.5.refs_1_), channel_id=1, source_target_pairs={{0,32},{8,40},{16,48},{24,56},{32,0},{40,8},{48,16},{56,24},{64,96... | collective-permute-start | bytes 626696 | tf_op jit(solution)/shard_map/ppermute | solution.py:350
  18.7 13.1 %collective-permute-start.8 = (bf16[272,384]{1,0:T(8,128)(2,1)S(1)}, bf16[272,384]{1,0:T(8,128)(2,1)S(1)}, u32[]{:S(2)}, u32[]{:S(2)}) collective-permute-start(bf16[272,384]{1,0:T(8,128)(2,1)S(1)} %hidden.8.refs_3_), channel_id=1, source_target_pairs={{0,32},{8,40},{16,48},{24,56},{32,0},{40,8},{48,16},{56,24},{64,96... | collective-permute-start | bytes 626696 | tf_op jit(solution)/shard_map/ppermute | solution.py:350
  19.0 14.2 %collective-permute-start.11 = (bf16[272,384]{1,0:T(8,128)(2,1)S(1)}, bf16[272,384]{1,0:T(8,128)(2,1)S(1)}, u32[]{:S(2)}, u32[]{:S(2)}) collective-permute-start(bf16[272,384]{1,0:T(8,128)(2,1)S(1)} %hidden.9.refs_5_), channel_id=1, source_target_pairs={{0,32},{8,40},{16,48},{24,56},{32,0},{40,8},{48,16},{56,24},{64,96... | collective-permute-start | bytes 626696 | tf_op jit(solution)/shard_map/ppermute | solution.py:350
  25.2 10.4 %collective-permute-start.2 = (bf16[144,384]{1,0:T(8,128)(2,1)S(1)}, bf16[144,384]{1,0:T(8,128)(2,1)S(1)}, u32[]{:S(2)}, u32[]{:S(2)}) collective-permute-start(bf16[144,384]{1,0:T(8,128)(2,1)S(1)} %hidden.6.refs_1_), channel_id=1, source_target_pairs={{0,32},{8,40},{16,48},{24,56},{32,0},{40,8},{48,16},{56,24},{64,96... | collective-permute-start | bytes 331784 | tf_op jit(solution)/shard_map/ppermute | solution.py:350
  30.3 7.0 %collective-permute-start.4 = (bf16[144,384]{1,0:T(8,128)(2,1)S(1)}, bf16[144,384]{1,0:T(8,128)(2,1)S(1)}, u32[]{:S(2)}, u32[]{:S(2)}) collective-permute-start(bf16[144,384]{1,0:T(8,128)(2,1)S(1)} %hidden.7.refs_3_), channel_id=1, source_target_pairs={{0,32},{8,40},{16,48},{24,56},{32,0},{40,8},{48,16},{56,24},{64,96... | collective-permute-start | bytes 331784 | tf_op jit(solution)/shard_map/ppermute | solution.py:350
  65.2 8.3 %collective-permute-start.12 = (f32[288,128]{1,0:T(8,128)S(1)}, f32[288,128]{1,0:T(8,128)S(1)}, u32[]{:S(2)}, u32[]{:S(2)}) collective-permute-start(f32[288,128]{1,0:T(8,128)S(1)} %slice.8), channel_id=1, source_target_pairs={{8,0},{24,16},{40,32},{56,48},{72,64},{88,80},{104,96},{120,112},{... | collective-permute-start | bytes 442376 | tf_op jit(solution)/shard_map/ppermute | solution.py:375

commit v3 on v2

--- a/solution.py
+++ b/solution.py
@@ -341,7 +341,7 @@
     shifts += [(2, 0), (2, 1)]
     member = lax.axis_index("expert").reshape(1)
     outgoing = pack(block_expert, member, tokens, experts_each, shifts, chips)
-    pairs = [(d, d ^ SIDE) for d in range(replicas)]
+    pairs = [(d, d ^ 1) for d in range(replicas)]
     arrived, gathered = [], []
     weights = bring(outgoing[0], gate_weight, up_weight)
 
@@ -363,24 +363,27 @@
     for g in range(1, len(EDGES) - 1):
         swap_rows(g)
     kept = experts_each // 2
-    first = (lax.axis_index("dp") // SIDE % 2 * kept).reshape(1)
+    first = (lax.axis_index("dp") % 2 * kept).reshape(1)
     partial_gram = gram(first, kept, [rows for pair in gathered[:-2] for rows in pair])
     tail = [rows for pair in gathered[-2:] for rows in pair]
     partial_gram = gram(first, kept, tail, (partial_gram,))
-    classes = [[d for d in range(replicas) if d // SIDE % 2 == p] for p in range(2)]
+    side = replicas // SIDE
+    classes = [[x * SIDE + z for z in range(p, SIDE, 2) for x in range(side)] for p in range(2)]
     pieces = lax.all_to_all(
         partial_gram, "dp", split_axis=0, concat_axis=0, axis_index_groups=classes, tiled=True
     )
     own = jnp.sum(pieces, axis=0)
-    other = lax.ppermute(own[:TIP], "dp", [(d + 1, d) for d in range(0, replicas, 2)])
+    halves = [(d + SIDE, d) for d in range(replicas) if d // SIDE % 2 == 0]
+    other = lax.ppermute(own[:TIP], "dp", halves)
     scale = experts_each / (tokens.shape[0] * replicas)
     top, mid = first_panels(own, scale)
     result = last_panel(own, other, top, mid, scale)
     row_count = hidden_width // replicas
     sent = result.reshape(replicas, row_count, hidden_width)
     returned = lax.all_to_all(sent, "dp", split_axis=0, concat_axis=0, tiled=True)
-    returned = returned.reshape(2, 2, 2, 2, row_count, hidden_width)[:, :, :, 0]
-    returned = jnp.swapaxes(returned, 0, 1).reshape(experts_each, row_count, hidden_width)
+    returned = returned.reshape(2, 2, 2, 2, row_count, hidden_width)[:, 0]
+    returned = jnp.transpose(returned, (2, 1, 0, 3, 4))
+    returned = returned.reshape(experts_each, row_count, hidden_width)
     return returned.astype(F32)
 
 

time: 91.4 us -> 92.1 us (level)
  starting transfers between devices: 18.9 us -> 20.2 us
  waiting for transfers between devices: 11.1 us -> 10 us
    all_to_all x1, blocking collectives: 12.7 us -> 14 us  [on_device(): lax.all_to_all(sent, 'dp', split_axis=0, concat_axis=0, tiled=True)]
    ppermute x5, starting transfers between devices: 7.69 us -> 8.97 us  [swap_rows(): gathered.append([rows, lax.ppermute(rows, 'dp', pairs)])]
where the time goes in v3:
time: 92.1 us; the launch traced here: 91.9 us
  blocking collectives  40.3 us (44%)
  Pallas kernels  20.4 us (22%)
  starting transfers between devices  20.2 us (22%)
  waiting for transfers between devices  10 us (11%)
    all_to_all x1, blocking collectives, on_device(): lax.all_to_all(partial_gram, 'dp', split_axis=0, concat_axis=0, axis_inde...  26.3 us
    all_to_all x1, blocking collectives, on_device(): lax.all_to_all(sent, 'dp', split_axis=0, concat_axis=0, tiled=True)  14 us
    ppermute x7, starting transfers between devices, on_device(): lax.ppermute(payload, 'expert', route)  9.75 us
    ppermute x5, starting transfers between devices, swap_rows(): gathered.append([rows, lax.ppermute(rows, 'dp', pairs)])  8.97 us
    pallas_call x1, Pallas kernels, first_panels(): pl.pallas_call(lambda *refs: first_kernel(*refs, scale=scale), out_shape=...  6.85 us
    ppermute x7, waiting for transfers between devices, on_device(): lax.ppermute(payload, 'expert', route)  5.66 us
    pallas_call x1, Pallas kernels, bring(): pl.pallas_call(bring_kernel, in_specs=[pl.BlockSpec(memory_space=pl.ANY)]...  4.62 us
    ppermute x5, waiting for transfers between devices, swap_rows(): gathered.append([rows, lax.ppermute(rows, 'dp', pairs)])  4.33 us
  transfers between devices with their start and end apart: 13, of which 5 were waited for; matrix products, arithmetic and copies ran while one was open for 0% of the time, Pallas kernels for 15%

profile of v3, /device:TPU:0, one launch (start us, length us, event | category | flops | bytes accessed | tf_op | source)
XLA Modules:
  0.0 91.9 jit_solution(16529041405827543684)
XLA Ops:
  0.0 1.7 %pack.1 = (bf16[1040,128]{1,0:T(8,128)(2,1)S(1)}, bf16[1040,128]{1,0:T(8,128)(2,1)S(1)}, bf16[1040,128]{1,0:T(8,128)(2,1)S(1)}, bf16[1040,128]{1,0:T(8,128)(2,1)...) custom-call(s32[1]{0:T(128)} %bitcast.1.refs_0_, ...), custom_call_target="tpu_custom_call" | custom-call | tf_op jit(solution)/shard_map/pack/pallas_call | solution.py:71
  1.7 0.1 collective-permute-start
  1.8 1.8 %collective-permute-start.6 = (bf16[1040,128]{1,0:T(8,128)(2,1)S(1)}, bf16[1040,128]{1,0:T(8,128)(2,1)S(1)}, u32[]{:S(2)}, u32[]{:S(2)}) collective-permute-start(bf16[1040,128]{1,0:T(8,128)(2,1)S(1)} %get-tuple-element.27), channel_id=1, source_target_pairs={{0,2},{1,3},{2,4},{3,5},{4,6},{5,7},{6,0},{7,1},{8,10},{9,11},{10,... | collective-permute-start | bytes 798728 | tf_op jit(solution)/shard_map/ppermute | solution.py:362
  3.5 1.5 %collective-permute-start.7 = (bf16[1040,128]{1,0:T(8,128)(2,1)S(1)}, bf16[1040,128]{1,0:T(8,128)(2,1)S(1)}, u32[]{:S(2)}, u32[]{:S(2)}) collective-permute-start(bf16[1040,128]{1,0:T(8,128)(2,1)S(1)} %get-tuple-element.28), channel_id=1, source_target_pairs={{0,6},{1,7},{2,0},{3,1},{4,2},{5,3},{6,4},{7,5},{8,14},{9,15},{10,... | collective-permute-start | bytes 798728 | tf_op jit(solution)/shard_map/ppermute | solution.py:362
  5.1 3.0 %collective-permute-start.10 = (bf16[1040,128]{1,0:T(8,128)(2,1)S(1)}, bf16[1040,128]{1,0:T(8,128)(2,1)S(1)}, u32[]{:S(2)}, u32[]{:S(2)}) collective-permute-start(bf16[1040,128]{1,0:T(8,128)(2,1)S(1)} %get-tuple-element.30), channel_id=1, source_target_pairs={{0,7},{1,6},{2,1},{3,0},{4,3},{5,2},{6,5},{7,4},{8,15},{9,14},{10,... | collective-permute-start | bytes 798728 | tf_op jit(solution)/shard_map/ppermute | solution.py:362
  8.0 4.6 %bring.1 = (bf16[8,1024,384]{2,1,0:T(8,128)(2,1)S(1)}, bf16[8,1024,384]{2,1,0:T(8,128)(2,1)S(1)}) custom-call(bf16[1040,128]{1,0:T(8,128)(2,1)S(1)} %get-tuple-element.20._.refs_0_, bf16[8,1024,384]{2,1,0:T(8,128)(2,1)} %gate_ref.1, bf16[8,1024,384]{2,1,0:T(8,128)(2,1)} %up_ref.1), custom_call_target="tpu_custom_call" | custom-call | tf_op jit(solution)/shard_map/bring/pallas_call | solution.py:141
  12.7 0.1 hidden.5.refs_1_
  12.8 1.4 %collective-permute-start.1 = (bf16[1040,128]{1,0:T(8,128)(2,1)S(1)}, bf16[1040,128]{1,0:T(8,128)(2,1)S(1)}, u32[]{:S(2)}, u32[]{:S(2)}) collective-permute-start(bf16[1040,128]{1,0:T(8,128)(2,1)S(1)} %get-tuple-element.24), channel_id=1, source_target_pairs={{0,4},{1,5},{2,6},{3,7},{4,0},{5,1},{6,2},{7,3},{8,12},{9,13},{10,... | collective-permute-start | bytes 798728 | tf_op jit(solution)/shard_map/ppermute | solution.py:362
  14.2 2.0 %collective-permute-start.3 = (bf16[1040,128]{1,0:T(8,128)(2,1)S(1)}, bf16[1040,128]{1,0:T(8,128)(2,1)S(1)}, u32[]{:S(2)}, u32[]{:S(2)}) collective-permute-start(bf16[1040,128]{1,0:T(8,128)(2,1)S(1)} %get-tuple-element.26), channel_id=1, source_target_pairs={{0,5},{1,4},{2,7},{3,6},{4,1},{5,0},{6,3},{7,2},{8,13},{9,12},{10,... | collective-permute-start | bytes 798728 | tf_op jit(solution)/shard_map/ppermute | solution.py:362
  16.2 1.5 %collective-permute-start.5 = (bf16[272,384]{1,0:T(8,128)(2,1)S(1)}, bf16[272,384]{1,0:T(8,128)(2,1)S(1)}, u32[]{:S(2)}, u32[]{:S(2)}) collective-permute-start(bf16[272,384]{1,0:T(8,128)(2,1)S(1)} %hidden.5.refs_1_), channel_id=1, source_target_pairs={{0,8},{8,0},{16,24},{24,16},{32,40},{40,32},{48,56},{56,48},{64,72... | collective-permute-start | bytes 626696 | tf_op jit(solution)/shard_map/ppermute | solution.py:350
  17.7 0.6 hidden.8.refs_3_
  18.3 1.1 %collective-permute-start.8 = (bf16[272,384]{1,0:T(8,128)(2,1)S(1)}, bf16[272,384]{1,0:T(8,128)(2,1)S(1)}, u32[]{:S(2)}, u32[]{:S(2)}) collective-permute-start(bf16[272,384]{1,0:T(8,128)(2,1)S(1)} %hidden.8.refs_3_), channel_id=1, source_target_pairs={{0,8},{8,0},{16,24},{24,16},{32,40},{40,32},{48,56},{56,48},{64,72... | collective-permute-start | bytes 626696 | tf_op jit(solution)/shard_map/ppermute | solution.py:350
  19.3 0.1 hidden.9.refs_5_
  19.5 2.0 %collective-permute-start.11 = (bf16[272,384]{1,0:T(8,128)(2,1)S(1)}, bf16[272,384]{1,0:T(8,128)(2,1)S(1)}, u32[]{:S(2)}, u32[]{:S(2)}) collective-permute-start(bf16[272,384]{1,0:T(8,128)(2,1)S(1)} %hidden.9.refs_5_), channel_id=1, source_target_pairs={{0,8},{8,0},{16,24},{24,16},{32,40},{40,32},{48,56},{56,48},{64,72... | collective-permute-start | bytes 626696 | tf_op jit(solution)/shard_map/ppermute | solution.py:350
  21.5 3.6 %collective-permute-done.1.refs_0_ = bf16[1040,128]{1,0:T(8,128)(2,1)S(1)} collective-permute-done((bf16[1040,128]{1,0:T(8,128)(2,1)S(1)}, bf16[1040,128]{1,0:T(8,128)(2,1)S(1)}, u32[]{:S(2)}, u32[]{:S(2)}) %collective-permute-start.1) | collective-permute-done | bytes 266272 | tf_op jit(solution)/shard_map/ppermute | solution.py:362
  25.1 0.1 hidden.6.refs_1_
  25.2 2.4 %collective-permute-start.2 = (bf16[144,384]{1,0:T(8,128)(2,1)S(1)}, bf16[144,384]{1,0:T(8,128)(2,1)S(1)}, u32[]{:S(2)}, u32[]{:S(2)}) collective-permute-start(bf16[144,384]{1,0:T(8,128)(2,1)S(1)} %hidden.6.refs_1_), channel_id=1, source_target_pairs={{0,8},{8,0},{16,24},{24,16},{32,40},{40,32},{48,56},{56,48},{64,72... | collective-permute-start | bytes 331784 | tf_op jit(solution)/shard_map/ppermute | solution.py:350
  27.6 2.1 %collective-permute-done.3.refs_0_ = bf16[1040,128]{1,0:T(8,128)(2,1)S(1)} collective-permute-done((bf16[1040,128]{1,0:T(8,128)(2,1)S(1)}, bf16[1040,128]{1,0:T(8,128)(2,1)S(1)}, u32[]{:S(2)}, u32[]{:S(2)}) %collective-permute-start.3) | collective-permute-done | bytes 266272 | tf_op jit(solution)/shard_map/ppermute | solution.py:362
  29.7 0.6 hidden.7.refs_3_
  30.3 2.0 %collective-permute-start.4 = (bf16[144,384]{1,0:T(8,128)(2,1)S(1)}, bf16[144,384]{1,0:T(8,128)(2,1)S(1)}, u32[]{:S(2)}, u32[]{:S(2)}) collective-permute-start(bf16[144,384]{1,0:T(8,128)(2,1)S(1)} %hidden.7.refs_3_), channel_id=1, source_target_pairs={{0,8},{8,0},{16,24},{24,16},{32,40},{40,32},{48,56},{56,48},{64,72... | collective-permute-start | bytes 331784 | tf_op jit(solution)/shard_map/ppermute | solution.py:350
  32.3 0.4 collective-permute-done.11.refs_6_
  32.7 0.8 gram.2.refs_5_
  33.5 1.5 %collective-permute-done.2.refs_2_ = bf16[144,384]{1,0:T(8,128)(2,1)S(1)} collective-permute-done((bf16[144,384]{1,0:T(8,128)(2,1)S(1)}, bf16[144,384]{1,0:T(8,128)(2,1)S(1)}, u32[]{:S(2)}, u32[]{:S(2)}) %collective-permute-start.2) | collective-permute-done | bytes 110624 | tf_op jit(solution)/shard_map/ppermute | solution.py:350
  35.1 2.4 %collective-permute-done.4.refs_4_ = bf16[144,384]{1,0:T(8,128)(2,1)S(1)} collective-permute-done((bf16[144,384]{1,0:T(8,128)(2,1)S(1)}, bf16[144,384]{1,0:T(8,128)(2,1)S(1)}, u32[]{:S(2)}, u32[]{:S(2)}) %collective-permute-start.4) | collective-permute-done | bytes 110624 | tf_op jit(solution)/shard_map/ppermute | solution.py:350
  37.4 0.8 gram.3
  38.2 26.3 %all_to_all.10 = f32[8,296,128]{2,1,0:T(8,128)S(1)} all-to-all(f32[8,296,128]{2,1,0:T(8,128)S(1)} %gram.3), channel_id=1, replica_groups={{0,32,64,96,16,48,80,112},{8,40,72,104,24,56,88,120},{1,33,65,97,17,49,..., dimensions={0} | all-to-all | bytes 2424832 | tf_op jit(solution)/shard_map/all_to_all | solution.py:372
  64.5 0.1 reduce_sum.9.refs_0_
  64.6 1.5 %collective-permute-start.12 = (f32[288,128]{1,0:T(8,128)S(1)}, f32[288,128]{1,0:T(8,128)S(1)}, u32[]{:S(2)}, u32[]{:S(2)}) collective-permute-start(f32[288,128]{1,0:T(8,128)S(1)} %slice.8), channel_id=1, source_target_pairs={{32,0},{40,8},{48,16},{56,24},{96,64},{104,72},{112,80},{120,88},{... | collective-permute-start | bytes 442376 | tf_op jit(solution)/shard_map/ppermute | solution.py:377
  66.1 6.8 %first_panels.1 = (f32[128,384]{1,0:T(8,128)S(1)}, f32[128,256]{1,0:T(8,128)S(1)}) custom-call(f32[296,128]{1,0:T(8,128)S(1)} %reduce_sum.9.refs_0_), custom_call_target="tpu_custom_call" | custom-call | tf_op jit(solution)/shard_map/first_panels/pallas_call | solution.py:295
  73.0 4.2 %last_panel.1 = bf16[384,384]{1,0:T(8,128)(2,1)S(1)} custom-call(f32[296,128]{1,0:T(8,128)S(1)} %reduce_sum.9.refs_0_, f32[288,128]{1,0:T(8,128)S(1)} %collective-permute-done.12.refs_1_, f32[128,384]{1,0:T(8,128)S(1)} %get-tuple-element.31.refs_2_, f32[128,256]{1,0:T(8,128)S(1)} %get-tuple-element.32.refs_3_), custom_call_target="tpu_custom_call" | custom-call | tf_op jit(solution)/shard_map/last_panel/pallas_call | solution.py:326
  77.1 14.0 %all_to_all.11 = bf16[16,24,384]{2,1,0:T(8,128)(2,1)S(1)} all-to-all(bf16[16,24,384]{2,1,0:T(8,128)(2,1)S(1)} %bitcast.12), channel_id=1, replica_groups=mesh['dp'=16,'expert'=8] {'dp'}, dimensions={0} | all-to-all | bytes 589824 | tf_op jit(solution)/shard_map/all_to_all | solution.py:383
  91.2 0.7 fusion
  (10 shorter events, 0.0 us)
Async XLA Ops:
  1.7 11.0 %collective-permute-start = (bf16[1040,128]{1,0:T(8,128)(2,1)S(1)}, bf16[1040,128]{1,0:T(8,128)(2,1)S(1)}, u32[]{:S(2)}, u32[]{:S(2)}) collective-permute-start(bf16[1040,128]{1,0:T(8,128)(2,1)S(1)} %get-tuple-element.21), channel_id=1, source_target_pairs={{0,1},{1,0},{2,3},{3,2},{4,5},{5,4},{6,7},{7,6},{8,9},{9,8},{10,11... | collective-permute-start | bytes 798728 | tf_op jit(solution)/shard_map/ppermute | solution.py:362
  1.8 12.4 %collective-permute-start.6 = (bf16[1040,128]{1,0:T(8,128)(2,1)S(1)}, bf16[1040,128]{1,0:T(8,128)(2,1)S(1)}, u32[]{:S(2)}, u32[]{:S(2)}) collective-permute-start(bf16[1040,128]{1,0:T(8,128)(2,1)S(1)} %get-tuple-element.27), channel_id=1, source_target_pairs={{0,2},{1,3},{2,4},{3,5},{4,6},{5,7},{6,0},{7,1},{8,10},{9,11},{10,... | collective-permute-start | bytes 798728 | tf_op jit(solution)/shard_map/ppermute | solution.py:362
  3.5 12.7 %collective-permute-start.7 = (bf16[1040,128]{1,0:T(8,128)(2,1)S(1)}, bf16[1040,128]{1,0:T(8,128)(2,1)S(1)}, u32[]{:S(2)}, u32[]{:S(2)}) collective-permute-start(bf16[1040,128]{1,0:T(8,128)(2,1)S(1)} %get-tuple-element.28), channel_id=1, source_target_pairs={{0,6},{1,7},{2,0},{3,1},{4,2},{5,3},{6,4},{7,5},{8,14},{9,15},{10,... | collective-permute-start | bytes 798728 | tf_op jit(solution)/shard_map/ppermute | solution.py:362
  5.1 13.2 %collective-permute-start.9 = (bf16[1040,128]{1,0:T(8,128)(2,1)S(1)}, bf16[1040,128]{1,0:T(8,128)(2,1)S(1)}, u32[]{:S(2)}, u32[]{:S(2)}) collective-permute-start(bf16[1040,128]{1,0:T(8,128)(2,1)S(1)} %get-tuple-element.29), channel_id=1, source_target_pairs={{0,3},{1,2},{2,5},{3,4},{4,7},{5,6},{6,1},{7,0},{8,11},{9,10},{10,... | collective-permute-start | bytes 798728 | tf_op jit(solution)/shard_map/ppermute | solution.py:362
  5.1 14.3 %collective-permute-start.10 = (bf16[1040,128]{1,0:T(8,128)(2,1)S(1)}, bf16[1040,128]{1,0:T(8,128)(2,1)S(1)}, u32[]{:S(2)}, u32[]{:S(2)}) collective-permute-start(bf16[1040,128]{1,0:T(8,128)(2,1)S(1)} %get-tuple-element.30), channel_id=1, source_target_pairs={{0,7},{1,6},{2,1},{3,0},{4,3},{5,2},{6,5},{7,4},{8,15},{9,14},{10,... | collective-permute-start | bytes 798728 | tf_op jit(solution)/shard_map/ppermute | solution.py:362
  12.8 12.3 %collective-permute-start.1 = (bf16[1040,128]{1,0:T(8,128)(2,1)S(1)}, bf16[1040,128]{1,0:T(8,128)(2,1)S(1)}, u32[]{:S(2)}, u32[]{:S(2)}) collective-permute-start(bf16[1040,128]{1,0:T(8,128)(2,1)S(1)} %get-tuple-element.24), channel_id=1, source_target_pairs={{0,4},{1,5},{2,6},{3,7},{4,0},{5,1},{6,2},{7,3},{8,12},{9,13},{10,... | collective-permute-start | bytes 798728 | tf_op jit(solution)/shard_map/ppermute | solution.py:362
  14.2 15.5 %collective-permute-start.3 = (bf16[1040,128]{1,0:T(8,128)(2,1)S(1)}, bf16[1040,128]{1,0:T(8,128)(2,1)S(1)}, u32[]{:S(2)}, u32[]{:S(2)}) collective-permute-start(bf16[1040,128]{1,0:T(8,128)(2,1)S(1)} %get-tuple-element.26), channel_id=1, source_target_pairs={{0,5},{1,4},{2,7},{3,6},{4,1},{5,0},{6,3},{7,2},{8,13},{9,12},{10,... | collective-permute-start | bytes 798728 | tf_op jit(solution)/shard_map/ppermute | solution.py:362
  16.2 16.0 %collective-permute-start.5 = (bf16[272,384]{1,0:T(8,128)(2,1)S(1)}, bf16[272,384]{1,0:T(8,128)(2,1)S(1)}, u32[]{:S(2)}, u32[]{:S(2)}) collective-permute-start(bf16[272,384]{1,0:T(8,128)(2,1)S(1)} %hidden.5.refs_1_), channel_id=1, source_target_pairs={{0,8},{8,0},{16,24},{24,16},{32,40},{40,32},{48,56},{56,48},{64,72... | collective-permute-start | bytes 626696 | tf_op jit(solution)/shard_map/ppermute | solution.py:350
  18.3 14.0 %collective-permute-start.8 = (bf16[272,384]{1,0:T(8,128)(2,1)S(1)}, bf16[272,384]{1,0:T(8,128)(2,1)S(1)}, u32[]{:S(2)}, u32[]{:S(2)}) collective-permute-start(bf16[272,384]{1,0:T(8,128)(2,1)S(1)} %hidden.8.refs_3_), channel_id=1, source_target_pairs={{0,8},{8,0},{16,24},{24,16},{32,40},{40,32},{48,56},{56,48},{64,72... | collective-permute-start | bytes 626696 | tf_op jit(solution)/shard_map/ppermute | solution.py:350
  19.5 13.2 %collective-permute-start.11 = (bf16[272,384]{1,0:T(8,128)(2,1)S(1)}, bf16[272,384]{1,0:T(8,128)(2,1)S(1)}, u32[]{:S(2)}, u32[]{:S(2)}) collective-permute-start(bf16[272,384]{1,0:T(8,128)(2,1)S(1)} %hidden.9.refs_5_), channel_id=1, source_target_pairs={{0,8},{8,0},{16,24},{24,16},{32,40},{40,32},{48,56},{56,48},{64,72... | collective-permute-start | bytes 626696 | tf_op jit(solution)/shard_map/ppermute | solution.py:350
  25.2 9.9 %collective-permute-start.2 = (bf16[144,384]{1,0:T(8,128)(2,1)S(1)}, bf16[144,384]{1,0:T(8,128)(2,1)S(1)}, u32[]{:S(2)}, u32[]{:S(2)}) collective-permute-start(bf16[144,384]{1,0:T(8,128)(2,1)S(1)} %hidden.6.refs_1_), channel_id=1, source_target_pairs={{0,8},{8,0},{16,24},{24,16},{32,40},{40,32},{48,56},{56,48},{64,72... | collective-permute-start | bytes 331784 | tf_op jit(solution)/shard_map/ppermute | solution.py:350
  30.3 7.2 %collective-permute-start.4 = (bf16[144,384]{1,0:T(8,128)(2,1)S(1)}, bf16[144,384]{1,0:T(8,128)(2,1)S(1)}, u32[]{:S(2)}, u32[]{:S(2)}) collective-permute-start(bf16[144,384]{1,0:T(8,128)(2,1)S(1)} %hidden.7.refs_3_), channel_id=1, source_target_pairs={{0,8},{8,0},{16,24},{24,16},{32,40},{40,32},{48,56},{56,48},{64,72... | collective-permute-start | bytes 331784 | tf_op jit(solution)/shard_map/ppermute | solution.py:350
  64.6 8.3 %collective-permute-start.12 = (f32[288,128]{1,0:T(8,128)S(1)}, f32[288,128]{1,0:T(8,128)S(1)}, u32[]{:S(2)}, u32[]{:S(2)}) collective-permute-start(f32[288,128]{1,0:T(8,128)S(1)} %slice.8), channel_id=1, source_target_pairs={{32,0},{40,8},{48,16},{56,24},{96,64},{104,72},{112,80},{120,88},{... | collective-permute-start | bytes 442376 | tf_op jit(solution)/shard_map/ppermute | solution.py:377

commit v4 on v3

--- a/solution.py
+++ b/solution.py
@@ -12,7 +12,7 @@
 TAG = 16
 SIDE = 4
 VMEM_BYTES = 20 << 20
-EDGES = (0, 2, 4, 6, 7, 8)
+EDGES = (0, 2, 4, 6, 8)
 STRIP = 64
 F32 = jnp.float32
 BF16 = jnp.bfloat16
@@ -349,24 +349,30 @@
         rows = hidden_rows(arrived[EDGES[g] : EDGES[g + 1]], *weights)
         gathered.append([rows, lax.ppermute(rows, "dp", pairs)])
 
-    for (dy, dc), payload in zip(shifts, outgoing):
+    def send(payload, dy, dc):
         route = [
             (y * 2 + c, ((y + dy) % chips) * 2 + (c + dc) % 2)
             for y in range(chips)
             for c in range(2)
         ]
-        if dy == 2 and not gathered:
-            swap_rows(0)
-        if dy == 2:
-            payload, _ = lax.optimization_barrier((payload, gathered[0][0]))
-        arrived.append(payload if dy == dc == 0 else lax.ppermute(payload, "expert", route))
-    for g in range(1, len(EDGES) - 1):
+        return lax.ppermute(payload, "expert", route)
+
+    half_way = {}
+    for slot, step in ((6, 1), (7, -1)):
+        half_way[slot] = send(outgoing[slot], step, 0)
+    for slot, (dy, dc) in enumerate(shifts):
+        if slot == 0:
+            arrived.append(outgoing[0])
+        elif slot in half_way:
+            arrived.append(send(half_way[slot], 1 if slot == 6 else -1, dc))
+        else:
+            arrived.append(send(outgoing[slot], dy, dc))
+    for g in range(len(EDGES) - 1):
         swap_rows(g)
     kept = experts_each // 2
     first = (lax.axis_index("dp") % 2 * kept).reshape(1)
-    partial_gram = gram(first, kept, [rows for pair in gathered[:-2] for rows in pair])
-    tail = [rows for pair in gathered[-2:] for rows in pair]
-    partial_gram = gram(first, kept, tail, (partial_gram,))
+    partial_gram = gram(first, kept, [rows for pair in gathered[:-1] for rows in pair])
+    partial_gram = gram(first, kept, gathered[-1], (partial_gram,))
     side = replicas // SIDE
     classes = [[x * SIDE + z for z in range(p, SIDE, 2) for x in range(side)] for p in range(2)]
     pieces = lax.all_to_all(

time: 92.1 us -> 99.1 us (1.076)
  waiting for transfers between devices: 10 us -> 19.5 us
  starting transfers between devices: 20.2 us -> 18.3 us
    ppermute x5 -> x4, waiting for transfers between devices: 4.33 us -> 12.7 us  [swap_rows(): gathered.append([rows, lax.ppermute(rows, 'dp', pairs)])]
    ppermute x5 -> x4, starting transfers between devices: 8.97 us -> 7.15 us  [swap_rows(): gathered.append([rows, lax.ppermute(rows, 'dp', pairs)])]
    ppermute x7 -> x9, waiting for transfers between devices: 5.66 us -> 6.82 us  [send(): return lax.ppermute(payload, 'expert', route)]
    ppermute x7 -> x9, starting transfers between devices: 9.75 us -> 9.66 us  [send(): return lax.ppermute(payload, 'expert', route)]
  transfers between devices with their start and end apart: 13 -> 14, of which waited for: 5 -> 7; matrix products, arithmetic and copies ran while one was open for 0% -> 0% of each run, Pallas kernels for 15% -> 14%
where the time goes in v4:
time: 99.1 us; the launch traced here: 98.9 us
  blocking collectives  39.8 us (40%)
  Pallas kernels  20.3 us (20%)
  waiting for transfers between devices  19.5 us (20%)
  starting transfers between devices  18.3 us (18%)
    all_to_all x1, blocking collectives, on_device(): lax.all_to_all(partial_gram, 'dp', split_axis=0, concat_axis=0, axis_inde...  26.3 us
    all_to_all x1, blocking collectives, on_device(): lax.all_to_all(sent, 'dp', split_axis=0, concat_axis=0, tiled=True)  13.5 us
    ppermute x4, waiting for transfers between devices, swap_rows(): gathered.append([rows, lax.ppermute(rows, 'dp', pairs)])  12.7 us
    ppermute x9, starting transfers between devices, send(): return lax.ppermute(payload, 'expert', route)  9.66 us
    ppermute x4, starting transfers between devices, swap_rows(): gathered.append([rows, lax.ppermute(rows, 'dp', pairs)])  7.15 us
    pallas_call x1, Pallas kernels, first_panels(): pl.pallas_call(lambda *refs: first_kernel(*refs, scale=scale), out_shape=...  6.85 us
    ppermute x9, waiting for transfers between devices, send(): return lax.ppermute(payload, 'expert', route)  6.82 us
    pallas_call x1, Pallas kernels, bring(): pl.pallas_call(bring_kernel, in_specs=[pl.BlockSpec(memory_space=pl.ANY)]...  4.62 us
  transfers between devices with their start and end apart: 14, of which 7 were waited for; matrix products, arithmetic and copies ran while one was open for 0% of the time, Pallas kernels for 14%

profile of v4, /device:TPU:0, one launch (start us, length us, event | category | flops | bytes accessed | tf_op | source)
XLA Modules:
  0.0 98.9 jit_solution(15875528290012756789)
XLA Ops:
  0.0 1.7 %pack.1 = (bf16[1040,128]{1,0:T(8,128)(2,1)S(1)}, bf16[1040,128]{1,0:T(8,128)(2,1)S(1)}, bf16[1040,128]{1,0:T(8,128)(2,1)S(1)}, bf16[1040,128]{1,0:T(8,128)(2,1)...) custom-call(s32[1]{0:T(128)} %bitcast.1.refs_0_, ...), custom_call_target="tpu_custom_call" | custom-call | tf_op jit(solution)/shard_map/pack/pallas_call | solution.py:71
  1.7 1.8 %collective-permute-start = (bf16[1040,128]{1,0:T(8,128)(2,1)S(1)}, bf16[1040,128]{1,0:T(8,128)(2,1)S(1)}, u32[]{:S(2)}, u32[]{:S(2)}) collective-permute-start(bf16[1040,128]{1,0:T(8,128)(2,1)S(1)} %get-tuple-element.17), channel_id=1, source_target_pairs={{0,2},{1,3},{2,4},{3,5},{4,6},{5,7},{6,0},{7,1},{8,10},{9,11},{10,... | collective-permute-start | bytes 798728 | tf_op jit(solution)/shard_map/ppermute | solution.py:358
  3.4 1.5 %collective-permute-start.2 = (bf16[1040,128]{1,0:T(8,128)(2,1)S(1)}, bf16[1040,128]{1,0:T(8,128)(2,1)S(1)}, u32[]{:S(2)}, u32[]{:S(2)}) collective-permute-start(bf16[1040,128]{1,0:T(8,128)(2,1)S(1)} %get-tuple-element.18), channel_id=1, source_target_pairs={{0,6},{1,7},{2,0},{3,1},{4,2},{5,3},{6,4},{7,5},{8,14},{9,15},{10,... | collective-permute-start | bytes 798728 | tf_op jit(solution)/shard_map/ppermute | solution.py:358
  5.0 0.5 collective-permute-start.7
  5.4 2.8 %collective-permute-start.8 = (bf16[1040,128]{1,0:T(8,128)(2,1)S(1)}, bf16[1040,128]{1,0:T(8,128)(2,1)S(1)}, u32[]{:S(2)}, u32[]{:S(2)}) collective-permute-start(bf16[1040,128]{1,0:T(8,128)(2,1)S(1)} %get-tuple-element.24), channel_id=1, source_target_pairs={{0,6},{1,7},{2,0},{3,1},{4,2},{5,3},{6,4},{7,5},{8,14},{9,15},{10,... | collective-permute-start | bytes 798728 | tf_op jit(solution)/shard_map/ppermute | solution.py:358
  8.2 4.0 %collective-permute-done = bf16[1040,128]{1,0:T(8,128)(2,1)S(1)} collective-permute-done((bf16[1040,128]{1,0:T(8,128)(2,1)S(1)}, bf16[1040,128]{1,0:T(8,128)(2,1)S(1)}, u32[]{:S(2)}, u32[]{:S(2)}) %collective-permute-start) | collective-permute-done | bytes 266272 | tf_op jit(solution)/shard_map/ppermute | solution.py:358
  12.2 0.5 collective-permute-done.2
  12.7 2.5 %collective-permute-start.11 = (bf16[1040,128]{1,0:T(8,128)(2,1)S(1)}, bf16[1040,128]{1,0:T(8,128)(2,1)S(1)}, u32[]{:S(2)}, u32[]{:S(2)}) collective-permute-start(bf16[1040,128]{1,0:T(8,128)(2,1)S(1)} %get-tuple-element.26), channel_id=1, source_target_pairs={{0,7},{1,6},{2,1},{3,0},{4,3},{5,2},{6,5},{7,4},{8,15},{9,14},{10,... | collective-permute-start | bytes 798728 | tf_op jit(solution)/shard_map/ppermute | solution.py:358
  15.2 2.3 %collective-permute-done.7.refs_0_ = bf16[1040,128]{1,0:T(8,128)(2,1)S(1)} collective-permute-done((bf16[1040,128]{1,0:T(8,128)(2,1)S(1)}, bf16[1040,128]{1,0:T(8,128)(2,1)S(1)}, u32[]{:S(2)}, u32[]{:S(2)}) %collective-permute-start.7) | collective-permute-done | bytes 266272 | tf_op jit(solution)/shard_map/ppermute | solution.py:358
  17.5 0.6 collective-permute-start.3
  18.1 4.6 %bring.1 = (bf16[8,1024,384]{2,1,0:T(8,128)(2,1)S(1)}, bf16[8,1024,384]{2,1,0:T(8,128)(2,1)S(1)}) custom-call(bf16[1040,128]{1,0:T(8,128)(2,1)S(1)} %get-tuple-element.19._.refs_0_, bf16[8,1024,384]{2,1,0:T(8,128)(2,1)} %gate_ref.1, bf16[8,1024,384]{2,1,0:T(8,128)(2,1)} %up_ref.1), custom_call_target="tpu_custom_call" | custom-call | tf_op jit(solution)/shard_map/bring/pallas_call | solution.py:141
  22.8 0.1 hidden.5.refs_1_
  22.9 3.0 %collective-permute-start.6 = (bf16[272,384]{1,0:T(8,128)(2,1)S(1)}, bf16[272,384]{1,0:T(8,128)(2,1)S(1)}, u32[]{:S(2)}, u32[]{:S(2)}) collective-permute-start(bf16[272,384]{1,0:T(8,128)(2,1)S(1)} %hidden.5.refs_1_), channel_id=1, source_target_pairs={{0,8},{8,0},{16,24},{24,16},{32,40},{40,32},{48,56},{56,48},{64,72... | collective-permute-start | bytes 626696 | tf_op jit(solution)/shard_map/ppermute | solution.py:350
  25.9 0.6 hidden.6.refs_3_
  26.5 0.5 collective-permute-start.9
  27.0 0.1 hidden.7.refs_5_
  27.2 2.5 %collective-permute-start.12 = (bf16[272,384]{1,0:T(8,128)(2,1)S(1)}, bf16[272,384]{1,0:T(8,128)(2,1)S(1)}, u32[]{:S(2)}, u32[]{:S(2)}) collective-permute-start(bf16[272,384]{1,0:T(8,128)(2,1)S(1)} %hidden.7.refs_5_), channel_id=1, source_target_pairs={{0,8},{8,0},{16,24},{24,16},{32,40},{40,32},{48,56},{56,48},{64,72... | collective-permute-start | bytes 626696 | tf_op jit(solution)/shard_map/ppermute | solution.py:350
  29.7 0.6 hidden.4.refs_1_
  30.2 1.1 %collective-permute-start.4 = (bf16[272,384]{1,0:T(8,128)(2,1)S(1)}, bf16[272,384]{1,0:T(8,128)(2,1)S(1)}, u32[]{:S(2)}, u32[]{:S(2)}) collective-permute-start(bf16[272,384]{1,0:T(8,128)(2,1)S(1)} %hidden.4.refs_1_), channel_id=1, source_target_pairs={{0,8},{8,0},{16,24},{24,16},{32,40},{40,32},{48,56},{56,48},{64,72... | collective-permute-start | bytes 626696 | tf_op jit(solution)/shard_map/ppermute | solution.py:350
  31.4 0.1 collective-permute-done.6.refs_2_
  31.5 4.5 %collective-permute-done.9.refs_4_ = bf16[272,384]{1,0:T(8,128)(2,1)S(1)} collective-permute-done((bf16[272,384]{1,0:T(8,128)(2,1)S(1)}, bf16[272,384]{1,0:T(8,128)(2,1)S(1)}, u32[]{:S(2)}, u32[]{:S(2)}) %collective-permute-start.9) | collective-permute-done | bytes 208928 | tf_op jit(solution)/shard_map/ppermute | solution.py:350
  36.0 4.5 %collective-permute-done.12.refs_6_ = bf16[272,384]{1,0:T(8,128)(2,1)S(1)} collective-permute-done((bf16[272,384]{1,0:T(8,128)(2,1)S(1)}, bf16[272,384]{1,0:T(8,128)(2,1)S(1)}, u32[]{:S(2)}, u32[]{:S(2)}) %collective-permute-start.12) | collective-permute-done | bytes 208928 | tf_op jit(solution)/shard_map/ppermute | solution.py:350
  40.5 0.8 gram.2.refs_3_
  41.3 3.6 %collective-permute-done.4.refs_2_ = bf16[272,384]{1,0:T(8,128)(2,1)S(1)} collective-permute-done((bf16[272,384]{1,0:T(8,128)(2,1)S(1)}, bf16[272,384]{1,0:T(8,128)(2,1)S(1)}, u32[]{:S(2)}, u32[]{:S(2)}) %collective-permute-start.4) | collective-permute-done | bytes 208928 | tf_op jit(solution)/shard_map/ppermute | solution.py:350
  44.9 0.8 gram.3
  45.7 26.3 %all_to_all.10 = f32[8,296,128]{2,1,0:T(8,128)S(1)} all-to-all(f32[8,296,128]{2,1,0:T(8,128)S(1)} %gram.3), channel_id=1, replica_groups={{0,32,64,96,16,48,80,112},{8,40,72,104,24,56,88,120},{1,33,65,97,17,49,..., dimensions={0} | all-to-all | bytes 2424832 | tf_op jit(solution)/shard_map/all_to_all | solution.py:378
  72.0 0.1 reduce_sum.9.refs_0_
  72.1 1.5 %collective-permute-start.13 = (f32[288,128]{1,0:T(8,128)S(1)}, f32[288,128]{1,0:T(8,128)S(1)}, u32[]{:S(2)}, u32[]{:S(2)}) collective-permute-start(f32[288,128]{1,0:T(8,128)S(1)} %slice.8), channel_id=1, source_target_pairs={{32,0},{40,8},{48,16},{56,24},{96,64},{104,72},{112,80},{120,88},{... | collective-permute-start | bytes 442376 | tf_op jit(solution)/shard_map/ppermute | solution.py:383
  73.5 6.8 %first_panels.1 = (f32[128,384]{1,0:T(8,128)S(1)}, f32[128,256]{1,0:T(8,128)S(1)}) custom-call(f32[296,128]{1,0:T(8,128)S(1)} %reduce_sum.9.refs_0_), custom_call_target="tpu_custom_call" | custom-call | tf_op jit(solution)/shard_map/first_panels/pallas_call | solution.py:295
  80.4 4.2 %last_panel.1 = bf16[384,384]{1,0:T(8,128)(2,1)S(1)} custom-call(f32[296,128]{1,0:T(8,128)S(1)} %reduce_sum.9.refs_0_, f32[288,128]{1,0:T(8,128)S(1)} %collective-permute-done.13.refs_1_, f32[128,384]{1,0:T(8,128)S(1)} %get-tuple-element.27.refs_2_, f32[128,256]{1,0:T(8,128)S(1)} %get-tuple-element.28.refs_3_), custom_call_target="tpu_custom_call" | custom-call | tf_op jit(solution)/shard_map/last_panel/pallas_call | solution.py:326
  84.6 13.5 %all_to_all.11 = bf16[16,24,384]{2,1,0:T(8,128)(2,1)S(1)} all-to-all(bf16[16,24,384]{2,1,0:T(8,128)(2,1)S(1)} %bitcast.12), channel_id=1, replica_groups=mesh['dp'=16,'expert'=8] {'dp'}, dimensions={0} | all-to-all | bytes 589824 | tf_op jit(solution)/shard_map/all_to_all | solution.py:389
  98.1 0.7 fusion
  (11 shorter events, 0.0 us)
Async XLA Ops:
  1.7 10.5 %collective-permute-start = (bf16[1040,128]{1,0:T(8,128)(2,1)S(1)}, bf16[1040,128]{1,0:T(8,128)(2,1)S(1)}, u32[]{:S(2)}, u32[]{:S(2)}) collective-permute-start(bf16[1040,128]{1,0:T(8,128)(2,1)S(1)} %get-tuple-element.17), channel_id=1, source_target_pairs={{0,2},{1,3},{2,4},{3,5},{4,6},{5,7},{6,0},{7,1},{8,10},{9,11},{10,... | collective-permute-start | bytes 798728 | tf_op jit(solution)/shard_map/ppermute | solution.py:358
  3.4 9.3 %collective-permute-start.2 = (bf16[1040,128]{1,0:T(8,128)(2,1)S(1)}, bf16[1040,128]{1,0:T(8,128)(2,1)S(1)}, u32[]{:S(2)}, u32[]{:S(2)}) collective-permute-start(bf16[1040,128]{1,0:T(8,128)(2,1)S(1)} %get-tuple-element.18), channel_id=1, source_target_pairs={{0,6},{1,7},{2,0},{3,1},{4,2},{5,3},{6,4},{7,5},{8,14},{9,15},{10,... | collective-permute-start | bytes 798728 | tf_op jit(solution)/shard_map/ppermute | solution.py:358
  5.0 10.2 %collective-permute-start.5 = (bf16[1040,128]{1,0:T(8,128)(2,1)S(1)}, bf16[1040,128]{1,0:T(8,128)(2,1)S(1)}, u32[]{:S(2)}, u32[]{:S(2)}) collective-permute-start(bf16[1040,128]{1,0:T(8,128)(2,1)S(1)} %get-tuple-element.22), channel_id=1, source_target_pairs={{0,1},{1,0},{2,3},{3,2},{4,5},{5,4},{6,7},{7,6},{8,9},{9,8},{10,11... | collective-permute-start | bytes 798728 | tf_op jit(solution)/shard_map/ppermute | solution.py:358
  5.0 12.5 %collective-permute-start.7 = (bf16[1040,128]{1,0:T(8,128)(2,1)S(1)}, bf16[1040,128]{1,0:T(8,128)(2,1)S(1)}, u32[]{:S(2)}, u32[]{:S(2)}) collective-permute-start(bf16[1040,128]{1,0:T(8,128)(2,1)S(1)} %get-tuple-element.23), channel_id=1, source_target_pairs={{0,2},{1,3},{2,4},{3,5},{4,6},{5,7},{6,0},{7,1},{8,10},{9,11},{10,... | collective-permute-start | bytes 798728 | tf_op jit(solution)/shard_map/ppermute | solution.py:358
  5.4 17.5 %collective-permute-start.8 = (bf16[1040,128]{1,0:T(8,128)(2,1)S(1)}, bf16[1040,128]{1,0:T(8,128)(2,1)S(1)}, u32[]{:S(2)}, u32[]{:S(2)}) collective-permute-start(bf16[1040,128]{1,0:T(8,128)(2,1)S(1)} %get-tuple-element.24), channel_id=1, source_target_pairs={{0,6},{1,7},{2,0},{3,1},{4,2},{5,3},{6,4},{7,5},{8,14},{9,15},{10,... | collective-permute-start | bytes 798728 | tf_op jit(solution)/shard_map/ppermute | solution.py:358
  12.2 14.3 %collective-permute-start.10 = (bf16[1040,128]{1,0:T(8,128)(2,1)S(1)}, bf16[1040,128]{1,0:T(8,128)(2,1)S(1)}, u32[]{:S(2)}, u32[]{:S(2)}) collective-permute-start(bf16[1040,128]{1,0:T(8,128)(2,1)S(1)} %get-tuple-element.25), channel_id=1, source_target_pairs={{0,3},{1,2},{2,5},{3,4},{4,7},{5,6},{6,1},{7,0},{8,11},{9,10},{10,... | collective-permute-start | bytes 798728 | tf_op jit(solution)/shard_map/ppermute | solution.py:358
  12.7 14.3 %collective-permute-start.11 = (bf16[1040,128]{1,0:T(8,128)(2,1)S(1)}, bf16[1040,128]{1,0:T(8,128)(2,1)S(1)}, u32[]{:S(2)}, u32[]{:S(2)}) collective-permute-start(bf16[1040,128]{1,0:T(8,128)(2,1)S(1)} %get-tuple-element.26), channel_id=1, source_target_pairs={{0,7},{1,6},{2,1},{3,0},{4,3},{5,2},{6,5},{7,4},{8,15},{9,14},{10,... | collective-permute-start | bytes 798728 | tf_op jit(solution)/shard_map/ppermute | solution.py:358
  15.2 14.5 %collective-permute-start.1 = (bf16[1040,128]{1,0:T(8,128)(2,1)S(1)}, bf16[1040,128]{1,0:T(8,128)(2,1)S(1)}, u32[]{:S(2)}, u32[]{:S(2)}) collective-permute-start(bf16[1040,128]{1,0:T(8,128)(2,1)S(1)} %collective-permute-done), channel_id=1, source_target_pairs={{0,2},{1,3},{2,4},{3,5},{4,6},{5,7},{6,0},{7,1},{8,10},{9,11},{10,... | collective-permute-start | bytes 798728 | tf_op jit(solution)/shard_map/ppermute | solution.py:358
  17.5 12.2 %collective-permute-start.3 = (bf16[1040,128]{1,0:T(8,128)(2,1)S(1)}, bf16[1040,128]{1,0:T(8,128)(2,1)S(1)}, u32[]{:S(2)}, u32[]{:S(2)}) collective-permute-start(bf16[1040,128]{1,0:T(8,128)(2,1)S(1)} %collective-permute-done.2), channel_id=1, source_target_pairs={{0,7},{1,6},{2,1},{3,0},{4,3},{5,2},{6,5},{7,4},{8,15},{9,14},{10,... | collective-permute-start | bytes 798728 | tf_op jit(solution)/shard_map/ppermute | solution.py:358
  22.9 8.6 %collective-permute-start.6 = (bf16[272,384]{1,0:T(8,128)(2,1)S(1)}, bf16[272,384]{1,0:T(8,128)(2,1)S(1)}, u32[]{:S(2)}, u32[]{:S(2)}) collective-permute-start(bf16[272,384]{1,0:T(8,128)(2,1)S(1)} %hidden.5.refs_1_), channel_id=1, source_target_pairs={{0,8},{8,0},{16,24},{24,16},{32,40},{40,32},{48,56},{56,48},{64,72... | collective-permute-start | bytes 626696 | tf_op jit(solution)/shard_map/ppermute | solution.py:350
  26.5 9.5 %collective-permute-start.9 = (bf16[272,384]{1,0:T(8,128)(2,1)S(1)}, bf16[272,384]{1,0:T(8,128)(2,1)S(1)}, u32[]{:S(2)}, u32[]{:S(2)}) collective-permute-start(bf16[272,384]{1,0:T(8,128)(2,1)S(1)} %hidden.6.refs_3_), channel_id=1, source_target_pairs={{0,8},{8,0},{16,24},{24,16},{32,40},{40,32},{48,56},{56,48},{64,72... | collective-permute-start | bytes 626696 | tf_op jit(solution)/shard_map/ppermute | solution.py:350
  27.2 13.3 %collective-permute-start.12 = (bf16[272,384]{1,0:T(8,128)(2,1)S(1)}, bf16[272,384]{1,0:T(8,128)(2,1)S(1)}, u32[]{:S(2)}, u32[]{:S(2)}) collective-permute-start(bf16[272,384]{1,0:T(8,128)(2,1)S(1)} %hidden.7.refs_5_), channel_id=1, source_target_pairs={{0,8},{8,0},{16,24},{24,16},{32,40},{40,32},{48,56},{56,48},{64,72... | collective-permute-start | bytes 626696 | tf_op jit(solution)/shard_map/ppermute | solution.py:350
  30.2 14.7 %collective-permute-start.4 = (bf16[272,384]{1,0:T(8,128)(2,1)S(1)}, bf16[272,384]{1,0:T(8,128)(2,1)S(1)}, u32[]{:S(2)}, u32[]{:S(2)}) collective-permute-start(bf16[272,384]{1,0:T(8,128)(2,1)S(1)} %hidden.4.refs_1_), channel_id=1, source_target_pairs={{0,8},{8,0},{16,24},{24,16},{32,40},{40,32},{48,56},{56,48},{64,72... | collective-permute-start | bytes 626696 | tf_op jit(solution)/shard_map/ppermute | solution.py:350
  72.1 8.3 %collective-permute-start.13 = (f32[288,128]{1,0:T(8,128)S(1)}, f32[288,128]{1,0:T(8,128)S(1)}, u32[]{:S(2)}, u32[]{:S(2)}) collective-permute-start(f32[288,128]{1,0:T(8,128)S(1)} %slice.8), channel_id=1, source_target_pairs={{32,0},{40,8},{48,16},{56,24},{96,64},{104,72},{112,80},{120,88},{... | collective-permute-start | bytes 442376 | tf_op jit(solution)/shard_map/ppermute | solution.py:383

commit v5 on v3

--- a/solution.py
+++ b/solution.py
@@ -84,14 +84,27 @@
     )(member, far(assign), far(tokens))
 
 
-def hidden_kernel(*refs, slots, model_width):
+def hidden_kernel(*refs, slots, model_width, fetch):
     xs = refs[:slots]
-    gate_ref, up_ref, out_ref = refs[slots:]
+    gate_ref, up_ref, out_ref = refs[slots : slots + 3]
     chunks = model_width // LANE
     codes = []
     for s in range(slots):
         tag = xs[s][chunks * BLOCK : chunks * BLOCK + TAG, :].astype(F32)
         codes.append(jnp.max(tag).astype(jnp.int32))
+    experts = [jnp.maximum(code - 1, 0) for code in codes]
+    if fetch:
+        gate_buf, up_buf, sem = refs[slots + 3 :]
+        copies = []
+        for s in range(slots):
+            copies.append(
+                (
+                    pltpu.make_async_copy(gate_ref.at[experts[s]], gate_buf.at[s], sem.at[0, s]),
+                    pltpu.make_async_copy(up_ref.at[experts[s]], up_buf.at[s], sem.at[1, s]),
+                )
+            )
+            for copy in copies[-1]:
+                copy.start()
 
     width = out_ref.shape[1]
     lane = lax.broadcasted_iota(jnp.int32, (TAG, width), 1)
@@ -100,30 +113,38 @@
         tags = jnp.where(lane == s, codes[s].astype(F32), tags)
     out_ref[slots * BLOCK :, :] = tags.astype(BF16)
     for s in range(slots):
+        if fetch:
+            for copy in copies[s]:
+                copy.wait()
 
         @pl.when(codes[s] > 0)
         def _(s=s):
-            expert = codes[s] - 1
             x = jnp.concatenate(
                 [xs[s][c * BLOCK : (c + 1) * BLOCK, :] for c in range(chunks)], axis=1
             )
-            gate = jnp.dot(x, gate_ref[expert], preferred_element_type=F32)
-            up = jnp.dot(x, up_ref[expert], preferred_element_type=F32)
+            gate_part = gate_buf[s] if fetch else gate_ref[experts[s]]
+            up_part = up_buf[s] if fetch else up_ref[experts[s]]
+            gate = jnp.dot(x, gate_part, preferred_element_type=F32)
+            up = jnp.dot(x, up_part, preferred_element_type=F32)
             hidden = gate / (1.0 + jnp.exp(-gate)) * up
             out_ref[s * BLOCK : (s + 1) * BLOCK, :] = hidden.astype(BF16)
 
 
-def hidden_rows(arrived, gate_weight, up_weight):
+def hidden_rows(arrived, gate_weight, up_weight, fetch=False):
     slots = len(arrived)
     _, model_width, hidden_width = gate_weight.shape
-    return pl.pallas_call(
-        lambda *refs: hidden_kernel(*refs, slots=slots, model_width=model_width),
-        in_specs=[pl.BlockSpec(memory_space=pltpu.VMEM)] * (slots + 2),
+    place = far if fetch else near
+    held = [pltpu.VMEM((slots, model_width, hidden_width), BF16)] * 2
+    return pl.pallas_call(
+        lambda *refs: hidden_kernel(*refs, slots=slots, model_width=model_width, fetch=fetch),
+        in_specs=[pl.BlockSpec(memory_space=pltpu.VMEM)] * slots
+        + [pl.BlockSpec(memory_space=pl.ANY if fetch else pltpu.VMEM)] * 2,
         out_specs=pl.BlockSpec(memory_space=pltpu.VMEM),
         out_shape=pltpu.VMEM((slots * BLOCK + TAG, hidden_width), BF16),
+        scratch_shapes=held + [pltpu.SemaphoreType.DMA((2, slots))] if fetch else [],
         compiler_params=pltpu.CompilerParams(vmem_limit_bytes=VMEM_BYTES),
         name="hidden",
-    )(*[near(x) for x in (*arrived, gate_weight, up_weight)])
+    )(*[near(x) for x in arrived], place(gate_weight), place(up_weight))
 
 
 def bring_kernel(_, gate_ref, up_ref, gate_out, up_out, sem):
@@ -343,10 +364,10 @@
     outgoing = pack(block_expert, member, tokens, experts_each, shifts, chips)
     pairs = [(d, d ^ 1) for d in range(replicas)]
     arrived, gathered = [], []
-    weights = bring(outgoing[0], gate_weight, up_weight)
+    weights = (gate_weight, up_weight)
 
     def swap_rows(g):
-        rows = hidden_rows(arrived[EDGES[g] : EDGES[g + 1]], *weights)
+        rows = hidden_rows(arrived[EDGES[g] : EDGES[g + 1]], *weights, fetch=g == 0)
         gathered.append([rows, lax.ppermute(rows, "dp", pairs)])
 
     for (dy, dc), payload in zip(shifts, outgoing):
@@ -357,6 +378,7 @@
         ]
         if dy == 2 and not gathered:
             swap_rows(0)
+            weights = bring(gathered[0][0], gate_weight, up_weight)
         if dy == 2:
             payload, _ = lax.optimization_barrier((payload, gathered[0][0]))
         arrived.append(payload if dy == dc == 0 else lax.ppermute(payload, "expert", route))

time: 92.1 us -> 93.7 us (1.017)
  Pallas kernels: 20.4 us -> 22.5 us
  starting transfers between devices: 20.2 us -> 19 us
    pallas_call x5, Pallas kernels: 1.51 us -> 3.6 us  [hidden_rows(): pl.pallas_call(lambda *refs: hidden_kernel(*refs, slots=slots, model_widt...]
    ppermute x5, waiting for transfers between devices: 4.33 us -> 6.06 us  [swap_rows(): gathered.append([rows, lax.ppermute(rows, 'dp', pairs)])]
    ppermute x7, starting transfers between devices: 9.75 us -> 8.02 us  [on_device(): lax.ppermute(payload, 'expert', route)]
  transfers between devices with their start and end apart: 13 -> 13, of which waited for: 5 -> 6; matrix products, arithmetic and copies ran while one was open for 0% -> 0% of each run, Pallas kernels for 15% -> 17%
where the time goes in v5:
time: 93.7 us; the launch traced here: 93.5 us
  blocking collectives  40.2 us (43%)
  Pallas kernels  22.5 us (24%)
  starting transfers between devices  19 us (20%)
  waiting for transfers between devices  10.9 us (12%)
    all_to_all x1, blocking collectives, on_device(): lax.all_to_all(partial_gram, 'dp', split_axis=0, concat_axis=0, axis_inde...  26.3 us
    all_to_all x1, blocking collectives, on_device(): lax.all_to_all(sent, 'dp', split_axis=0, concat_axis=0, tiled=True)  14 us
    ppermute x5, starting transfers between devices, swap_rows(): gathered.append([rows, lax.ppermute(rows, 'dp', pairs)])  9.48 us
    ppermute x7, starting transfers between devices, on_device(): lax.ppermute(payload, 'expert', route)  8.02 us
    pallas_call x1, Pallas kernels, first_panels(): pl.pallas_call(lambda *refs: first_kernel(*refs, scale=scale), out_shape=...  6.85 us
    ppermute x5, waiting for transfers between devices, swap_rows(): gathered.append([rows, lax.ppermute(rows, 'dp', pairs)])  6.06 us
    ppermute x7, waiting for transfers between devices, on_device(): lax.ppermute(payload, 'expert', route)  4.8 us
    pallas_call x1, Pallas kernels, bring(): pl.pallas_call(bring_kernel, in_specs=[pl.BlockSpec(memory_space=pl.ANY)]...  4.62 us
  transfers between devices with their start and end apart: 13, of which 6 were waited for; matrix products, arithmetic and copies ran while one was open for 0% of the time, Pallas kernels for 17%

profile of v5, /device:TPU:0, one launch (start us, length us, event | category | flops | bytes accessed | tf_op | source)
XLA Modules:
  0.0 93.5 jit_solution(17446161986344543297)
XLA Ops:
  0.0 1.7 %pack.1 = (bf16[1040,128]{1,0:T(8,128)(2,1)S(1)}, bf16[1040,128]{1,0:T(8,128)(2,1)S(1)}, bf16[1040,128]{1,0:T(8,128)(2,1)S(1)}, bf16[1040,128]{1,0:T(8,128)(2,1)...) custom-call(s32[1]{0:T(128)} %bitcast.1.refs_0_, ...), custom_call_target="tpu_custom_call" | custom-call | tf_op jit(solution)/shard_map/pack/pallas_call | solution.py:71
  1.7 0.1 collective-permute-start
  1.8 1.8 %collective-permute-start.6 = (bf16[1040,128]{1,0:T(8,128)(2,1)S(1)}, bf16[1040,128]{1,0:T(8,128)(2,1)S(1)}, u32[]{:S(2)}, u32[]{:S(2)}) collective-permute-start(bf16[1040,128]{1,0:T(8,128)(2,1)S(1)} %get-tuple-element.27), channel_id=1, source_target_pairs={{0,2},{1,3},{2,4},{3,5},{4,6},{5,7},{6,0},{7,1},{8,10},{9,11},{10,... | collective-permute-start | bytes 798728 | tf_op jit(solution)/shard_map/ppermute | solution.py:384
  3.5 1.5 %collective-permute-start.7 = (bf16[1040,128]{1,0:T(8,128)(2,1)S(1)}, bf16[1040,128]{1,0:T(8,128)(2,1)S(1)}, u32[]{:S(2)}, u32[]{:S(2)}) collective-permute-start(bf16[1040,128]{1,0:T(8,128)(2,1)S(1)} %get-tuple-element.28), channel_id=1, source_target_pairs={{0,6},{1,7},{2,0},{3,1},{4,2},{5,3},{6,4},{7,5},{8,14},{9,15},{10,... | collective-permute-start | bytes 798728 | tf_op jit(solution)/shard_map/ppermute | solution.py:384
  5.1 3.0 %collective-permute-start.10 = (bf16[1040,128]{1,0:T(8,128)(2,1)S(1)}, bf16[1040,128]{1,0:T(8,128)(2,1)S(1)}, u32[]{:S(2)}, u32[]{:S(2)}) collective-permute-start(bf16[1040,128]{1,0:T(8,128)(2,1)S(1)} %get-tuple-element.30), channel_id=1, source_target_pairs={{0,7},{1,6},{2,1},{3,0},{4,3},{5,2},{6,5},{7,4},{8,15},{9,14},{10,... | collective-permute-start | bytes 798728 | tf_op jit(solution)/shard_map/ppermute | solution.py:384
  8.0 2.2 %hidden.5._.refs_1_ = bf16[272,384]{1,0:T(8,128)(2,1)S(1)} custom-call(bf16[1040,128]{1,0:T(8,128)(2,1)S(1)} %get-tuple-element.20.refs_0_, bf16[1040,128]{1,0:T(8,128)(2,1)S(1)} %collective-permute-done.refs_1_, bf16[8,1024,384]{2,1,0:T(8,128)(2,1)} %gate_ref.1, bf16[8,1024,384]{2,1,0:T(8,128)(2,1)} %up_ref.1), custom_call_target="tpu_custom_call" | custom-call | tf_op jit(solution)/shard_map/hidden/pallas_call | solution.py:138
  10.2 0.8 collective-permute-start.1
  11.0 1.3 %collective-permute-done.6.refs_0_ = bf16[1040,128]{1,0:T(8,128)(2,1)S(1)} collective-permute-done((bf16[1040,128]{1,0:T(8,128)(2,1)S(1)}, bf16[1040,128]{1,0:T(8,128)(2,1)S(1)}, u32[]{:S(2)}, u32[]{:S(2)}) %collective-permute-start.6) | collective-permute-done | bytes 266272 | tf_op jit(solution)/shard_map/ppermute | solution.py:384
  12.3 0.9 collective-permute-start.3
  13.2 4.6 %bring.1 = (bf16[8,1024,384]{2,1,0:T(8,128)(2,1)S(1)}, bf16[8,1024,384]{2,1,0:T(8,128)(2,1)S(1)}) custom-call(bf16[272,384]{1,0:T(8,128)(2,1)S(1)} %hidden.5._.refs_1_, bf16[8,1024,384]{2,1,0:T(8,128)(2,1)} %gate_ref.1, bf16[8,1024,384]{2,1,0:T(8,128)(2,1)} %up_ref.1), custom_call_target="tpu_custom_call" | custom-call | tf_op jit(solution)/shard_map/bring/pallas_call | solution.py:162
  17.9 2.0 %collective-permute-start.5 = (bf16[272,384]{1,0:T(8,128)(2,1)S(1)}, bf16[272,384]{1,0:T(8,128)(2,1)S(1)}, u32[]{:S(2)}, u32[]{:S(2)}) collective-permute-start(bf16[272,384]{1,0:T(8,128)(2,1)S(1)} %hidden.5._.refs_1_), channel_id=1, source_target_pairs={{0,8},{8,0},{16,24},{24,16},{32,40},{40,32},{48,56},{56,48},{64,72... | collective-permute-start | bytes 626696 | tf_op jit(solution)/shard_map/ppermute | solution.py:371
  19.9 0.6 hidden.8.refs_3_
  20.4 0.6 collective-permute-start.8
  21.1 0.1 hidden.9.refs_5_
  21.2 2.4 %collective-permute-start.11 = (bf16[272,384]{1,0:T(8,128)(2,1)S(1)}, bf16[272,384]{1,0:T(8,128)(2,1)S(1)}, u32[]{:S(2)}, u32[]{:S(2)}) collective-permute-start(bf16[272,384]{1,0:T(8,128)(2,1)S(1)} %hidden.9.refs_5_), channel_id=1, source_target_pairs={{0,8},{8,0},{16,24},{24,16},{32,40},{40,32},{48,56},{56,48},{64,72... | collective-permute-start | bytes 626696 | tf_op jit(solution)/shard_map/ppermute | solution.py:371
  23.6 1.4 %collective-permute-done.1.refs_0_ = bf16[1040,128]{1,0:T(8,128)(2,1)S(1)} collective-permute-done((bf16[1040,128]{1,0:T(8,128)(2,1)S(1)}, bf16[1040,128]{1,0:T(8,128)(2,1)S(1)}, u32[]{:S(2)}, u32[]{:S(2)}) %collective-permute-start.1) | collective-permute-done | bytes 266272 | tf_op jit(solution)/shard_map/ppermute | solution.py:384
  25.1 0.1 hidden.6.refs_1_
  25.2 2.4 %collective-permute-start.2 = (bf16[144,384]{1,0:T(8,128)(2,1)S(1)}, bf16[144,384]{1,0:T(8,128)(2,1)S(1)}, u32[]{:S(2)}, u32[]{:S(2)}) collective-permute-start(bf16[144,384]{1,0:T(8,128)(2,1)S(1)} %hidden.6.refs_1_), channel_id=1, source_target_pairs={{0,8},{8,0},{16,24},{24,16},{32,40},{40,32},{48,56},{56,48},{64,72... | collective-permute-start | bytes 331784 | tf_op jit(solution)/shard_map/ppermute | solution.py:371
  27.6 2.1 %collective-permute-done.3.refs_0_ = bf16[1040,128]{1,0:T(8,128)(2,1)S(1)} collective-permute-done((bf16[1040,128]{1,0:T(8,128)(2,1)S(1)}, bf16[1040,128]{1,0:T(8,128)(2,1)S(1)}, u32[]{:S(2)}, u32[]{:S(2)}) %collective-permute-start.3) | collective-permute-done | bytes 266272 | tf_op jit(solution)/shard_map/ppermute | solution.py:384
  29.7 0.6 hidden.7.refs_3_
  30.3 2.0 %collective-permute-start.4 = (bf16[144,384]{1,0:T(8,128)(2,1)S(1)}, bf16[144,384]{1,0:T(8,128)(2,1)S(1)}, u32[]{:S(2)}, u32[]{:S(2)}) collective-permute-start(bf16[144,384]{1,0:T(8,128)(2,1)S(1)} %hidden.7.refs_3_), channel_id=1, source_target_pairs={{0,8},{8,0},{16,24},{24,16},{32,40},{40,32},{48,56},{56,48},{64,72... | collective-permute-start | bytes 331784 | tf_op jit(solution)/shard_map/ppermute | solution.py:371
  32.3 2.2 %collective-permute-done.11.refs_6_ = bf16[272,384]{1,0:T(8,128)(2,1)S(1)} collective-permute-done((bf16[272,384]{1,0:T(8,128)(2,1)S(1)}, bf16[272,384]{1,0:T(8,128)(2,1)S(1)}, u32[]{:S(2)}, u32[]{:S(2)}) %collective-permute-start.11) | collective-permute-done | bytes 208928 | tf_op jit(solution)/shard_map/ppermute | solution.py:371
  34.4 0.8 gram.2.refs_5_
  35.3 1.5 %collective-permute-done.2.refs_2_ = bf16[144,384]{1,0:T(8,128)(2,1)S(1)} collective-permute-done((bf16[144,384]{1,0:T(8,128)(2,1)S(1)}, bf16[144,384]{1,0:T(8,128)(2,1)S(1)}, u32[]{:S(2)}, u32[]{:S(2)}) %collective-permute-start.2) | collective-permute-done | bytes 110624 | tf_op jit(solution)/shard_map/ppermute | solution.py:371
  36.8 2.4 %collective-permute-done.4.refs_4_ = bf16[144,384]{1,0:T(8,128)(2,1)S(1)} collective-permute-done((bf16[144,384]{1,0:T(8,128)(2,1)S(1)}, bf16[144,384]{1,0:T(8,128)(2,1)S(1)}, u32[]{:S(2)}, u32[]{:S(2)}) %collective-permute-start.4) | collective-permute-done | bytes 110624 | tf_op jit(solution)/shard_map/ppermute | solution.py:371
  39.2 0.8 gram.3
  39.9 26.3 %all_to_all.10 = f32[8,296,128]{2,1,0:T(8,128)S(1)} all-to-all(f32[8,296,128]{2,1,0:T(8,128)S(1)} %gram.3), channel_id=1, replica_groups={{0,32,64,96,16,48,80,112},{8,40,72,104,24,56,88,120},{1,33,65,97,17,49,..., dimensions={0} | all-to-all | bytes 2424832 | tf_op jit(solution)/shard_map/all_to_all | solution.py:394
  66.3 1.5 %collective-permute-start.12 = (f32[288,128]{1,0:T(8,128)S(1)}, f32[288,128]{1,0:T(8,128)S(1)}, u32[]{:S(2)}, u32[]{:S(2)}) collective-permute-start(f32[288,128]{1,0:T(8,128)S(1)} %slice.8), channel_id=1, source_target_pairs={{32,0},{40,8},{48,16},{56,24},{96,64},{104,72},{112,80},{120,88},{... | collective-permute-start | bytes 442376 | tf_op jit(solution)/shard_map/ppermute | solution.py:399
  67.8 6.8 %first_panels.1 = (f32[128,384]{1,0:T(8,128)S(1)}, f32[128,256]{1,0:T(8,128)S(1)}) custom-call(f32[296,128]{1,0:T(8,128)S(1)} %reduce_sum.9.refs_0_), custom_call_target="tpu_custom_call" | custom-call | tf_op jit(solution)/shard_map/first_panels/pallas_call | solution.py:316
  74.6 4.2 %last_panel.1 = bf16[384,384]{1,0:T(8,128)(2,1)S(1)} custom-call(f32[296,128]{1,0:T(8,128)S(1)} %reduce_sum.9.refs_0_, f32[288,128]{1,0:T(8,128)S(1)} %collective-permute-done.12.refs_1_, f32[128,384]{1,0:T(8,128)S(1)} %get-tuple-element.31.refs_2_, f32[128,256]{1,0:T(8,128)S(1)} %get-tuple-element.32.refs_3_), custom_call_target="tpu_custom_call" | custom-call | tf_op jit(solution)/shard_map/last_panel/pallas_call | solution.py:347
  78.8 14.0 %all_to_all.11 = bf16[16,24,384]{2,1,0:T(8,128)(2,1)S(1)} all-to-all(bf16[16,24,384]{2,1,0:T(8,128)(2,1)S(1)} %bitcast.12), channel_id=1, replica_groups=mesh['dp'=16,'expert'=8] {'dp'}, dimensions={0} | all-to-all | bytes 589824 | tf_op jit(solution)/shard_map/all_to_all | solution.py:405
  92.8 0.7 fusion
  (10 shorter events, 0.1 us)
Async XLA Ops:
  1.7 6.4 %collective-permute-start = (bf16[1040,128]{1,0:T(8,128)(2,1)S(1)}, bf16[1040,128]{1,0:T(8,128)(2,1)S(1)}, u32[]{:S(2)}, u32[]{:S(2)}) collective-permute-start(bf16[1040,128]{1,0:T(8,128)(2,1)S(1)} %get-tuple-element.21), channel_id=1, source_target_pairs={{0,1},{1,0},{2,3},{3,2},{4,5},{5,4},{6,7},{7,6},{8,9},{9,8},{10,11... | collective-permute-start | bytes 798728 | tf_op jit(solution)/shard_map/ppermute | solution.py:384
  1.8 10.5 %collective-permute-start.6 = (bf16[1040,128]{1,0:T(8,128)(2,1)S(1)}, bf16[1040,128]{1,0:T(8,128)(2,1)S(1)}, u32[]{:S(2)}, u32[]{:S(2)}) collective-permute-start(bf16[1040,128]{1,0:T(8,128)(2,1)S(1)} %get-tuple-element.27), channel_id=1, source_target_pairs={{0,2},{1,3},{2,4},{3,5},{4,6},{5,7},{6,0},{7,1},{8,10},{9,11},{10,... | collective-permute-start | bytes 798728 | tf_op jit(solution)/shard_map/ppermute | solution.py:384
  3.5 14.3 %collective-permute-start.7 = (bf16[1040,128]{1,0:T(8,128)(2,1)S(1)}, bf16[1040,128]{1,0:T(8,128)(2,1)S(1)}, u32[]{:S(2)}, u32[]{:S(2)}) collective-permute-start(bf16[1040,128]{1,0:T(8,128)(2,1)S(1)} %get-tuple-element.28), channel_id=1, source_target_pairs={{0,6},{1,7},{2,0},{3,1},{4,2},{5,3},{6,4},{7,5},{8,14},{9,15},{10,... | collective-permute-start | bytes 798728 | tf_op jit(solution)/shard_map/ppermute | solution.py:384
  5.1 15.4 %collective-permute-start.9 = (bf16[1040,128]{1,0:T(8,128)(2,1)S(1)}, bf16[1040,128]{1,0:T(8,128)(2,1)S(1)}, u32[]{:S(2)}, u32[]{:S(2)}) collective-permute-start(bf16[1040,128]{1,0:T(8,128)(2,1)S(1)} %get-tuple-element.29), channel_id=1, source_target_pairs={{0,3},{1,2},{2,5},{3,4},{4,7},{5,6},{6,1},{7,0},{8,11},{9,10},{10,... | collective-permute-start | bytes 798728 | tf_op jit(solution)/shard_map/ppermute | solution.py:384
  5.1 16.0 %collective-permute-start.10 = (bf16[1040,128]{1,0:T(8,128)(2,1)S(1)}, bf16[1040,128]{1,0:T(8,128)(2,1)S(1)}, u32[]{:S(2)}, u32[]{:S(2)}) collective-permute-start(bf16[1040,128]{1,0:T(8,128)(2,1)S(1)} %get-tuple-element.30), channel_id=1, source_target_pairs={{0,7},{1,6},{2,1},{3,0},{4,3},{5,2},{6,5},{7,4},{8,15},{9,14},{10,... | collective-permute-start | bytes 798728 | tf_op jit(solution)/shard_map/ppermute | solution.py:384
  10.2 14.8 %collective-permute-start.1 = (bf16[1040,128]{1,0:T(8,128)(2,1)S(1)}, bf16[1040,128]{1,0:T(8,128)(2,1)S(1)}, u32[]{:S(2)}, u32[]{:S(2)}) collective-permute-start(bf16[1040,128]{1,0:T(8,128)(2,1)S(1)} %get-tuple-element.22), channel_id=1, source_target_pairs={{0,4},{1,5},{2,6},{3,7},{4,0},{5,1},{6,2},{7,3},{8,12},{9,13},{10,... | collective-permute-start | bytes 798728 | tf_op jit(solution)/shard_map/ppermute | solution.py:384
  12.3 17.4 %collective-permute-start.3 = (bf16[1040,128]{1,0:T(8,128)(2,1)S(1)}, bf16[1040,128]{1,0:T(8,128)(2,1)S(1)}, u32[]{:S(2)}, u32[]{:S(2)}) collective-permute-start(bf16[1040,128]{1,0:T(8,128)(2,1)S(1)} %get-tuple-element.26), channel_id=1, source_target_pairs={{0,5},{1,4},{2,7},{3,6},{4,1},{5,0},{6,3},{7,2},{8,13},{9,12},{10,... | collective-permute-start | bytes 798728 | tf_op jit(solution)/shard_map/ppermute | solution.py:384
  17.9 14.4 %collective-permute-start.5 = (bf16[272,384]{1,0:T(8,128)(2,1)S(1)}, bf16[272,384]{1,0:T(8,128)(2,1)S(1)}, u32[]{:S(2)}, u32[]{:S(2)}) collective-permute-start(bf16[272,384]{1,0:T(8,128)(2,1)S(1)} %hidden.5._.refs_1_), channel_id=1, source_target_pairs={{0,8},{8,0},{16,24},{24,16},{32,40},{40,32},{48,56},{56,48},{64,72... | collective-permute-start | bytes 626696 | tf_op jit(solution)/shard_map/ppermute | solution.py:371
  20.4 11.8 %collective-permute-start.8 = (bf16[272,384]{1,0:T(8,128)(2,1)S(1)}, bf16[272,384]{1,0:T(8,128)(2,1)S(1)}, u32[]{:S(2)}, u32[]{:S(2)}) collective-permute-start(bf16[272,384]{1,0:T(8,128)(2,1)S(1)} %hidden.8.refs_3_), channel_id=1, source_target_pairs={{0,8},{8,0},{16,24},{24,16},{32,40},{40,32},{48,56},{56,48},{64,72... | collective-permute-start | bytes 626696 | tf_op jit(solution)/shard_map/ppermute | solution.py:371
  21.2 13.2 %collective-permute-start.11 = (bf16[272,384]{1,0:T(8,128)(2,1)S(1)}, bf16[272,384]{1,0:T(8,128)(2,1)S(1)}, u32[]{:S(2)}, u32[]{:S(2)}) collective-permute-start(bf16[272,384]{1,0:T(8,128)(2,1)S(1)} %hidden.9.refs_5_), channel_id=1, source_target_pairs={{0,8},{8,0},{16,24},{24,16},{32,40},{40,32},{48,56},{56,48},{64,72... | collective-permute-start | bytes 626696 | tf_op jit(solution)/shard_map/ppermute | solution.py:371
  25.2 11.6 %collective-permute-start.2 = (bf16[144,384]{1,0:T(8,128)(2,1)S(1)}, bf16[144,384]{1,0:T(8,128)(2,1)S(1)}, u32[]{:S(2)}, u32[]{:S(2)}) collective-permute-start(bf16[144,384]{1,0:T(8,128)(2,1)S(1)} %hidden.6.refs_1_), channel_id=1, source_target_pairs={{0,8},{8,0},{16,24},{24,16},{32,40},{40,32},{48,56},{56,48},{64,72... | collective-permute-start | bytes 331784 | tf_op jit(solution)/shard_map/ppermute | solution.py:371
  30.3 8.9 %collective-permute-start.4 = (bf16[144,384]{1,0:T(8,128)(2,1)S(1)}, bf16[144,384]{1,0:T(8,128)(2,1)S(1)}, u32[]{:S(2)}, u32[]{:S(2)}) collective-permute-start(bf16[144,384]{1,0:T(8,128)(2,1)S(1)} %hidden.7.refs_3_), channel_id=1, source_target_pairs={{0,8},{8,0},{16,24},{24,16},{32,40},{40,32},{48,56},{56,48},{64,72... | collective-permute-start | bytes 331784 | tf_op jit(solution)/shard_map/ppermute | solution.py:371
  66.3 8.3 %collective-permute-start.12 = (f32[288,128]{1,0:T(8,128)S(1)}, f32[288,128]{1,0:T(8,128)S(1)}, u32[]{:S(2)}, u32[]{:S(2)}) collective-permute-start(f32[288,128]{1,0:T(8,128)S(1)} %slice.8), channel_id=1, source_target_pairs={{32,0},{40,8},{48,16},{56,24},{96,64},{104,72},{112,80},{120,88},{... | collective-permute-start | bytes 442376 | tf_op jit(solution)/shard_map/ppermute | solution.py:399

commit v6 on v5

--- a/solution.py
+++ b/solution.py
@@ -362,7 +362,8 @@
     shifts += [(2, 0), (2, 1)]
     member = lax.axis_index("expert").reshape(1)
     outgoing = pack(block_expert, member, tokens, experts_each, shifts, chips)
-    pairs = [(d, d ^ 1) for d in range(replicas)]
+    side = replicas // SIDE
+    pairs = [(x * SIDE + z, (side - 1 - x) * SIDE + z) for x in range(side) for z in range(SIDE)]
     arrived, gathered = [], []
     weights = (gate_weight, up_weight)
 
@@ -385,12 +386,13 @@
     for g in range(1, len(EDGES) - 1):
         swap_rows(g)
     kept = experts_each // 2
-    first = (lax.axis_index("dp") % 2 * kept).reshape(1)
+    first = (lax.axis_index("dp") // (replicas // 2) * kept).reshape(1)
     partial_gram = gram(first, kept, [rows for pair in gathered[:-2] for rows in pair])
     tail = [rows for pair in gathered[-2:] for rows in pair]
     partial_gram = gram(first, kept, tail, (partial_gram,))
-    side = replicas // SIDE
-    classes = [[x * SIDE + z for z in range(p, SIDE, 2) for x in range(side)] for p in range(2)]
+    classes = [
+        [x * SIDE + z for z in range(SIDE) for x in (2 * p, 2 * p + 1)] for p in range(2)
+    ]
     pieces = lax.all_to_all(
         partial_gram, "dp", split_axis=0, concat_axis=0, axis_index_groups=classes, tiled=True
     )
@@ -403,8 +405,7 @@
     row_count = hidden_width // replicas
     sent = result.reshape(replicas, row_count, hidden_width)
     returned = lax.all_to_all(sent, "dp", split_axis=0, concat_axis=0, tiled=True)
-    returned = returned.reshape(2, 2, 2, 2, row_count, hidden_width)[:, 0]
-    returned = jnp.transpose(returned, (2, 1, 0, 3, 4))
+    returned = returned.reshape(2, 2, SIDE, row_count, hidden_width)[:, 0]
     returned = returned.reshape(experts_each, row_count, hidden_width)
     return returned.astype(F32)
 

time: 93.7 us -> 93.3 us (level)
  starting transfers between devices: 19 us -> 21.6 us
  blocking collectives: 40.2 us -> 38.4 us
  waiting for transfers between devices: 10.9 us -> 9.29 us
    all_to_all x1, blocking collectives: 26.3 us -> 23.3 us  [on_device(): lax.all_to_all(partial_gram, 'dp', split_axis=0, concat_axis=0, axis_inde...]
    ppermute x5, starting transfers between devices: 9.48 us -> 12.1 us  [swap_rows(): gathered.append([rows, lax.ppermute(rows, 'dp', pairs)])]
    ppermute x7, waiting for transfers between devices: 4.8 us -> 2.54 us  [on_device(): lax.ppermute(payload, 'expert', route)]
    all_to_all x1, blocking collectives: 14 us -> 15.1 us  [on_device(): lax.all_to_all(sent, 'dp', split_axis=0, concat_axis=0, tiled=True)]
  transfers between devices with their start and end apart: 13 -> 13, of which waited for: 6 -> 5; matrix products, arithmetic and copies ran while one was open for 0% -> 0% of each run, Pallas kernels for 17% -> 17%
where the time goes in v6:
time: 93.3 us; the launch traced here: 93.1 us
  blocking collectives  38.4 us (41%)
  Pallas kernels  22.8 us (24%)
  starting transfers between devices  21.6 us (23%)
  waiting for transfers between devices  9.29 us (10%)
    all_to_all x1, blocking collectives, on_device(): lax.all_to_all(partial_gram, 'dp', split_axis=0, concat_axis=0, axis_inde...  23.3 us
    all_to_all x1, blocking collectives, on_device(): lax.all_to_all(sent, 'dp', split_axis=0, concat_axis=0, tiled=True)  15.1 us
    ppermute x5, starting transfers between devices, swap_rows(): gathered.append([rows, lax.ppermute(rows, 'dp', pairs)])  12.1 us
    ppermute x7, starting transfers between devices, on_device(): lax.ppermute(payload, 'expert', route)  8.02 us
    pallas_call x1, Pallas kernels, first_panels(): pl.pallas_call(lambda *refs: first_kernel(*refs, scale=scale), out_shape=...  6.85 us
    ppermute x5, waiting for transfers between devices, swap_rows(): gathered.append([rows, lax.ppermute(rows, 'dp', pairs)])  6.74 us
    pallas_call x1, Pallas kernels, bring(): pl.pallas_call(bring_kernel, in_specs=[pl.BlockSpec(memory_space=pl.ANY)]...  4.62 us
    pallas_call x1, Pallas kernels, last_panel(): pl.pallas_call(lambda *refs: last_kernel(*refs, scale=scale), out_shape=p...  4.17 us
  transfers between devices with their start and end apart: 13, of which 5 were waited for; matrix products, arithmetic and copies ran while one was open for 0% of the time, Pallas kernels for 17%

profile of v6, /device:TPU:0, one launch (start us, length us, event | category | flops | bytes accessed | tf_op | source)
XLA Modules:
  0.0 93.1 jit_solution(10251978306263321346)
XLA Ops:
  0.0 1.7 %pack.1 = (bf16[1040,128]{1,0:T(8,128)(2,1)S(1)}, bf16[1040,128]{1,0:T(8,128)(2,1)S(1)}, bf16[1040,128]{1,0:T(8,128)(2,1)S(1)}, bf16[1040,128]{1,0:T(8,128)(2,1)...) custom-call(s32[1]{0:T(128)} %bitcast.1.refs_0_, ...), custom_call_target="tpu_custom_call" | custom-call | tf_op jit(solution)/shard_map/pack/pallas_call | solution.py:71
  1.7 0.1 collective-permute-start
  1.8 1.8 %collective-permute-start.6 = (bf16[1040,128]{1,0:T(8,128)(2,1)S(1)}, bf16[1040,128]{1,0:T(8,128)(2,1)S(1)}, u32[]{:S(2)}, u32[]{:S(2)}) collective-permute-start(bf16[1040,128]{1,0:T(8,128)(2,1)S(1)} %get-tuple-element.27), channel_id=1, source_target_pairs={{0,2},{1,3},{2,4},{3,5},{4,6},{5,7},{6,0},{7,1},{8,10},{9,11},{10,... | collective-permute-start | bytes 798728 | tf_op jit(solution)/shard_map/ppermute | solution.py:385
  3.5 1.5 %collective-permute-start.7 = (bf16[1040,128]{1,0:T(8,128)(2,1)S(1)}, bf16[1040,128]{1,0:T(8,128)(2,1)S(1)}, u32[]{:S(2)}, u32[]{:S(2)}) collective-permute-start(bf16[1040,128]{1,0:T(8,128)(2,1)S(1)} %get-tuple-element.28), channel_id=1, source_target_pairs={{0,6},{1,7},{2,0},{3,1},{4,2},{5,3},{6,4},{7,5},{8,14},{9,15},{10,... | collective-permute-start | bytes 798728 | tf_op jit(solution)/shard_map/ppermute | solution.py:385
  5.1 3.0 %collective-permute-start.10 = (bf16[1040,128]{1,0:T(8,128)(2,1)S(1)}, bf16[1040,128]{1,0:T(8,128)(2,1)S(1)}, u32[]{:S(2)}, u32[]{:S(2)}) collective-permute-start(bf16[1040,128]{1,0:T(8,128)(2,1)S(1)} %get-tuple-element.30), channel_id=1, source_target_pairs={{0,7},{1,6},{2,1},{3,0},{4,3},{5,2},{6,5},{7,4},{8,15},{9,14},{10,... | collective-permute-start | bytes 798728 | tf_op jit(solution)/shard_map/ppermute | solution.py:385
  8.0 2.2 %hidden.5._.refs_1_ = bf16[272,384]{1,0:T(8,128)(2,1)S(1)} custom-call(bf16[1040,128]{1,0:T(8,128)(2,1)S(1)} %get-tuple-element.20.refs_0_, bf16[1040,128]{1,0:T(8,128)(2,1)S(1)} %collective-permute-done.refs_1_, bf16[8,1024,384]{2,1,0:T(8,128)(2,1)} %gate_ref.1, bf16[8,1024,384]{2,1,0:T(8,128)(2,1)} %up_ref.1), custom_call_target="tpu_custom_call" | custom-call | tf_op jit(solution)/shard_map/hidden/pallas_call | solution.py:138
  10.2 0.8 collective-permute-start.1
  11.0 1.3 %collective-permute-done.6.refs_0_ = bf16[1040,128]{1,0:T(8,128)(2,1)S(1)} collective-permute-done((bf16[1040,128]{1,0:T(8,128)(2,1)S(1)}, bf16[1040,128]{1,0:T(8,128)(2,1)S(1)}, u32[]{:S(2)}, u32[]{:S(2)}) %collective-permute-start.6) | collective-permute-done | bytes 266272 | tf_op jit(solution)/shard_map/ppermute | solution.py:385
  12.3 0.9 collective-permute-start.3
  13.2 4.6 %bring.1 = (bf16[8,1024,384]{2,1,0:T(8,128)(2,1)S(1)}, bf16[8,1024,384]{2,1,0:T(8,128)(2,1)S(1)}) custom-call(bf16[272,384]{1,0:T(8,128)(2,1)S(1)} %hidden.5._.refs_1_, bf16[8,1024,384]{2,1,0:T(8,128)(2,1)} %gate_ref.1, bf16[8,1024,384]{2,1,0:T(8,128)(2,1)} %up_ref.1), custom_call_target="tpu_custom_call" | custom-call | tf_op jit(solution)/shard_map/bring/pallas_call | solution.py:162
  17.9 3.1 %collective-permute-start.5 = (bf16[272,384]{1,0:T(8,128)(2,1)S(1)}, bf16[272,384]{1,0:T(8,128)(2,1)S(1)}, u32[]{:S(2)}, u32[]{:S(2)}) collective-permute-start(bf16[272,384]{1,0:T(8,128)(2,1)S(1)} %hidden.5._.refs_1_), channel_id=1, source_target_pairs={{0,96},{8,104},{16,112},{24,120},{32,64},{40,72},{48,80},{56,88},{... | collective-permute-start | bytes 626696 | tf_op jit(solution)/shard_map/ppermute | solution.py:372
  20.9 0.6 hidden.8.refs_3_
  21.5 0.1 collective-permute-start.8
  21.6 0.1 hidden.9.refs_5_
  21.7 4.2 %collective-permute-start.11 = (bf16[272,384]{1,0:T(8,128)(2,1)S(1)}, bf16[272,384]{1,0:T(8,128)(2,1)S(1)}, u32[]{:S(2)}, u32[]{:S(2)}) collective-permute-start(bf16[272,384]{1,0:T(8,128)(2,1)S(1)} %hidden.9.refs_5_), channel_id=1, source_target_pairs={{0,96},{8,104},{16,112},{24,120},{32,64},{40,72},{48,80},{56,88},{... | collective-permute-start | bytes 626696 | tf_op jit(solution)/shard_map/ppermute | solution.py:372
  25.9 0.1 hidden.6.refs_1_
  26.1 2.4 %collective-permute-start.2 = (bf16[144,384]{1,0:T(8,128)(2,1)S(1)}, bf16[144,384]{1,0:T(8,128)(2,1)S(1)}, u32[]{:S(2)}, u32[]{:S(2)}) collective-permute-start(bf16[144,384]{1,0:T(8,128)(2,1)S(1)} %hidden.6.refs_1_), channel_id=1, source_target_pairs={{0,96},{8,104},{16,112},{24,120},{32,64},{40,72},{48,80},{56,88},{... | collective-permute-start | bytes 331784 | tf_op jit(solution)/shard_map/ppermute | solution.py:372
  28.5 1.2 %collective-permute-done.3.refs_0_ = bf16[1040,128]{1,0:T(8,128)(2,1)S(1)} collective-permute-done((bf16[1040,128]{1,0:T(8,128)(2,1)S(1)}, bf16[1040,128]{1,0:T(8,128)(2,1)S(1)}, u32[]{:S(2)}, u32[]{:S(2)}) %collective-permute-start.3) | collective-permute-done | bytes 266272 | tf_op jit(solution)/shard_map/ppermute | solution.py:385
  29.7 0.6 hidden.7.refs_3_
  30.3 2.4 %collective-permute-start.4 = (bf16[144,384]{1,0:T(8,128)(2,1)S(1)}, bf16[144,384]{1,0:T(8,128)(2,1)S(1)}, u32[]{:S(2)}, u32[]{:S(2)}) collective-permute-start(bf16[144,384]{1,0:T(8,128)(2,1)S(1)} %hidden.7.refs_3_), channel_id=1, source_target_pairs={{0,96},{8,104},{16,112},{24,120},{32,64},{40,72},{48,80},{56,88},{... | collective-permute-start | bytes 331784 | tf_op jit(solution)/shard_map/ppermute | solution.py:372
  32.7 3.2 %collective-permute-done.11.refs_6_ = bf16[272,384]{1,0:T(8,128)(2,1)S(1)} collective-permute-done((bf16[272,384]{1,0:T(8,128)(2,1)S(1)}, bf16[272,384]{1,0:T(8,128)(2,1)S(1)}, u32[]{:S(2)}, u32[]{:S(2)}) %collective-permute-start.11) | collective-permute-done | bytes 208928 | tf_op jit(solution)/shard_map/ppermute | solution.py:372
  35.8 1.1 %gram.2.refs_5_ = f32[8,296,128]{2,1,0:T(8,128)S(1)} custom-call(s32[1]{0:T(128)} %bitcast.refs_0_, bf16[272,384]{1,0:T(8,128)(2,1)S(1)} %hidden.5._.refs_1_, bf16[272,384]{1,0:T(8,128)(2,1)S(1)} %collective-permute-done.5.refs_2_, bf16[272,384]{1,0:T(8,128)(2,1)S(1)} %hidden.8.refs_3_, bf16[272,384]{1,0:T(8,128)(2,1)S(1)} %collective-permute-done.8.refs_4_, ...), custom_call_target="tpu_custom_call" | custom-call | tf_op jit(solution)/shard_map/gram/pallas_call | solution.py:231
  37.0 1.2 %collective-permute-done.2.refs_2_ = bf16[144,384]{1,0:T(8,128)(2,1)S(1)} collective-permute-done((bf16[144,384]{1,0:T(8,128)(2,1)S(1)}, bf16[144,384]{1,0:T(8,128)(2,1)S(1)}, u32[]{:S(2)}, u32[]{:S(2)}) %collective-permute-start.2) | collective-permute-done | bytes 110624 | tf_op jit(solution)/shard_map/ppermute | solution.py:372
  38.2 2.4 %collective-permute-done.4.refs_4_ = bf16[144,384]{1,0:T(8,128)(2,1)S(1)} collective-permute-done((bf16[144,384]{1,0:T(8,128)(2,1)S(1)}, bf16[144,384]{1,0:T(8,128)(2,1)S(1)}, u32[]{:S(2)}, u32[]{:S(2)}) %collective-permute-start.4) | collective-permute-done | bytes 110624 | tf_op jit(solution)/shard_map/ppermute | solution.py:372
  40.6 0.8 gram.3
  41.3 23.3 %all_to_all.10 = f32[8,296,128]{2,1,0:T(8,128)S(1)} all-to-all(f32[8,296,128]{2,1,0:T(8,128)S(1)} %gram.3), channel_id=1, replica_groups={{0,32,8,40,16,48,24,56},{64,96,72,104,80,112,88,120},{1,33,9,41,17,49,2..., dimensions={0} | all-to-all | bytes 2424832 | tf_op jit(solution)/shard_map/all_to_all | solution.py:396
  64.6 0.1 reduce_sum.9.refs_0_
  64.7 1.5 %collective-permute-start.12 = (f32[288,128]{1,0:T(8,128)S(1)}, f32[288,128]{1,0:T(8,128)S(1)}, u32[]{:S(2)}, u32[]{:S(2)}) collective-permute-start(f32[288,128]{1,0:T(8,128)S(1)} %slice.8), channel_id=1, source_target_pairs={{32,0},{40,8},{48,16},{56,24},{96,64},{104,72},{112,80},{120,88},{... | collective-permute-start | bytes 442376 | tf_op jit(solution)/shard_map/ppermute | solution.py:401
  66.2 6.9 %first_panels.1 = (f32[128,384]{1,0:T(8,128)S(1)}, f32[128,256]{1,0:T(8,128)S(1)}) custom-call(f32[296,128]{1,0:T(8,128)S(1)} %reduce_sum.9.refs_0_), custom_call_target="tpu_custom_call" | custom-call | tf_op jit(solution)/shard_map/first_panels/pallas_call | solution.py:316
  73.0 4.2 %last_panel.1 = bf16[384,384]{1,0:T(8,128)(2,1)S(1)} custom-call(f32[296,128]{1,0:T(8,128)S(1)} %reduce_sum.9.refs_0_, f32[288,128]{1,0:T(8,128)S(1)} %collective-permute-done.12.refs_1_, f32[128,384]{1,0:T(8,128)S(1)} %get-tuple-element.31.refs_2_, f32[128,256]{1,0:T(8,128)S(1)} %get-tuple-element.32.refs_3_), custom_call_target="tpu_custom_call" | custom-call | tf_op jit(solution)/shard_map/last_panel/pallas_call | solution.py:347
  77.2 15.1 %all_to_all.11 = bf16[16,24,384]{2,1,0:T(8,128)(2,1)S(1)} all-to-all(bf16[16,24,384]{2,1,0:T(8,128)(2,1)S(1)} %bitcast.9), channel_id=1, replica_groups=mesh['dp'=16,'expert'=8] {'dp'}, dimensions={0} | all-to-all | bytes 589824 | tf_op jit(solution)/shard_map/all_to_all | solution.py:407
  92.3 0.8 bitcast_convert_fusion
  (11 shorter events, 0.1 us)
Async XLA Ops:
  1.7 6.4 %collective-permute-start = (bf16[1040,128]{1,0:T(8,128)(2,1)S(1)}, bf16[1040,128]{1,0:T(8,128)(2,1)S(1)}, u32[]{:S(2)}, u32[]{:S(2)}) collective-permute-start(bf16[1040,128]{1,0:T(8,128)(2,1)S(1)} %get-tuple-element.21), channel_id=1, source_target_pairs={{0,1},{1,0},{2,3},{3,2},{4,5},{5,4},{6,7},{7,6},{8,9},{9,8},{10,11... | collective-permute-start | bytes 798728 | tf_op jit(solution)/shard_map/ppermute | solution.py:385
  1.8 10.5 %collective-permute-start.6 = (bf16[1040,128]{1,0:T(8,128)(2,1)S(1)}, bf16[1040,128]{1,0:T(8,128)(2,1)S(1)}, u32[]{:S(2)}, u32[]{:S(2)}) collective-permute-start(bf16[1040,128]{1,0:T(8,128)(2,1)S(1)} %get-tuple-element.27), channel_id=1, source_target_pairs={{0,2},{1,3},{2,4},{3,5},{4,6},{5,7},{6,0},{7,1},{8,10},{9,11},{10,... | collective-permute-start | bytes 798728 | tf_op jit(solution)/shard_map/ppermute | solution.py:385
  3.5 14.3 %collective-permute-start.7 = (bf16[1040,128]{1,0:T(8,128)(2,1)S(1)}, bf16[1040,128]{1,0:T(8,128)(2,1)S(1)}, u32[]{:S(2)}, u32[]{:S(2)}) collective-permute-start(bf16[1040,128]{1,0:T(8,128)(2,1)S(1)} %get-tuple-element.28), channel_id=1, source_target_pairs={{0,6},{1,7},{2,0},{3,1},{4,2},{5,3},{6,4},{7,5},{8,14},{9,15},{10,... | collective-permute-start | bytes 798728 | tf_op jit(solution)/shard_map/ppermute | solution.py:385
  5.1 16.4 %collective-permute-start.9 = (bf16[1040,128]{1,0:T(8,128)(2,1)S(1)}, bf16[1040,128]{1,0:T(8,128)(2,1)S(1)}, u32[]{:S(2)}, u32[]{:S(2)}) collective-permute-start(bf16[1040,128]{1,0:T(8,128)(2,1)S(1)} %get-tuple-element.29), channel_id=1, source_target_pairs={{0,3},{1,2},{2,5},{3,4},{4,7},{5,6},{6,1},{7,0},{8,11},{9,10},{10,... | collective-permute-start | bytes 798728 | tf_op jit(solution)/shard_map/ppermute | solution.py:385
  5.1 16.5 %collective-permute-start.10 = (bf16[1040,128]{1,0:T(8,128)(2,1)S(1)}, bf16[1040,128]{1,0:T(8,128)(2,1)S(1)}, u32[]{:S(2)}, u32[]{:S(2)}) collective-permute-start(bf16[1040,128]{1,0:T(8,128)(2,1)S(1)} %get-tuple-element.30), channel_id=1, source_target_pairs={{0,7},{1,6},{2,1},{3,0},{4,3},{5,2},{6,5},{7,4},{8,15},{9,14},{10,... | collective-permute-start | bytes 798728 | tf_op jit(solution)/shard_map/ppermute | solution.py:385
  10.2 15.7 %collective-permute-start.1 = (bf16[1040,128]{1,0:T(8,128)(2,1)S(1)}, bf16[1040,128]{1,0:T(8,128)(2,1)S(1)}, u32[]{:S(2)}, u32[]{:S(2)}) collective-permute-start(bf16[1040,128]{1,0:T(8,128)(2,1)S(1)} %get-tuple-element.22), channel_id=1, source_target_pairs={{0,4},{1,5},{2,6},{3,7},{4,0},{5,1},{6,2},{7,3},{8,12},{9,13},{10,... | collective-permute-start | bytes 798728 | tf_op jit(solution)/shard_map/ppermute | solution.py:385
  12.3 17.4 %collective-permute-start.3 = (bf16[1040,128]{1,0:T(8,128)(2,1)S(1)}, bf16[1040,128]{1,0:T(8,128)(2,1)S(1)}, u32[]{:S(2)}, u32[]{:S(2)}) collective-permute-start(bf16[1040,128]{1,0:T(8,128)(2,1)S(1)} %get-tuple-element.26), channel_id=1, source_target_pairs={{0,5},{1,4},{2,7},{3,6},{4,1},{5,0},{6,3},{7,2},{8,13},{9,12},{10,... | collective-permute-start | bytes 798728 | tf_op jit(solution)/shard_map/ppermute | solution.py:385
  17.9 14.8 %collective-permute-start.5 = (bf16[272,384]{1,0:T(8,128)(2,1)S(1)}, bf16[272,384]{1,0:T(8,128)(2,1)S(1)}, u32[]{:S(2)}, u32[]{:S(2)}) collective-permute-start(bf16[272,384]{1,0:T(8,128)(2,1)S(1)} %hidden.5._.refs_1_), channel_id=1, source_target_pairs={{0,96},{8,104},{16,112},{24,120},{32,64},{40,72},{48,80},{56,88},{... | collective-permute-start | bytes 626696 | tf_op jit(solution)/shard_map/ppermute | solution.py:372
  21.5 11.2 %collective-permute-start.8 = (bf16[272,384]{1,0:T(8,128)(2,1)S(1)}, bf16[272,384]{1,0:T(8,128)(2,1)S(1)}, u32[]{:S(2)}, u32[]{:S(2)}) collective-permute-start(bf16[272,384]{1,0:T(8,128)(2,1)S(1)} %hidden.8.refs_3_), channel_id=1, source_target_pairs={{0,96},{8,104},{16,112},{24,120},{32,64},{40,72},{48,80},{56,88},{... | collective-permute-start | bytes 626696 | tf_op jit(solution)/shard_map/ppermute | solution.py:372
  21.7 14.1 %collective-permute-start.11 = (bf16[272,384]{1,0:T(8,128)(2,1)S(1)}, bf16[272,384]{1,0:T(8,128)(2,1)S(1)}, u32[]{:S(2)}, u32[]{:S(2)}) collective-permute-start(bf16[272,384]{1,0:T(8,128)(2,1)S(1)} %hidden.9.refs_5_), channel_id=1, source_target_pairs={{0,96},{8,104},{16,112},{24,120},{32,64},{40,72},{48,80},{56,88},{... | collective-permute-start | bytes 626696 | tf_op jit(solution)/shard_map/ppermute | solution.py:372
  26.1 12.1 %collective-permute-start.2 = (bf16[144,384]{1,0:T(8,128)(2,1)S(1)}, bf16[144,384]{1,0:T(8,128)(2,1)S(1)}, u32[]{:S(2)}, u32[]{:S(2)}) collective-permute-start(bf16[144,384]{1,0:T(8,128)(2,1)S(1)} %hidden.6.refs_1_), channel_id=1, source_target_pairs={{0,96},{8,104},{16,112},{24,120},{32,64},{40,72},{48,80},{56,88},{... | collective-permute-start | bytes 331784 | tf_op jit(solution)/shard_map/ppermute | solution.py:372
  30.3 10.3 %collective-permute-start.4 = (bf16[144,384]{1,0:T(8,128)(2,1)S(1)}, bf16[144,384]{1,0:T(8,128)(2,1)S(1)}, u32[]{:S(2)}, u32[]{:S(2)}) collective-permute-start(bf16[144,384]{1,0:T(8,128)(2,1)S(1)} %hidden.7.refs_3_), channel_id=1, source_target_pairs={{0,96},{8,104},{16,112},{24,120},{32,64},{40,72},{48,80},{56,88},{... | collective-permute-start | bytes 331784 | tf_op jit(solution)/shard_map/ppermute | solution.py:372
  64.7 8.3 %collective-permute-start.12 = (f32[288,128]{1,0:T(8,128)S(1)}, f32[288,128]{1,0:T(8,128)S(1)}, u32[]{:S(2)}, u32[]{:S(2)}) collective-permute-start(f32[288,128]{1,0:T(8,128)S(1)} %slice.8), channel_id=1, source_target_pairs={{32,0},{40,8},{48,16},{56,24},{96,64},{104,72},{112,80},{120,88},{... | collective-permute-start | bytes 442376 | tf_op jit(solution)/shard_map/ppermute | solution.py:401

commit v7 on v5

--- a/solution.py
+++ b/solution.py
@@ -12,7 +12,7 @@
 TAG = 16
 SIDE = 4
 VMEM_BYTES = 20 << 20
-EDGES = (0, 2, 4, 6, 7, 8)
+EDGES = (0, 2, 6, 7, 8)
 STRIP = 64
 F32 = jnp.float32
 BF16 = jnp.bfloat16
@@ -300,7 +300,7 @@
     return unfold(folded * scale, corner * scale) + RIDGE * identity_tile()
 
 
-def first_kernel(part_ref, top_ref, mid_ref, *, scale):
+def first_kernel(part_ref, top_ref, mid_ref, cross_ref, *, scale):
     tip = lambda i: part_ref[TIP + i : TIP + i + 1, :]
     top_ref[:, :LANE] = diagonal(part_ref[:HALF, :], tip(0), scale)
     top_ref[:, LANE : 2 * LANE] = part_ref[HALF:SECOND, :] * scale
@@ -309,21 +309,23 @@
     side = top_ref[:, LANE : 2 * LANE]
     mid_ref[:, :LANE] = diagonal(part_ref[SECOND:THIRD, :], tip(1), scale) - dot_high(side, side, TN)
     mid_ref[:, LANE:] = identity_tile()
+    cross_ref[...] = dot_high(side, top_ref[:, 2 * LANE :], TN)
     factor_panel(mid_ref)
 
 
 def first_panels(part, scale):
     return pl.pallas_call(
         lambda *refs: first_kernel(*refs, scale=scale),
-        out_shape=[pltpu.VMEM((LANE, 3 * LANE), F32), pltpu.VMEM((LANE, 2 * LANE), F32)],
+        out_shape=[pltpu.VMEM((LANE, n * LANE), F32) for n in (3, 2, 1)],
         compiler_params=pltpu.CompilerParams(vmem_limit_bytes=VMEM_BYTES),
         name="first_panels",
     )(near(part))
 
 
-def last_kernel(part_ref, other_ref, top_ref, mid_ref, out_ref, low, *, scale):
-    right = dot_high(top_ref[:, 2 * LANE :], other_ref[:LANE, :] * scale, NN)
-    rest = other_ref[LANE : 2 * LANE, :] * scale - dot_high(top_ref[:, LANE : 2 * LANE], right, TN)
+def last_kernel(part_ref, other_ref, top_ref, mid_ref, cross_ref, out_ref, low, *, scale):
+    corner = other_ref[:LANE, :] * scale
+    right = dot_high(top_ref[:, 2 * LANE :], corner, NN)
+    rest = other_ref[LANE : 2 * LANE, :] * scale - dot_high(cross_ref[...], corner, NN)
     below = dot_high(mid_ref[:, LANE:], rest, NN)
     folded = jnp.concatenate([part_ref[THIRD:TIP, :], other_ref[THIRD:TIP, :]], axis=0)
     low[...] = (
@@ -342,7 +344,7 @@
     out_ref[2 * LANE :, 2 * LANE :] = low[...].astype(kind)
 
 
-def last_panel(part, other, top, mid, scale):
+def last_panel(part, other, top, mid, cross, scale):
     width = top.shape[1]
     return pl.pallas_call(
         lambda *refs: last_kernel(*refs, scale=scale),
@@ -350,7 +352,7 @@
         scratch_shapes=[pltpu.VMEM((LANE, LANE), F32)],
         compiler_params=pltpu.CompilerParams(vmem_limit_bytes=VMEM_BYTES),
         name="last_panel",
-    )(near(part), near(other), near(top), near(mid))
+    )(*[near(x) for x in (part, other, top, mid, cross)])
 
 
 def on_device(tokens, block_expert, gate_weight, up_weight):
@@ -398,8 +400,8 @@
     halves = [(d + SIDE, d) for d in range(replicas) if d // SIDE % 2 == 0]
     other = lax.ppermute(own[:TIP], "dp", halves)
     scale = experts_each / (tokens.shape[0] * replicas)
-    top, mid = first_panels(own, scale)
-    result = last_panel(own, other, top, mid, scale)
+    top, mid, cross = first_panels(own, scale)
+    result = last_panel(own, other, top, mid, cross, scale)
     row_count = hidden_width // replicas
     sent = result.reshape(replicas, row_count, hidden_width)
     returned = lax.all_to_all(sent, "dp", split_axis=0, concat_axis=0, tiled=True)

time: 93.7 us -> 93.3 us (level)
  waiting for transfers between devices: 10.9 us -> 17.3 us
  starting transfers between devices: 19 us -> 14.2 us
  blocking collectives: 40.2 us -> 38.4 us
    ppermute x7, waiting for transfers between devices: 4.8 us -> 12.8 us  [on_device(): lax.ppermute(payload, 'expert', route)]
    ppermute x5 -> x4, starting transfers between devices: 9.48 us -> 4.68 us  [swap_rows(): gathered.append([rows, lax.ppermute(rows, 'dp', pairs)])]
    ppermute x5 -> x4, waiting for transfers between devices: 6.06 us -> 4.48 us  [swap_rows(): gathered.append([rows, lax.ppermute(rows, 'dp', pairs)])]
    all_to_all x1, blocking collectives: 14 us -> 12.8 us  [on_device(): lax.all_to_all(sent, 'dp', split_axis=0, concat_axis=0, tiled=True)]
    pallas_call x5 -> x4, Pallas kernels: 3.6 us -> 3.49 us  [hidden_rows(): pl.pallas_call(lambda *refs: hidden_kernel(*refs, slots=slots, model_widt...]
  transfers between devices with their start and end apart: 13 -> 12, of which waited for: 6 -> 5; matrix products, arithmetic and copies ran while one was open for 0% -> 0% of each run, Pallas kernels for 17% -> 16%
where the time goes in v7:
time: 93.3 us; the launch traced here: 93.1 us
  blocking collectives  38.4 us (41%)
  Pallas kernels  22.2 us (24%)
  waiting for transfers between devices  17.3 us (19%)
  starting transfers between devices  14.2 us (15%)
    all_to_all x1, blocking collectives, on_device(): lax.all_to_all(partial_gram, 'dp', split_axis=0, concat_axis=0, axis_inde...  25.7 us
    ppermute x7, waiting for transfers between devices, on_device(): lax.ppermute(payload, 'expert', route)  12.8 us
    all_to_all x1, blocking collectives, on_device(): lax.all_to_all(sent, 'dp', split_axis=0, concat_axis=0, tiled=True)  12.8 us
    ppermute x7, starting transfers between devices, on_device(): lax.ppermute(payload, 'expert', route)  8.05 us
    pallas_call x1, Pallas kernels, first_panels(): pl.pallas_call(lambda *refs: first_kernel(*refs, scale=scale), out_shape=...  6.83 us
    ppermute x4, starting transfers between devices, swap_rows(): gathered.append([rows, lax.ppermute(rows, 'dp', pairs)])  4.68 us
    pallas_call x1, Pallas kernels, bring(): pl.pallas_call(bring_kernel, in_specs=[pl.BlockSpec(memory_space=pl.ANY)]...  4.63 us
    ppermute x4, waiting for transfers between devices, swap_rows(): gathered.append([rows, lax.ppermute(rows, 'dp', pairs)])  4.48 us
  transfers between devices with their start and end apart: 12, of which 5 were waited for; matrix products, arithmetic and copies ran while one was open for 0% of the time, Pallas kernels for 16%

profile of v7, /device:TPU:0, one launch (start us, length us, event | category | flops | bytes accessed | tf_op | source)
XLA Modules:
  0.0 93.1 jit_solution(13517523000750770661)
XLA Ops:
  0.0 1.7 %pack.1 = (bf16[1040,128]{1,0:T(8,128)(2,1)S(1)}, bf16[1040,128]{1,0:T(8,128)(2,1)S(1)}, bf16[1040,128]{1,0:T(8,128)(2,1)S(1)}, bf16[1040,128]{1,0:T(8,128)(2,1)...) custom-call(s32[1]{0:T(128)} %bitcast.1.refs_0_, ...), custom_call_target="tpu_custom_call" | custom-call | tf_op jit(solution)/shard_map/pack/pallas_call | solution.py:71
  1.7 0.1 collective-permute-start
  1.8 1.8 %collective-permute-start.6 = (bf16[1040,128]{1,0:T(8,128)(2,1)S(1)}, bf16[1040,128]{1,0:T(8,128)(2,1)S(1)}, u32[]{:S(2)}, u32[]{:S(2)}) collective-permute-start(bf16[1040,128]{1,0:T(8,128)(2,1)S(1)} %get-tuple-element.28), channel_id=1, source_target_pairs={{0,2},{1,3},{2,4},{3,5},{4,6},{5,7},{6,0},{7,1},{8,10},{9,11},{10,... | collective-permute-start | bytes 798728 | tf_op jit(solution)/shard_map/ppermute | solution.py:386
  3.5 1.5 %collective-permute-start.7 = (bf16[1040,128]{1,0:T(8,128)(2,1)S(1)}, bf16[1040,128]{1,0:T(8,128)(2,1)S(1)}, u32[]{:S(2)}, u32[]{:S(2)}) collective-permute-start(bf16[1040,128]{1,0:T(8,128)(2,1)S(1)} %get-tuple-element.29), channel_id=1, source_target_pairs={{0,6},{1,7},{2,0},{3,1},{4,2},{5,3},{6,4},{7,5},{8,14},{9,15},{10,... | collective-permute-start | bytes 798728 | tf_op jit(solution)/shard_map/ppermute | solution.py:386
  5.1 0.0 collective-permute-start.8
  5.1 3.0 %collective-permute-start.9 = (bf16[1040,128]{1,0:T(8,128)(2,1)S(1)}, bf16[1040,128]{1,0:T(8,128)(2,1)S(1)}, u32[]{:S(2)}, u32[]{:S(2)}) collective-permute-start(bf16[1040,128]{1,0:T(8,128)(2,1)S(1)} %get-tuple-element.31), channel_id=1, source_target_pairs={{0,7},{1,6},{2,1},{3,0},{4,3},{5,2},{6,5},{7,4},{8,15},{9,14},{10,... | collective-permute-start | bytes 798728 | tf_op jit(solution)/shard_map/ppermute | solution.py:386
  8.0 2.2 %hidden.4._.refs_1_ = bf16[272,384]{1,0:T(8,128)(2,1)S(1)} custom-call(bf16[1040,128]{1,0:T(8,128)(2,1)S(1)} %get-tuple-element.21.refs_0_, bf16[1040,128]{1,0:T(8,128)(2,1)S(1)} %collective-permute-done.refs_1_, bf16[8,1024,384]{2,1,0:T(8,128)(2,1)} %gate_ref.1, bf16[8,1024,384]{2,1,0:T(8,128)(2,1)} %up_ref.1), custom_call_target="tpu_custom_call" | custom-call | tf_op jit(solution)/shard_map/hidden/pallas_call | solution.py:138
  10.2 4.6 %bring.1 = (bf16[8,1024,384]{2,1,0:T(8,128)(2,1)S(1)}, bf16[8,1024,384]{2,1,0:T(8,128)(2,1)S(1)}) custom-call(bf16[272,384]{1,0:T(8,128)(2,1)S(1)} %hidden.4._.refs_1_, bf16[8,1024,384]{2,1,0:T(8,128)(2,1)} %gate_ref.1, bf16[8,1024,384]{2,1,0:T(8,128)(2,1)} %up_ref.1), custom_call_target="tpu_custom_call" | custom-call | tf_op jit(solution)/shard_map/bring/pallas_call | solution.py:162
  14.9 0.0 collective-permute-done.6.refs_0_
  14.9 2.4 %collective-permute-done.8.refs_2_ = bf16[1040,128]{1,0:T(8,128)(2,1)S(1)} collective-permute-done((bf16[1040,128]{1,0:T(8,128)(2,1)S(1)}, bf16[1040,128]{1,0:T(8,128)(2,1)S(1)}, u32[]{:S(2)}, u32[]{:S(2)}) %collective-permute-start.8) | collective-permute-done | bytes 266272 | tf_op jit(solution)/shard_map/ppermute | solution.py:386
  17.3 0.0 collective-permute-done.9.refs_3_
  17.3 0.6 hidden.7.refs_3_
  17.9 3.2 %collective-permute-start.10 = (bf16[528,384]{1,0:T(8,128)(2,1)S(1)}, bf16[528,384]{1,0:T(8,128)(2,1)S(1)}, u32[]{:S(2)}, u32[]{:S(2)}) collective-permute-start(bf16[528,384]{1,0:T(8,128)(2,1)S(1)} %hidden.7.refs_3_), channel_id=1, source_target_pairs={{0,8},{8,0},{16,24},{24,16},{32,40},{40,32},{48,56},{56,48},{64,72... | collective-permute-start | bytes 1216520 | tf_op jit(solution)/shard_map/ppermute | solution.py:373
  21.1 1.7 %collective-permute-start.1 = (bf16[1040,128]{1,0:T(8,128)(2,1)S(1)}, bf16[1040,128]{1,0:T(8,128)(2,1)S(1)}, u32[]{:S(2)}, u32[]{:S(2)}) collective-permute-start(bf16[1040,128]{1,0:T(8,128)(2,1)S(1)} %get-tuple-element.23), channel_id=1, source_target_pairs={{0,4},{1,5},{2,6},{3,7},{4,0},{5,1},{6,2},{7,3},{8,12},{9,13},{10,... | collective-permute-start | bytes 798728 | tf_op jit(solution)/shard_map/ppermute | solution.py:386
  22.8 0.3 collective-permute-start.5
  23.0 8.8 %collective-permute-done.1.refs_0_ = bf16[1040,128]{1,0:T(8,128)(2,1)S(1)} collective-permute-done((bf16[1040,128]{1,0:T(8,128)(2,1)S(1)}, bf16[1040,128]{1,0:T(8,128)(2,1)S(1)}, u32[]{:S(2)}, u32[]{:S(2)}) %collective-permute-start.1) | collective-permute-done | bytes 266272 | tf_op jit(solution)/shard_map/ppermute | solution.py:386
  31.8 0.1 hidden.5.refs_1_
  32.0 0.6 collective-permute-start.2
  32.6 1.6 %collective-permute-done.3.refs_0_ = bf16[1040,128]{1,0:T(8,128)(2,1)S(1)} collective-permute-done((bf16[1040,128]{1,0:T(8,128)(2,1)S(1)}, bf16[1040,128]{1,0:T(8,128)(2,1)S(1)}, u32[]{:S(2)}, u32[]{:S(2)}) %collective-permute-start.3) | collective-permute-done | bytes 266272 | tf_op jit(solution)/shard_map/ppermute | solution.py:386
  34.2 0.6 hidden.6.refs_3_
  34.8 0.6 collective-permute-start.4
  35.4 0.8 gram.2.refs_5_
  36.3 0.5 collective-permute-done.2.refs_2_
  36.8 3.9 %collective-permute-done.4.refs_4_ = bf16[144,384]{1,0:T(8,128)(2,1)S(1)} collective-permute-done((bf16[144,384]{1,0:T(8,128)(2,1)S(1)}, bf16[144,384]{1,0:T(8,128)(2,1)S(1)}, u32[]{:S(2)}, u32[]{:S(2)}) %collective-permute-start.4) | collective-permute-done | bytes 110624 | tf_op jit(solution)/shard_map/ppermute | solution.py:373
  40.7 0.8 gram.3
  41.5 25.7 %all_to_all.10 = f32[8,296,128]{2,1,0:T(8,128)S(1)} all-to-all(f32[8,296,128]{2,1,0:T(8,128)S(1)} %gram.3), channel_id=1, replica_groups={{0,32,64,96,16,48,80,112},{8,40,72,104,24,56,88,120},{1,33,65,97,17,49,..., dimensions={0} | all-to-all | bytes 2424832 | tf_op jit(solution)/shard_map/all_to_all | solution.py:396
  67.2 0.1 reduce_sum.9.refs_0_
  67.3 1.5 %collective-permute-start.11 = (f32[288,128]{1,0:T(8,128)S(1)}, f32[288,128]{1,0:T(8,128)S(1)}, u32[]{:S(2)}, u32[]{:S(2)}) collective-permute-start(f32[288,128]{1,0:T(8,128)S(1)} %slice.8), channel_id=1, source_target_pairs={{32,0},{40,8},{48,16},{56,24},{96,64},{104,72},{112,80},{120,88},{... | collective-permute-start | bytes 442376 | tf_op jit(solution)/shard_map/ppermute | solution.py:401
  68.7 6.8 %first_panels.1 = (f32[128,384]{1,0:T(8,128)S(1)}, f32[128,256]{1,0:T(8,128)S(1)}, f32[128,128]{1,0:T(8,128)S(1)}) custom-call(f32[296,128]{1,0:T(8,128)S(1)} %reduce_sum.9.refs_0_), custom_call_target="tpu_custom_call" | custom-call | tf_op jit(solution)/shard_map/first_panels/pallas_call | solution.py:317
  75.6 4.0 %last_panel.1 = bf16[384,384]{1,0:T(8,128)(2,1)S(1)} custom-call(f32[296,128]{1,0:T(8,128)S(1)} %reduce_sum.9.refs_0_, f32[288,128]{1,0:T(8,128)S(1)} %collective-permute-done.11.refs_1_, f32[128,384]{1,0:T(8,128)S(1)} %get-tuple-element.32.refs_2_, f32[128,256]{1,0:T(8,128)S(1)} %get-tuple-element.33.refs_3_, f32[128,128]{1,0:T(8,128)S(1)} %get-tuple-element.34.refs_4_), custom_call_target="tpu_custom_call" | custom-call | tf_op jit(solution)/shard_map/last_panel/pallas_call | solution.py:349
  79.6 12.8 %all_to_all.11 = bf16[16,24,384]{2,1,0:T(8,128)(2,1)S(1)} all-to-all(bf16[16,24,384]{2,1,0:T(8,128)(2,1)S(1)} %bitcast.12), channel_id=1, replica_groups=mesh['dp'=16,'expert'=8] {'dp'}, dimensions={0} | all-to-all | bytes 589824 | tf_op jit(solution)/shard_map/all_to_all | solution.py:407
  92.4 0.7 fusion
  (7 shorter events, 0.0 us)
Async XLA Ops:
  1.7 6.4 %collective-permute-start = (bf16[1040,128]{1,0:T(8,128)(2,1)S(1)}, bf16[1040,128]{1,0:T(8,128)(2,1)S(1)}, u32[]{:S(2)}, u32[]{:S(2)}) collective-permute-start(bf16[1040,128]{1,0:T(8,128)(2,1)S(1)} %get-tuple-element.22), channel_id=1, source_target_pairs={{0,1},{1,0},{2,3},{3,2},{4,5},{5,4},{6,7},{7,6},{8,9},{9,8},{10,11... | collective-permute-start | bytes 798728 | tf_op jit(solution)/shard_map/ppermute | solution.py:386
  1.8 13.1 %collective-permute-start.6 = (bf16[1040,128]{1,0:T(8,128)(2,1)S(1)}, bf16[1040,128]{1,0:T(8,128)(2,1)S(1)}, u32[]{:S(2)}, u32[]{:S(2)}) collective-permute-start(bf16[1040,128]{1,0:T(8,128)(2,1)S(1)} %get-tuple-element.28), channel_id=1, source_target_pairs={{0,2},{1,3},{2,4},{3,5},{4,6},{5,7},{6,0},{7,1},{8,10},{9,11},{10,... | collective-permute-start | bytes 798728 | tf_op jit(solution)/shard_map/ppermute | solution.py:386
  3.5 11.4 %collective-permute-start.7 = (bf16[1040,128]{1,0:T(8,128)(2,1)S(1)}, bf16[1040,128]{1,0:T(8,128)(2,1)S(1)}, u32[]{:S(2)}, u32[]{:S(2)}) collective-permute-start(bf16[1040,128]{1,0:T(8,128)(2,1)S(1)} %get-tuple-element.29), channel_id=1, source_target_pairs={{0,6},{1,7},{2,0},{3,1},{4,2},{5,3},{6,4},{7,5},{8,14},{9,15},{10,... | collective-permute-start | bytes 798728 | tf_op jit(solution)/shard_map/ppermute | solution.py:386
  5.1 12.2 %collective-permute-start.8 = (bf16[1040,128]{1,0:T(8,128)(2,1)S(1)}, bf16[1040,128]{1,0:T(8,128)(2,1)S(1)}, u32[]{:S(2)}, u32[]{:S(2)}) collective-permute-start(bf16[1040,128]{1,0:T(8,128)(2,1)S(1)} %get-tuple-element.30), channel_id=1, source_target_pairs={{0,3},{1,2},{2,5},{3,4},{4,7},{5,6},{6,1},{7,0},{8,11},{9,10},{10,... | collective-permute-start | bytes 798728 | tf_op jit(solution)/shard_map/ppermute | solution.py:386
  5.1 12.2 %collective-permute-start.9 = (bf16[1040,128]{1,0:T(8,128)(2,1)S(1)}, bf16[1040,128]{1,0:T(8,128)(2,1)S(1)}, u32[]{:S(2)}, u32[]{:S(2)}) collective-permute-start(bf16[1040,128]{1,0:T(8,128)(2,1)S(1)} %get-tuple-element.31), channel_id=1, source_target_pairs={{0,7},{1,6},{2,1},{3,0},{4,3},{5,2},{6,5},{7,4},{8,15},{9,14},{10,... | collective-permute-start | bytes 798728 | tf_op jit(solution)/shard_map/ppermute | solution.py:386
  17.9 17.5 %collective-permute-start.10 = (bf16[528,384]{1,0:T(8,128)(2,1)S(1)}, bf16[528,384]{1,0:T(8,128)(2,1)S(1)}, u32[]{:S(2)}, u32[]{:S(2)}) collective-permute-start(bf16[528,384]{1,0:T(8,128)(2,1)S(1)} %hidden.7.refs_3_), channel_id=1, source_target_pairs={{0,8},{8,0},{16,24},{24,16},{32,40},{40,32},{48,56},{56,48},{64,72... | collective-permute-start | bytes 1216520 | tf_op jit(solution)/shard_map/ppermute | solution.py:373
  21.1 10.8 %collective-permute-start.1 = (bf16[1040,128]{1,0:T(8,128)(2,1)S(1)}, bf16[1040,128]{1,0:T(8,128)(2,1)S(1)}, u32[]{:S(2)}, u32[]{:S(2)}) collective-permute-start(bf16[1040,128]{1,0:T(8,128)(2,1)S(1)} %get-tuple-element.23), channel_id=1, source_target_pairs={{0,4},{1,5},{2,6},{3,7},{4,0},{5,1},{6,2},{7,3},{8,12},{9,13},{10,... | collective-permute-start | bytes 798728 | tf_op jit(solution)/shard_map/ppermute | solution.py:386
  22.8 11.4 %collective-permute-start.3 = (bf16[1040,128]{1,0:T(8,128)(2,1)S(1)}, bf16[1040,128]{1,0:T(8,128)(2,1)S(1)}, u32[]{:S(2)}, u32[]{:S(2)}) collective-permute-start(bf16[1040,128]{1,0:T(8,128)(2,1)S(1)} %get-tuple-element.27), channel_id=1, source_target_pairs={{0,5},{1,4},{2,7},{3,6},{4,1},{5,0},{6,3},{7,2},{8,13},{9,12},{10,... | collective-permute-start | bytes 798728 | tf_op jit(solution)/shard_map/ppermute | solution.py:386
  22.8 12.6 %collective-permute-start.5 = (bf16[272,384]{1,0:T(8,128)(2,1)S(1)}, bf16[272,384]{1,0:T(8,128)(2,1)S(1)}, u32[]{:S(2)}, u32[]{:S(2)}) collective-permute-start(bf16[272,384]{1,0:T(8,128)(2,1)S(1)} %hidden.4._.refs_1_), channel_id=1, source_target_pairs={{0,8},{8,0},{16,24},{24,16},{32,40},{40,32},{48,56},{56,48},{64,72... | collective-permute-start | bytes 626696 | tf_op jit(solution)/shard_map/ppermute | solution.py:373
  32.0 4.8 %collective-permute-start.2 = (bf16[144,384]{1,0:T(8,128)(2,1)S(1)}, bf16[144,384]{1,0:T(8,128)(2,1)S(1)}, u32[]{:S(2)}, u32[]{:S(2)}) collective-permute-start(bf16[144,384]{1,0:T(8,128)(2,1)S(1)} %hidden.5.refs_1_), channel_id=1, source_target_pairs={{0,8},{8,0},{16,24},{24,16},{32,40},{40,32},{48,56},{56,48},{64,72... | collective-permute-start | bytes 331784 | tf_op jit(solution)/shard_map/ppermute | solution.py:373
  34.8 6.0 %collective-permute-start.4 = (bf16[144,384]{1,0:T(8,128)(2,1)S(1)}, bf16[144,384]{1,0:T(8,128)(2,1)S(1)}, u32[]{:S(2)}, u32[]{:S(2)}) collective-permute-start(bf16[144,384]{1,0:T(8,128)(2,1)S(1)} %hidden.6.refs_3_), channel_id=1, source_target_pairs={{0,8},{8,0},{16,24},{24,16},{32,40},{40,32},{48,56},{56,48},{64,72... | collective-permute-start | bytes 331784 | tf_op jit(solution)/shard_map/ppermute | solution.py:373
  67.3 8.3 %collective-permute-start.11 = (f32[288,128]{1,0:T(8,128)S(1)}, f32[288,128]{1,0:T(8,128)S(1)}, u32[]{:S(2)}, u32[]{:S(2)}) collective-permute-start(f32[288,128]{1,0:T(8,128)S(1)} %slice.8), channel_id=1, source_target_pairs={{32,0},{40,8},{48,16},{56,24},{96,64},{104,72},{112,80},{120,88},{... | collective-permute-start | bytes 442376 | tf_op jit(solution)/shard_map/ppermute | solution.py:401

commit v8 on v7

--- a/solution.py
+++ b/solution.py
@@ -12,7 +12,7 @@
 TAG = 16
 SIDE = 4
 VMEM_BYTES = 20 << 20
-EDGES = (0, 2, 6, 7, 8)
+EDGES = (0, 2, 4, 6, 7, 8)
 STRIP = 64
 F32 = jnp.float32
 BF16 = jnp.bfloat16
@@ -388,8 +388,8 @@
         swap_rows(g)
     kept = experts_each // 2
     first = (lax.axis_index("dp") % 2 * kept).reshape(1)
-    partial_gram = gram(first, kept, [rows for pair in gathered[:-2] for rows in pair])
-    tail = [rows for pair in gathered[-2:] for rows in pair]
+    partial_gram = gram(first, kept, [rows for pair in gathered[:-1] for rows in pair])
+    tail = [rows for pair in gathered[-1:] for rows in pair]
     partial_gram = gram(first, kept, tail, (partial_gram,))
     side = replicas // SIDE
     classes = [[x * SIDE + z for z in range(p, SIDE, 2) for x in range(side)] for p in range(2)]

time: 93.3 us -> 93.2 us (level)
  waiting for transfers between devices: 17.3 us -> 10.5 us
  starting transfers between devices: 14.2 us -> 19 us
  blocking collectives: 38.4 us -> 40.2 us
    ppermute x7, waiting for transfers between devices: 12.8 us -> 4.8 us  [on_device(): lax.ppermute(payload, 'expert', route)]
    ppermute x4 -> x5, starting transfers between devices: 4.68 us -> 9.48 us  [swap_rows(): gathered.append([rows, lax.ppermute(rows, 'dp', pairs)])]
    ppermute x4 -> x5, waiting for transfers between devices: 4.48 us -> 5.74 us  [swap_rows(): gathered.append([rows, lax.ppermute(rows, 'dp', pairs)])]
    pallas_call x4 -> x5, Pallas kernels: 3.49 us -> 3.6 us  [hidden_rows(): pl.pallas_call(lambda *refs: hidden_kernel(*refs, slots=slots, model_widt...]
  transfers between devices with their start and end apart: 12 -> 13, of which waited for: 5 -> 6; matrix products, arithmetic and copies ran while one was open for 0% -> 0% of each run, Pallas kernels for 16% -> 17%
where the time goes in v8:
time: 93.2 us; the launch traced here: 93 us
  blocking collectives  40.2 us (43%)
  Pallas kernels  22.3 us (24%)
  starting transfers between devices  19 us (20%)
  waiting for transfers between devices  10.5 us (11%)
    all_to_all x1, blocking collectives, on_device(): lax.all_to_all(partial_gram, 'dp', split_axis=0, concat_axis=0, axis_inde...  26.6 us
    all_to_all x1, blocking collectives, on_device(): lax.all_to_all(sent, 'dp', split_axis=0, concat_axis=0, tiled=True)  13.7 us
    ppermute x5, starting transfers between devices, swap_rows(): gathered.append([rows, lax.ppermute(rows, 'dp', pairs)])  9.48 us
    ppermute x7, starting transfers between devices, on_device(): lax.ppermute(payload, 'expert', route)  8.02 us
    pallas_call x1, Pallas kernels, first_panels(): pl.pallas_call(lambda *refs: first_kernel(*refs, scale=scale), out_shape=...  6.83 us
    ppermute x5, waiting for transfers between devices, swap_rows(): gathered.append([rows, lax.ppermute(rows, 'dp', pairs)])  5.74 us
    ppermute x7, waiting for transfers between devices, on_device(): lax.ppermute(payload, 'expert', route)  4.8 us
    pallas_call x1, Pallas kernels, bring(): pl.pallas_call(bring_kernel, in_specs=[pl.BlockSpec(memory_space=pl.ANY)]...  4.62 us
  transfers between devices with their start and end apart: 13, of which 6 were waited for; matrix products, arithmetic and copies ran while one was open for 0% of the time, Pallas kernels for 17%

profile of v8, /device:TPU:0, one launch (start us, length us, event | category | flops | bytes accessed | tf_op | source)
XLA Modules:
  0.0 93.0 jit_solution(18093229543876935222)
XLA Ops:
  0.0 1.7 %pack.1 = (bf16[1040,128]{1,0:T(8,128)(2,1)S(1)}, bf16[1040,128]{1,0:T(8,128)(2,1)S(1)}, bf16[1040,128]{1,0:T(8,128)(2,1)S(1)}, bf16[1040,128]{1,0:T(8,128)(2,1)...) custom-call(s32[1]{0:T(128)} %bitcast.1.refs_0_, ...), custom_call_target="tpu_custom_call" | custom-call | tf_op jit(solution)/shard_map/pack/pallas_call | solution.py:71
  1.7 0.1 collective-permute-start
  1.8 1.8 %collective-permute-start.4 = (bf16[1040,128]{1,0:T(8,128)(2,1)S(1)}, bf16[1040,128]{1,0:T(8,128)(2,1)S(1)}, u32[]{:S(2)}, u32[]{:S(2)}) collective-permute-start(bf16[1040,128]{1,0:T(8,128)(2,1)S(1)} %get-tuple-element.26), channel_id=1, source_target_pairs={{0,2},{1,3},{2,4},{3,5},{4,6},{5,7},{6,0},{7,1},{8,10},{9,11},{10,... | collective-permute-start | bytes 798728 | tf_op jit(solution)/shard_map/ppermute | solution.py:386
  3.5 1.5 %collective-permute-start.5 = (bf16[1040,128]{1,0:T(8,128)(2,1)S(1)}, bf16[1040,128]{1,0:T(8,128)(2,1)S(1)}, u32[]{:S(2)}, u32[]{:S(2)}) collective-permute-start(bf16[1040,128]{1,0:T(8,128)(2,1)S(1)} %get-tuple-element.27), channel_id=1, source_target_pairs={{0,6},{1,7},{2,0},{3,1},{4,2},{5,3},{6,4},{7,5},{8,14},{9,15},{10,... | collective-permute-start | bytes 798728 | tf_op jit(solution)/shard_map/ppermute | solution.py:386
  5.1 3.0 %collective-permute-start.8 = (bf16[1040,128]{1,0:T(8,128)(2,1)S(1)}, bf16[1040,128]{1,0:T(8,128)(2,1)S(1)}, u32[]{:S(2)}, u32[]{:S(2)}) collective-permute-start(bf16[1040,128]{1,0:T(8,128)(2,1)S(1)} %get-tuple-element.29), channel_id=1, source_target_pairs={{0,7},{1,6},{2,1},{3,0},{4,3},{5,2},{6,5},{7,4},{8,15},{9,14},{10,... | collective-permute-start | bytes 798728 | tf_op jit(solution)/shard_map/ppermute | solution.py:386
  8.0 2.2 %hidden.5._.refs_1_ = bf16[272,384]{1,0:T(8,128)(2,1)S(1)} custom-call(bf16[1040,128]{1,0:T(8,128)(2,1)S(1)} %get-tuple-element.21.refs_0_, bf16[1040,128]{1,0:T(8,128)(2,1)S(1)} %collective-permute-done.refs_1_, bf16[8,1024,384]{2,1,0:T(8,128)(2,1)} %gate_ref.1, bf16[8,1024,384]{2,1,0:T(8,128)(2,1)} %up_ref.1), custom_call_target="tpu_custom_call" | custom-call | tf_op jit(solution)/shard_map/hidden/pallas_call | solution.py:138
  10.2 0.8 collective-permute-start.10
  11.0 1.3 %collective-permute-done.4.refs_0_ = bf16[1040,128]{1,0:T(8,128)(2,1)S(1)} collective-permute-done((bf16[1040,128]{1,0:T(8,128)(2,1)S(1)}, bf16[1040,128]{1,0:T(8,128)(2,1)S(1)}, u32[]{:S(2)}, u32[]{:S(2)}) %collective-permute-start.4) | collective-permute-done | bytes 266272 | tf_op jit(solution)/shard_map/ppermute | solution.py:386
  12.3 0.9 collective-permute-start.1
  13.2 4.6 %bring.1 = (bf16[8,1024,384]{2,1,0:T(8,128)(2,1)S(1)}, bf16[8,1024,384]{2,1,0:T(8,128)(2,1)S(1)}) custom-call(bf16[272,384]{1,0:T(8,128)(2,1)S(1)} %hidden.5._.refs_1_, bf16[8,1024,384]{2,1,0:T(8,128)(2,1)} %gate_ref.1, bf16[8,1024,384]{2,1,0:T(8,128)(2,1)} %up_ref.1), custom_call_target="tpu_custom_call" | custom-call | tf_op jit(solution)/shard_map/bring/pallas_call | solution.py:162
  17.9 2.0 %collective-permute-start.3 = (bf16[272,384]{1,0:T(8,128)(2,1)S(1)}, bf16[272,384]{1,0:T(8,128)(2,1)S(1)}, u32[]{:S(2)}, u32[]{:S(2)}) collective-permute-start(bf16[272,384]{1,0:T(8,128)(2,1)S(1)} %hidden.5._.refs_1_), channel_id=1, source_target_pairs={{0,8},{8,0},{16,24},{24,16},{32,40},{40,32},{48,56},{56,48},{64,72... | collective-permute-start | bytes 626696 | tf_op jit(solution)/shard_map/ppermute | solution.py:373
  19.9 0.6 hidden.7.refs_3_
  20.4 0.6 collective-permute-start.6
  21.1 0.1 hidden.8.refs_5_
  21.2 2.4 %collective-permute-start.9 = (bf16[272,384]{1,0:T(8,128)(2,1)S(1)}, bf16[272,384]{1,0:T(8,128)(2,1)S(1)}, u32[]{:S(2)}, u32[]{:S(2)}) collective-permute-start(bf16[272,384]{1,0:T(8,128)(2,1)S(1)} %hidden.8.refs_5_), channel_id=1, source_target_pairs={{0,8},{8,0},{16,24},{24,16},{32,40},{40,32},{48,56},{56,48},{64,72... | collective-permute-start | bytes 626696 | tf_op jit(solution)/shard_map/ppermute | solution.py:373
  23.6 1.4 %collective-permute-done.10.refs_0_ = bf16[1040,128]{1,0:T(8,128)(2,1)S(1)} collective-permute-done((bf16[1040,128]{1,0:T(8,128)(2,1)S(1)}, bf16[1040,128]{1,0:T(8,128)(2,1)S(1)}, u32[]{:S(2)}, u32[]{:S(2)}) %collective-permute-start.10) | collective-permute-done | bytes 266272 | tf_op jit(solution)/shard_map/ppermute | solution.py:386
  25.1 0.1 hidden.9.refs_7_
  25.2 2.4 %collective-permute-start.11 = (bf16[144,384]{1,0:T(8,128)(2,1)S(1)}, bf16[144,384]{1,0:T(8,128)(2,1)S(1)}, u32[]{:S(2)}, u32[]{:S(2)}) collective-permute-start(bf16[144,384]{1,0:T(8,128)(2,1)S(1)} %hidden.9.refs_7_), channel_id=1, source_target_pairs={{0,8},{8,0},{16,24},{24,16},{32,40},{40,32},{48,56},{56,48},{64,72... | collective-permute-start | bytes 331784 | tf_op jit(solution)/shard_map/ppermute | solution.py:373
  27.6 2.1 %collective-permute-done.1.refs_0_ = bf16[1040,128]{1,0:T(8,128)(2,1)S(1)} collective-permute-done((bf16[1040,128]{1,0:T(8,128)(2,1)S(1)}, bf16[1040,128]{1,0:T(8,128)(2,1)S(1)}, u32[]{:S(2)}, u32[]{:S(2)}) %collective-permute-start.1) | collective-permute-done | bytes 266272 | tf_op jit(solution)/shard_map/ppermute | solution.py:386
  29.7 0.6 hidden.6.refs_1_
  30.3 2.0 %collective-permute-start.2 = (bf16[144,384]{1,0:T(8,128)(2,1)S(1)}, bf16[144,384]{1,0:T(8,128)(2,1)S(1)}, u32[]{:S(2)}, u32[]{:S(2)}) collective-permute-start(bf16[144,384]{1,0:T(8,128)(2,1)S(1)} %hidden.6.refs_1_), channel_id=1, source_target_pairs={{0,8},{8,0},{16,24},{24,16},{32,40},{40,32},{48,56},{56,48},{64,72... | collective-permute-start | bytes 331784 | tf_op jit(solution)/shard_map/ppermute | solution.py:373
  32.3 2.2 %collective-permute-done.9.refs_6_ = bf16[272,384]{1,0:T(8,128)(2,1)S(1)} collective-permute-done((bf16[272,384]{1,0:T(8,128)(2,1)S(1)}, bf16[272,384]{1,0:T(8,128)(2,1)S(1)}, u32[]{:S(2)}, u32[]{:S(2)}) %collective-permute-start.9) | collective-permute-done | bytes 208928 | tf_op jit(solution)/shard_map/ppermute | solution.py:373
  34.4 2.4 %collective-permute-done.11.refs_8_ = bf16[144,384]{1,0:T(8,128)(2,1)S(1)} collective-permute-done((bf16[144,384]{1,0:T(8,128)(2,1)S(1)}, bf16[144,384]{1,0:T(8,128)(2,1)S(1)}, u32[]{:S(2)}, u32[]{:S(2)}) %collective-permute-start.11) | collective-permute-done | bytes 110624 | tf_op jit(solution)/shard_map/ppermute | solution.py:373
  36.8 1.2 %gram.2.refs_3_ = f32[8,296,128]{2,1,0:T(8,128)S(1)} custom-call(s32[1]{0:T(128)} %bitcast.refs_0_, bf16[272,384]{1,0:T(8,128)(2,1)S(1)} %hidden.5._.refs_1_, bf16[272,384]{1,0:T(8,128)(2,1)S(1)} %collective-permute-done.3.refs_2_, bf16[272,384]{1,0:T(8,128)(2,1)S(1)} %hidden.7.refs_3_, bf16[272,384]{1,0:T(8,128)(2,1)S(1)} %collective-permute-done.6.refs_4_, ...), custom_call_target="tpu_custom_call" | custom-call | tf_op jit(solution)/shard_map/gram/pallas_call | solution.py:231
  38.0 1.2 %collective-permute-done.2.refs_2_ = bf16[144,384]{1,0:T(8,128)(2,1)S(1)} collective-permute-done((bf16[144,384]{1,0:T(8,128)(2,1)S(1)}, bf16[144,384]{1,0:T(8,128)(2,1)S(1)}, u32[]{:S(2)}, u32[]{:S(2)}) %collective-permute-start.2) | collective-permute-done | bytes 110624 | tf_op jit(solution)/shard_map/ppermute | solution.py:373
  39.2 0.4 gram.3
  39.6 26.6 %all_to_all.10 = f32[8,296,128]{2,1,0:T(8,128)S(1)} all-to-all(f32[8,296,128]{2,1,0:T(8,128)S(1)} %gram.3), channel_id=1, replica_groups={{0,32,64,96,16,48,80,112},{8,40,72,104,24,56,88,120},{1,33,65,97,17,49,..., dimensions={0} | all-to-all | bytes 2424832 | tf_op jit(solution)/shard_map/all_to_all | solution.py:396
  66.3 1.5 %collective-permute-start.12 = (f32[288,128]{1,0:T(8,128)S(1)}, f32[288,128]{1,0:T(8,128)S(1)}, u32[]{:S(2)}, u32[]{:S(2)}) collective-permute-start(f32[288,128]{1,0:T(8,128)S(1)} %slice.8), channel_id=1, source_target_pairs={{32,0},{40,8},{48,16},{56,24},{96,64},{104,72},{112,80},{120,88},{... | collective-permute-start | bytes 442376 | tf_op jit(solution)/shard_map/ppermute | solution.py:401
  67.7 6.8 %first_panels.1 = (f32[128,384]{1,0:T(8,128)S(1)}, f32[128,256]{1,0:T(8,128)S(1)}, f32[128,128]{1,0:T(8,128)S(1)}) custom-call(f32[296,128]{1,0:T(8,128)S(1)} %reduce_sum.9.refs_0_), custom_call_target="tpu_custom_call" | custom-call | tf_op jit(solution)/shard_map/first_panels/pallas_call | solution.py:317
  74.6 4.0 %last_panel.1 = bf16[384,384]{1,0:T(8,128)(2,1)S(1)} custom-call(f32[296,128]{1,0:T(8,128)S(1)} %reduce_sum.9.refs_0_, f32[288,128]{1,0:T(8,128)S(1)} %collective-permute-done.12.refs_1_, f32[128,384]{1,0:T(8,128)S(1)} %get-tuple-element.32.refs_2_, f32[128,256]{1,0:T(8,128)S(1)} %get-tuple-element.33.refs_3_, f32[128,128]{1,0:T(8,128)S(1)} %get-tuple-element.34.refs_4_), custom_call_target="tpu_custom_call" | custom-call | tf_op jit(solution)/shard_map/last_panel/pallas_call | solution.py:349
  78.6 13.7 %all_to_all.11 = bf16[16,24,384]{2,1,0:T(8,128)(2,1)S(1)} all-to-all(bf16[16,24,384]{2,1,0:T(8,128)(2,1)S(1)} %bitcast.12), channel_id=1, replica_groups=mesh['dp'=16,'expert'=8] {'dp'}, dimensions={0} | all-to-all | bytes 589824 | tf_op jit(solution)/shard_map/all_to_all | solution.py:407
  92.3 0.7 fusion
  (10 shorter events, 0.1 us)
Async XLA Ops:
  1.7 6.4 %collective-permute-start = (bf16[1040,128]{1,0:T(8,128)(2,1)S(1)}, bf16[1040,128]{1,0:T(8,128)(2,1)S(1)}, u32[]{:S(2)}, u32[]{:S(2)}) collective-permute-start(bf16[1040,128]{1,0:T(8,128)(2,1)S(1)} %get-tuple-element.22), channel_id=1, source_target_pairs={{0,1},{1,0},{2,3},{3,2},{4,5},{5,4},{6,7},{7,6},{8,9},{9,8},{10,11... | collective-permute-start | bytes 798728 | tf_op jit(solution)/shard_map/ppermute | solution.py:386
  1.8 10.5 %collective-permute-start.4 = (bf16[1040,128]{1,0:T(8,128)(2,1)S(1)}, bf16[1040,128]{1,0:T(8,128)(2,1)S(1)}, u32[]{:S(2)}, u32[]{:S(2)}) collective-permute-start(bf16[1040,128]{1,0:T(8,128)(2,1)S(1)} %get-tuple-element.26), channel_id=1, source_target_pairs={{0,2},{1,3},{2,4},{3,5},{4,6},{5,7},{6,0},{7,1},{8,10},{9,11},{10,... | collective-permute-start | bytes 798728 | tf_op jit(solution)/shard_map/ppermute | solution.py:386
  3.5 14.3 %collective-permute-start.5 = (bf16[1040,128]{1,0:T(8,128)(2,1)S(1)}, bf16[1040,128]{1,0:T(8,128)(2,1)S(1)}, u32[]{:S(2)}, u32[]{:S(2)}) collective-permute-start(bf16[1040,128]{1,0:T(8,128)(2,1)S(1)} %get-tuple-element.27), channel_id=1, source_target_pairs={{0,6},{1,7},{2,0},{3,1},{4,2},{5,3},{6,4},{7,5},{8,14},{9,15},{10,... | collective-permute-start | bytes 798728 | tf_op jit(solution)/shard_map/ppermute | solution.py:386
  5.1 15.4 %collective-permute-start.7 = (bf16[1040,128]{1,0:T(8,128)(2,1)S(1)}, bf16[1040,128]{1,0:T(8,128)(2,1)S(1)}, u32[]{:S(2)}, u32[]{:S(2)}) collective-permute-start(bf16[1040,128]{1,0:T(8,128)(2,1)S(1)} %get-tuple-element.28), channel_id=1, source_target_pairs={{0,3},{1,2},{2,5},{3,4},{4,7},{5,6},{6,1},{7,0},{8,11},{9,10},{10,... | collective-permute-start | bytes 798728 | tf_op jit(solution)/shard_map/ppermute | solution.py:386
  5.1 16.0 %collective-permute-start.8 = (bf16[1040,128]{1,0:T(8,128)(2,1)S(1)}, bf16[1040,128]{1,0:T(8,128)(2,1)S(1)}, u32[]{:S(2)}, u32[]{:S(2)}) collective-permute-start(bf16[1040,128]{1,0:T(8,128)(2,1)S(1)} %get-tuple-element.29), channel_id=1, source_target_pairs={{0,7},{1,6},{2,1},{3,0},{4,3},{5,2},{6,5},{7,4},{8,15},{9,14},{10,... | collective-permute-start | bytes 798728 | tf_op jit(solution)/shard_map/ppermute | solution.py:386
  10.2 14.8 %collective-permute-start.10 = (bf16[1040,128]{1,0:T(8,128)(2,1)S(1)}, bf16[1040,128]{1,0:T(8,128)(2,1)S(1)}, u32[]{:S(2)}, u32[]{:S(2)}) collective-permute-start(bf16[1040,128]{1,0:T(8,128)(2,1)S(1)} %get-tuple-element.31), channel_id=1, source_target_pairs={{0,4},{1,5},{2,6},{3,7},{4,0},{5,1},{6,2},{7,3},{8,12},{9,13},{10,... | collective-permute-start | bytes 798728 | tf_op jit(solution)/shard_map/ppermute | solution.py:386
  12.3 17.4 %collective-permute-start.1 = (bf16[1040,128]{1,0:T(8,128)(2,1)S(1)}, bf16[1040,128]{1,0:T(8,128)(2,1)S(1)}, u32[]{:S(2)}, u32[]{:S(2)}) collective-permute-start(bf16[1040,128]{1,0:T(8,128)(2,1)S(1)} %get-tuple-element.23), channel_id=1, source_target_pairs={{0,5},{1,4},{2,7},{3,6},{4,1},{5,0},{6,3},{7,2},{8,13},{9,12},{10,... | collective-permute-start | bytes 798728 | tf_op jit(solution)/shard_map/ppermute | solution.py:386
  17.9 14.4 %collective-permute-start.3 = (bf16[272,384]{1,0:T(8,128)(2,1)S(1)}, bf16[272,384]{1,0:T(8,128)(2,1)S(1)}, u32[]{:S(2)}, u32[]{:S(2)}) collective-permute-start(bf16[272,384]{1,0:T(8,128)(2,1)S(1)} %hidden.5._.refs_1_), channel_id=1, source_target_pairs={{0,8},{8,0},{16,24},{24,16},{32,40},{40,32},{48,56},{56,48},{64,72... | collective-permute-start | bytes 626696 | tf_op jit(solution)/shard_map/ppermute | solution.py:373
  20.4 11.8 %collective-permute-start.6 = (bf16[272,384]{1,0:T(8,128)(2,1)S(1)}, bf16[272,384]{1,0:T(8,128)(2,1)S(1)}, u32[]{:S(2)}, u32[]{:S(2)}) collective-permute-start(bf16[272,384]{1,0:T(8,128)(2,1)S(1)} %hidden.7.refs_3_), channel_id=1, source_target_pairs={{0,8},{8,0},{16,24},{24,16},{32,40},{40,32},{48,56},{56,48},{64,72... | collective-permute-start | bytes 626696 | tf_op jit(solution)/shard_map/ppermute | solution.py:373
  21.2 13.2 %collective-permute-start.9 = (bf16[272,384]{1,0:T(8,128)(2,1)S(1)}, bf16[272,384]{1,0:T(8,128)(2,1)S(1)}, u32[]{:S(2)}, u32[]{:S(2)}) collective-permute-start(bf16[272,384]{1,0:T(8,128)(2,1)S(1)} %hidden.8.refs_5_), channel_id=1, source_target_pairs={{0,8},{8,0},{16,24},{24,16},{32,40},{40,32},{48,56},{56,48},{64,72... | collective-permute-start | bytes 626696 | tf_op jit(solution)/shard_map/ppermute | solution.py:373
  25.2 11.6 %collective-permute-start.11 = (bf16[144,384]{1,0:T(8,128)(2,1)S(1)}, bf16[144,384]{1,0:T(8,128)(2,1)S(1)}, u32[]{:S(2)}, u32[]{:S(2)}) collective-permute-start(bf16[144,384]{1,0:T(8,128)(2,1)S(1)} %hidden.9.refs_7_), channel_id=1, source_target_pairs={{0,8},{8,0},{16,24},{24,16},{32,40},{40,32},{48,56},{56,48},{64,72... | collective-permute-start | bytes 331784 | tf_op jit(solution)/shard_map/ppermute | solution.py:373
  30.3 8.9 %collective-permute-start.2 = (bf16[144,384]{1,0:T(8,128)(2,1)S(1)}, bf16[144,384]{1,0:T(8,128)(2,1)S(1)}, u32[]{:S(2)}, u32[]{:S(2)}) collective-permute-start(bf16[144,384]{1,0:T(8,128)(2,1)S(1)} %hidden.6.refs_1_), channel_id=1, source_target_pairs={{0,8},{8,0},{16,24},{24,16},{32,40},{40,32},{48,56},{56,48},{64,72... | collective-permute-start | bytes 331784 | tf_op jit(solution)/shard_map/ppermute | solution.py:373
  66.3 8.3 %collective-permute-start.12 = (f32[288,128]{1,0:T(8,128)S(1)}, f32[288,128]{1,0:T(8,128)S(1)}, u32[]{:S(2)}, u32[]{:S(2)}) collective-permute-start(f32[288,128]{1,0:T(8,128)S(1)} %slice.8), channel_id=1, source_target_pairs={{32,0},{40,8},{48,16},{56,24},{96,64},{104,72},{112,80},{120,88},{... | collective-permute-start | bytes 442376 | tf_op jit(solution)/shard_map/ppermute | solution.py:401
